TPU v7x, 32 devices: a whole 2x2x4 slice. The times are simulated.
32 devices in a mesh: fsdp: 4 (over x, core), ctx: 2 (over y), tp: 4 (over z).
Axes of the slice: x: 2, y: 2, z: 4, core: 2. Of those that a mesh axis runs over, the one named last changes fastest.
Arguments:
- tokens: bfloat16 [8, 1024, 2048], P('fsdp', 'ctx'), may hold values from -6 to 6
- w_query: bfloat16 [2048, 2048], P(('fsdp', 'ctx'), 'tp'), may hold values from -0.125 to 0.125
- w_key: bfloat16 [2048, 2048], P(('fsdp', 'ctx'), 'tp'), may hold values from -0.125 to 0.125
- w_value: bfloat16 [2048, 2048], P(('fsdp', 'ctx'), 'tp'), may hold values from -0.125 to 0.125
- w_output: bfloat16 [2048, 2048], P('tp', ('fsdp', 'ctx')), may hold values from -0.125 to 0.125
- w_gate: bfloat16 [2048, 8192], P(('fsdp', 'ctx'), 'tp'), may hold values from -0.125 to 0.125
- w_up: bfloat16 [2048, 8192], P(('fsdp', 'ctx'), 'tp'), may hold values from -0.125 to 0.125
- w_down: bfloat16 [8192, 2048], P('tp', ('fsdp', 'ctx')), may hold values from -0.0625 to 0.0625
- gain_query: bfloat16 [2048], P('tp'), may hold values from 0.25 to 1.75
- gain_key: bfloat16 [2048], P('tp'), may hold values from 0.25 to 1.75
- gain_attn: bfloat16 [2048], replicated, may hold values from 0.25 to 1.75
- gain_mlp: bfloat16 [2048], replicated, may hold values from 0.25 to 1.75
- cotangent: bfloat16 [8, 1024, 2048], P('fsdp', 'ctx'), may hold values from -6 to 6
Outputs:
- output: bfloat16 [8, 1024, 2048], P('fsdp', 'ctx')
- grad_tokens: bfloat16 [8, 1024, 2048], P('fsdp', 'ctx')
- grad_w_query: float32 [2048, 2048], P(('fsdp', 'ctx'), 'tp')
- grad_w_key: float32 [2048, 2048], P(('fsdp', 'ctx'), 'tp')
- grad_w_value: float32 [2048, 2048], P(('fsdp', 'ctx'), 'tp')
- grad_w_output: float32 [2048, 2048], P('tp', ('fsdp', 'ctx'))
- grad_w_gate: float32 [2048, 8192], P(('fsdp', 'ctx'), 'tp')
- grad_w_up: float32 [2048, 8192], P(('fsdp', 'ctx'), 'tp')
- grad_w_down: float32 [8192, 2048], P('tp', ('fsdp', 'ctx'))
- grad_gain_query: float32 [2048], P('tp')
- grad_gain_key: float32 [2048], P('tp')
- grad_gain_attn: float32 [2048], replicated
- grad_gain_mlp: float32 [2048], replicated
All inputs are finite; a program needn't handle non-finite values.
Results may differ from a plain program's by a relative error of at most 0.025.
Values may be sent and summed in bfloat16 or wider, within the bound.
A program may use at most 256 MiB of HBM per device.

v0:
```python
import jax
import jax.numpy as jnp
from jax import lax
from jax.sharding import PartitionSpec as P

HD = 128
SEQ_MB = 1
MICRO = 2


norm_eps = 1e-06
rope_theta = 500000.0
masked_value = -1e30


def post_norm(branch, gain_vector):
    return (
        branch
        * lax.rsqrt(jnp.mean(branch * branch, axis=-1, keepdims=True) + norm_eps)
        * gain_vector
    )


def gating(gate_proj, up_proj):
    return jax.nn.silu(gate_proj) * up_proj


def rotation_tables(positions, head_dim):
    half_width = head_dim // 2
    frequency = rope_theta ** (-jnp.arange(half_width, dtype=jnp.float32) * 2.0 / head_dim)
    angles = positions.astype(jnp.float32)[:, None] * frequency[None, :]
    return (jnp.cos(angles)[None, :, None, :], jnp.sin(angles)[None, :, None, :])


def rotate(values, cosine, sine_table):
    half_width = values.shape[-1] // 2
    first_half = values[..., :half_width]
    second_half = values[..., half_width:]
    return jnp.concatenate(
        [
            first_half * cosine - second_half * sine_table,
            second_half * cosine + first_half * sine_table,
        ],
        axis=-1,
    )


def gather_weights(w_query, w_key, w_value, w_output, w_gate, w_up, w_down):
    return (
        lax.all_gather(w_query, ("fsdp", "ctx"), axis=0, tiled=True),
        lax.all_gather(w_key, ("fsdp", "ctx"), axis=0, tiled=True),
        lax.all_gather(w_value, ("fsdp", "ctx"), axis=0, tiled=True),
        lax.all_gather(w_output, ("fsdp", "ctx"), axis=1, tiled=True),
        lax.all_gather(w_gate, ("fsdp", "ctx"), axis=0, tiled=True),
        lax.all_gather(w_up, ("fsdp", "ctx"), axis=0, tiled=True),
        lax.all_gather(w_down, ("fsdp", "ctx"), axis=1, tiled=True),
    )


def per_device(
    tokens,
    w_query,
    w_key,
    w_value,
    w_output,
    w_gate,
    w_up,
    w_down,
    gain_query,
    gain_key,
    gain_attn,
    gain_mlp,
    cotangent,
):
    model_width = tokens.shape[2]
    group_len = tokens.shape[1]
    local_width = w_query.shape[1]
    head_count = local_width // HD
    seq_count = SEQ_MB
    full_len = group_len * lax.axis_size("ctx")
    ctx_rank = lax.axis_index("ctx")
    positions = ctx_rank * group_len + jnp.arange(group_len, dtype=jnp.int32)
    cosine, sine_table = rotation_tables(positions, HD)
    score_scale = HD ** (-0.5)
    block_len = min(512, full_len)
    blocks_needed = (ctx_rank * group_len + group_len - 1) // block_len + 1
    shape_four = (seq_count, group_len, head_count, HD)
    shape_flat = (seq_count, group_len, local_width)
    gain_q = gain_query.astype(jnp.float32)
    gain_k = gain_key.astype(jnp.float32)
    gain_a = gain_attn.astype(jnp.float32)
    gain_m = gain_mlp.astype(jnp.float32)
    held = gather_weights(w_query, w_key, w_value, w_output, w_gate, w_up, w_down)

    def one_micro(x_micro, grad_micro):
        mat_query, mat_key, mat_value, mat_output, mat_gate, mat_up, mat_down = held
        queries = jnp.einsum("scd,de->sce", x_micro, mat_query, preferred_element_type=jnp.float32)
        key_raw = jnp.einsum("scd,de->sce", x_micro, mat_key, preferred_element_type=jnp.float32)
        value_low = jnp.einsum(
            "scd,de->sce", x_micro, mat_value, preferred_element_type=jnp.float32
        ).astype(jnp.bfloat16)
        square_sums = lax.psum(
            (jnp.sum(queries * queries, axis=-1), jnp.sum(key_raw * key_raw, axis=-1)), "tp"
        )
        rms_query = lax.rsqrt(square_sums[0] / model_width + norm_eps)[..., None]
        rms_key = lax.rsqrt(square_sums[1] / model_width + norm_eps)[..., None]
        q_normed = (queries * rms_query * gain_q).reshape(shape_four)
        k_normed = (key_raw * rms_key * gain_k).reshape(shape_four)
        q_low = rotate(q_normed, cosine, sine_table).astype(jnp.bfloat16)
        k_low = rotate(k_normed, cosine, sine_table).astype(jnp.bfloat16).reshape(shape_flat)
        attend_row_top = jnp.full(shape_four[:3], masked_value, jnp.float32)
        key_piece = lax.all_gather(k_low, "ctx", axis=1, tiled=True)
        value_piece = lax.all_gather(value_low, "ctx", axis=1, tiled=True)
        row_count = key_piece.shape[1]
        key_piece = key_piece.reshape(seq_count, row_count, head_count, HD)
        value_piece = value_piece.reshape(seq_count, row_count, head_count, HD)
        scores = (
            jnp.einsum("sqhd,skhd->sqhk", q_low, key_piece, preferred_element_type=jnp.float32)
            * score_scale
        )
        key_pos = jnp.arange(row_count, dtype=jnp.int32)
        allowed = (key_pos[None, :] <= positions[:, None])[None, :, None, :]
        scores = jnp.where(allowed, scores, masked_value)
        new_top = jnp.maximum(attend_row_top, jnp.max(scores, axis=-1))
        weights_exp = jnp.where(allowed, jnp.exp(scores - new_top[..., None]), 0.0)
        attend_row_total = jnp.sum(weights_exp, axis=-1)
        weighted = jnp.einsum(
            "sqhk,skhd->sqhd",
            weights_exp.astype(jnp.bfloat16),
            value_piece,
            preferred_element_type=jnp.float32,
        )
        row_top, row_total, weighted = (new_top, attend_row_total, weighted)
        head_out = weighted / row_total[..., None]
        head_low = head_out.reshape(shape_flat).astype(jnp.bfloat16)
        attention = lax.psum(
            jnp.einsum(
                "sce,ed->scd", head_low, mat_output, preferred_element_type=jnp.float32
            ).astype(jnp.bfloat16),
            "tp",
        ).astype(jnp.float32)
        mixed_rows = x_micro.astype(jnp.float32) + post_norm(attention, gain_a)
        mlp_in = mixed_rows.astype(jnp.bfloat16)
        gate_proj = jnp.einsum("scd,df->scf", mlp_in, mat_gate, preferred_element_type=jnp.float32)
        up_proj = jnp.einsum("scd,df->scf", mlp_in, mat_up, preferred_element_type=jnp.float32)
        hidden = gating(gate_proj, up_proj).astype(jnp.bfloat16)
        down_proj = lax.psum(
            jnp.einsum("scf,fd->scd", hidden, mat_down, preferred_element_type=jnp.float32).astype(
                jnp.bfloat16
            ),
            "tp",
        ).astype(jnp.float32)
        result = (mixed_rows + post_norm(down_proj, gain_m)).astype(jnp.bfloat16)
        mat_query, mat_key, mat_value, mat_output, mat_gate, mat_up, mat_down = held
        grad_rows = grad_micro.astype(jnp.float32)
        pull_mlp = jax.vjp(post_norm, down_proj, gain_m)[1]
        grad_down, grad_gain_m = pull_mlp(grad_rows)
        down_low = grad_down.astype(jnp.bfloat16)
        grad_mat_down = jnp.einsum(
            "scf,scd->fd", hidden, down_low, preferred_element_type=jnp.float32
        )
        grad_hidden = jnp.einsum(
            "scd,fd->scf", down_low, mat_down, preferred_element_type=jnp.float32
        )
        pull_gate = jax.vjp(gating, gate_proj, up_proj)[1]
        grad_gate, grad_up = pull_gate(grad_hidden)
        gate_low = grad_gate.astype(jnp.bfloat16)
        up_low = grad_up.astype(jnp.bfloat16)
        grad_mat_gate = jnp.einsum(
            "scd,scf->df", mlp_in, gate_low, preferred_element_type=jnp.float32
        )
        grad_mat_up = jnp.einsum("scd,scf->df", mlp_in, up_low, preferred_element_type=jnp.float32)
        mlp_terms = jnp.einsum(
            "scf,df->scd", gate_low, mat_gate, preferred_element_type=jnp.float32
        ) + jnp.einsum("scf,df->scd", up_low, mat_up, preferred_element_type=jnp.float32)
        grad_mixed = grad_rows + lax.psum(mlp_terms.astype(jnp.bfloat16), "tp").astype(jnp.float32)
        pull_attn = jax.vjp(post_norm, attention, gain_a)[1]
        grad_attention, grad_gain_a = pull_attn(grad_mixed)
        attn_low = grad_attention.astype(jnp.bfloat16)
        grad_mat_output = jnp.einsum(
            "sce,scd->ed", head_low, attn_low, preferred_element_type=jnp.float32
        )
        grad_heads = (
            jnp.einsum("scd,ed->sce", attn_low, mat_output, preferred_element_type=jnp.float32)
            .astype(jnp.bfloat16)
            .reshape(shape_four)
        )
        delta = jnp.sum(grad_heads.astype(jnp.float32) * head_out, axis=-1)
        keys_all, values_all = (
            lax.all_gather(k_low, "ctx", axis=1, tiled=True),
            lax.all_gather(value_low, "ctx", axis=1, tiled=True),
        )

        def key_block(block_index, running):
            grad_q_rot, grad_keys_all, grad_values_all = running
            first_row = block_index * block_len
            key_rows = lax.dynamic_slice_in_dim(keys_all, first_row, block_len, 1).reshape(
                seq_count, block_len, head_count, HD
            )
            value_rows = lax.dynamic_slice_in_dim(values_all, first_row, block_len, 1).reshape(
                seq_count, block_len, head_count, HD
            )
            scores = (
                jnp.einsum("sqhd,skhd->sqhk", q_low, key_rows, preferred_element_type=jnp.float32)
                * score_scale
            )
            key_pos = first_row + jnp.arange(block_len, dtype=jnp.int32)
            allowed = (key_pos[None, :] <= positions[:, None])[None, :, None, :]
            probs = jnp.where(
                allowed, jnp.exp(scores - row_top[..., None]) / row_total[..., None], 0.0
            )
            grad_probs = jnp.einsum(
                "sqhd,skhd->sqhk", grad_heads, value_rows, preferred_element_type=jnp.float32
            )
            grad_scores = (probs * (grad_probs - delta[..., None])).astype(jnp.bfloat16)
            grad_q_rot = (
                grad_q_rot
                + jnp.einsum(
                    "sqhk,skhd->sqhd", grad_scores, key_rows, preferred_element_type=jnp.float32
                )
                * score_scale
            )
            key_term = (
                jnp.einsum(
                    "sqhk,sqhd->skhd", grad_scores, q_low, preferred_element_type=jnp.float32
                )
                * score_scale
            )
            value_term = jnp.einsum(
                "sqhk,sqhd->skhd",
                probs.astype(jnp.bfloat16),
                grad_heads,
                preferred_element_type=jnp.float32,
            )
            grad_keys_all = lax.dynamic_update_slice_in_dim(grad_keys_all, key_term, first_row, 1)
            grad_values_all = lax.dynamic_update_slice_in_dim(
                grad_values_all, value_term, first_row, 1
            )
            return (grad_q_rot, grad_keys_all, grad_values_all)

        whole_shape = (seq_count, full_len, head_count, HD)
        grad_q_rot, grad_keys_all, grad_values_all = lax.fori_loop(
            0,
            blocks_needed,
            key_block,
            (
                jnp.zeros(shape_four, jnp.float32),
                jnp.zeros(whole_shape, jnp.float32),
                jnp.zeros(whole_shape, jnp.float32),
            ),
        )
        grad_k_rot, grad_values = (
            lax.psum_scatter(
                grad_keys_all.reshape(seq_count, full_len, local_width).astype(jnp.bfloat16),
                "ctx",
                scatter_dimension=1,
                tiled=True,
            ).astype(jnp.float32),
            lax.psum_scatter(
                grad_values_all.reshape(seq_count, full_len, local_width).astype(jnp.bfloat16),
                "ctx",
                scatter_dimension=1,
                tiled=True,
            ).astype(jnp.float32),
        )
        value_grad = grad_values.astype(jnp.bfloat16)
        pull_rot = jax.vjp(lambda inputs: rotate(inputs, cosine, sine_table), q_normed)[1]
        grad_q_normed = pull_rot(grad_q_rot)[0].reshape(shape_flat)
        grad_k_normed = pull_rot(grad_k_rot.reshape(shape_four))[0].reshape(shape_flat)
        inner_sums = lax.psum(
            (
                jnp.sum(grad_q_normed * queries * gain_q, axis=-1),
                jnp.sum(grad_k_normed * key_raw * gain_k, axis=-1),
            ),
            "tp",
        )
        grad_queries = (
            grad_q_normed * rms_query * gain_q
            - queries * rms_query**3 * (inner_sums[0] / model_width)[..., None]
        ).astype(jnp.bfloat16)
        grad_keys = (
            grad_k_normed * rms_key * gain_k
            - key_raw * rms_key**3 * (inner_sums[1] / model_width)[..., None]
        ).astype(jnp.bfloat16)
        grad_gain_q = jnp.sum(grad_q_normed * queries * rms_query, axis=(0, 1))
        grad_gain_k = jnp.sum(grad_k_normed * key_raw * rms_key, axis=(0, 1))
        grad_mat_query = jnp.einsum(
            "scd,sce->de", x_micro, grad_queries, preferred_element_type=jnp.float32
        )
        grad_mat_key = jnp.einsum(
            "scd,sce->de", x_micro, grad_keys, preferred_element_type=jnp.float32
        )
        grad_mat_value = jnp.einsum(
            "scd,sce->de", x_micro, value_grad, preferred_element_type=jnp.float32
        )
        input_terms = jnp.einsum(
            "sce,de->scd", grad_queries, mat_query, preferred_element_type=jnp.float32
        )
        input_terms = input_terms + jnp.einsum(
            "sce,de->scd", grad_keys, mat_key, preferred_element_type=jnp.float32
        )
        input_terms = input_terms + jnp.einsum(
            "sce,de->scd", value_grad, mat_value, preferred_element_type=jnp.float32
        )
        grad_input = (
            grad_mixed + lax.psum(input_terms.astype(jnp.bfloat16), "tp").astype(jnp.float32)
        ).astype(jnp.bfloat16)
        mats = (
            grad_mat_query,
            grad_mat_key,
            grad_mat_value,
            grad_mat_output,
            grad_mat_gate,
            grad_mat_up,
            grad_mat_down,
        )
        gains = (grad_gain_q, grad_gain_k, grad_gain_a, grad_gain_m)
        return (result, grad_input, mats, gains)

    results = []
    input_grads = []
    mat_sums = None
    gain_sums = None
    for micro_index in range(MICRO):
        rows_start = micro_index * seq_count
        result, grad_input, mats, gains = one_micro(
            tokens[rows_start : rows_start + seq_count],
            cotangent[rows_start : rows_start + seq_count],
        )
        results.append(result)
        input_grads.append(grad_input)
        if mat_sums is None:
            mat_sums, gain_sums = (mats, gains)
        else:
            mat_sums = tuple((prior + extra for prior, extra in zip(mat_sums, mats)))
            gain_sums = tuple((prior + extra for prior, extra in zip(gain_sums, gains)))
    owned = (
        lax.psum_scatter(
            mat_sums[0].astype(jnp.bfloat16), ("fsdp", "ctx"), scatter_dimension=0, tiled=True
        ).astype(jnp.float32),
        lax.psum_scatter(
            mat_sums[1].astype(jnp.bfloat16), ("fsdp", "ctx"), scatter_dimension=0, tiled=True
        ).astype(jnp.float32),
        lax.psum_scatter(
            mat_sums[2].astype(jnp.bfloat16), ("fsdp", "ctx"), scatter_dimension=0, tiled=True
        ).astype(jnp.float32),
        lax.psum_scatter(
            mat_sums[3].astype(jnp.bfloat16), ("fsdp", "ctx"), scatter_dimension=1, tiled=True
        ).astype(jnp.float32),
        lax.psum_scatter(
            mat_sums[4].astype(jnp.bfloat16), ("fsdp", "ctx"), scatter_dimension=0, tiled=True
        ).astype(jnp.float32),
        lax.psum_scatter(
            mat_sums[5].astype(jnp.bfloat16), ("fsdp", "ctx"), scatter_dimension=0, tiled=True
        ).astype(jnp.float32),
        lax.psum_scatter(
            mat_sums[6].astype(jnp.bfloat16), ("fsdp", "ctx"), scatter_dimension=1, tiled=True
        ).astype(jnp.float32),
    )
    gain_totals = lax.psum(
        (gain_sums[0], gain_sums[1], gain_sums[2], gain_sums[3]), ("fsdp", "ctx")
    )
    return (
        jnp.concatenate(results, axis=0),
        jnp.concatenate(input_grads, axis=0),
        owned[0],
        owned[1],
        owned[2],
        owned[3],
        owned[4],
        owned[5],
        owned[6],
        gain_totals[0],
        gain_totals[1],
        gain_totals[2],
        gain_totals[3],
    )


def solution(mesh):
    in_specs = (
        P("fsdp", "ctx", None),
        P(("fsdp", "ctx"), "tp"),
        P(("fsdp", "ctx"), "tp"),
        P(("fsdp", "ctx"), "tp"),
        P("tp", ("fsdp", "ctx")),
        P(("fsdp", "ctx"), "tp"),
        P(("fsdp", "ctx"), "tp"),
        P("tp", ("fsdp", "ctx")),
        P("tp"),
        P("tp"),
        P(),
        P(),
        P("fsdp", "ctx", None),
    )
    out_specs = (
        P("fsdp", "ctx", None),
        P("fsdp", "ctx", None),
        P(("fsdp", "ctx"), "tp"),
        P(("fsdp", "ctx"), "tp"),
        P(("fsdp", "ctx"), "tp"),
        P("tp", ("fsdp", "ctx")),
        P(("fsdp", "ctx"), "tp"),
        P(("fsdp", "ctx"), "tp"),
        P("tp", ("fsdp", "ctx")),
        P("tp"),
        P("tp"),
        P(),
        P(),
    )
    return jax.shard_map(
        per_device, mesh=mesh, in_specs=in_specs, out_specs=out_specs, check_vma=False
    )
```

profile of v0, /device:TPU:0, one launch (start us, length us, event | category | flops | bytes accessed | tf_op | source)
XLA Modules:
  0.0 1732.6 jit_solution(6454780086592739977)
XLA Ops:
  12.6 27.9 %all-gather.16.cloned.1.call-done = bf16[2048,512]{1,0:T(8,128)(2,1)} async-done(((bf16[256,512]{1,0:T(8,128)(2,1)}), bf16[2048,512]{1,0:T(8,128)(2,1)}) %all-gather.16.cloned.1.call-update) | async-done | bytes 2097168 | tf_op jit(solution)/shard_map/all_gather | solution.py:51
  47.0 23.3 %all-gather.20.cloned.1.call-done = bf16[2048,512]{1,0:T(8,128)(2,1)} async-done(((bf16[256,512]{1,0:T(8,128)(2,1)}), bf16[2048,512]{1,0:T(8,128)(2,1)}) %all-gather.20.cloned.1.call-update) | async-done | bytes 2097168 | tf_op jit(solution)/shard_map/all_gather | solution.py:50
  146.3 16.1 all-gather.34.cloned.1.call-done
  164.6 21.1 %all-gather.32.cloned.1.call-done = bf16[1024,512]{1,0:T(8,128)(2,1)} async-done(((bf16[512,512]{1,0:T(8,128)(2,1)}), bf16[1024,512]{1,0:T(8,128)(2,1)}) %all-gather.32.cloned.1.call-update) | async-done | bytes 1048592 | tf_op jit(solution)/shard_map/all_gather | solution.py:113
  187.2 22.0 %all-gather.30.cloned.1.call-done = bf16[1,1024,512]{1,2,0:T(8,128)(2,1)} async-done(((bf16[1,512,512]{1,2,0:T(8,128)(2,1)}), bf16[1,1024,512]{1,2,0:T(8,128)(2,1)}) %all-gather.30.cloned.1.call-update) | async-done | bytes 1048592 | tf_op jit(solution)/shard_map/all_gather | solution.py:112
  225.4 13.9 all-gather.22.cloned.1.call-done
  259.5 142.3 %all-reduce.26.cloned.1.call-done = (bf16[1,512,2048]{2,1,0:T(8,128)(2,1)}, bf16[1,512,2048]{2,1,0:T(8,128)(2,1)}) async-done(((bf16[1,512,2048]{2,1,0:T(8,128)(2,1)}, bf16[1,512,2048]{2,1,0:T(8,128)(2,1)}), (bf16[1,512,2048]{2,1,0:T(8,128)(2,1)}, bf16[1,512,2048]{2,1,0:T(8,128)(2,1)})) %all-reduce.26.cloned.1.call-update) | async-done | bytes 4194320 | tf_op jit(solution)/shard_map/psum | solution.py:136
  410.9 46.1 %all-gather.24.cloned.1.call-done = bf16[2048,2048]{1,0:T(8,128)(2,1)} async-done(((bf16[256,2048]{1,0:T(8,128)(2,1)}), bf16[2048,2048]{1,0:T(8,128)(2,1)}) %all-gather.24.cloned.1.call-update) | async-done | bytes 8388624 | tf_op jit(solution)/shard_map/all_gather | solution.py:54
  472.6 41.0 %all-gather.26.cloned.1.call-done = bf16[2048,2048]{1,0:T(8,128)(2,1)} async-done(((bf16[256,2048]{1,0:T(8,128)(2,1)}), bf16[2048,2048]{1,0:T(8,128)(2,1)}) %all-gather.26.cloned.1.call-update) | async-done | bytes 8388624 | tf_op jit(solution)/shard_map/all_gather | solution.py:55
  530.8 40.6 %all-gather.28.cloned.1.call-done = bf16[2048,2048]{1,0:T(8,128)(2,1)} async-done(((bf16[2048,256]{1,0:T(8,128)(2,1)}), bf16[2048,2048]{1,0:T(8,128)(2,1)}) %all-gather.28.cloned.1.call-update) | async-done | bytes 8388624 | tf_op jit(solution)/shard_map/all_gather | solution.py:56
  587.9 154.8 %all-reduce.24.cloned.1.call-done = (bf16[1,512,2048]{2,1,0:T(8,128)(2,1)}, bf16[1,512,2048]{2,1,0:T(8,128)(2,1)}) async-done(((bf16[1,512,2048]{2,1,0:T(8,128)(2,1)}, bf16[1,512,2048]{2,1,0:T(8,128)(2,1)}), (bf16[1,512,2048]{2,1,0:T(8,128)(2,1)}, bf16[1,512,2048]{2,1,0:T(8,128)(2,1)})) %all-reduce.24.cloned.1.call-update) | async-done | bytes 4194320 | tf_op jit(solution)/shard_map/psum | solution.py:147
  819.2 150.0 %all-reduce.22.cloned.1.call-done = (bf16[1,512,2048]{2,1,0:T(8,128)(2,1)}, bf16[1,512,2048]{2,1,0:T(8,128)(2,1)}) async-done(((bf16[1,512,2048]{2,1,0:T(8,128)(2,1)}, bf16[1,512,2048]{2,1,0:T(8,128)(2,1)}), (bf16[1,512,2048]{2,1,0:T(8,128)(2,1)}, bf16[1,512,2048]{2,1,0:T(8,128)(2,1)})) %all-reduce.22.cloned.1.call-update) | async-done | bytes 4194320 | tf_op jit(solution)/shard_map/psum | solution.py:176
  991.5 24.6 %while.30 = (s32[]{:T(128)}, f32[1,512,4,128]{1,3,2,0:T(8,128)}, bf16[1,1024,4,128]{1,3,2,0:T(8,128)(2,1)}, bf16[1,1024,4,128]{1,3,2,0:T(8,128)(2,1)}, s32[]{:T(...) while((s32[]{:T(128)}, f32[1,512,4,128]{1,3,2,0:T(8,128)}, ...), condition=%wide.region_25.26_spmd.clone, body=%wide.region_24.25_spmd.clone.sunk | while | flops 1351877632 | bytes 35684604 | solution.py:242
  1023.7 24.6 %while.31 = (s32[]{:T(128)}, f32[1,512,4,128]{1,3,2,0:T(8,128)}, bf16[1,1024,4,128]{1,3,2,0:T(8,128)(2,1)}, bf16[1,1024,4,128]{1,3,2,0:T(8,128)(2,1)}, s32[]{:T(...) while((s32[]{:T(128)}, f32[1,512,4,128]{1,3,2,0:T(8,128)}, ...), condition=%wide.region_38.39_spmd.clone, body=%wide.region_37.38_spmd.clone.sunk | while | flops 1351877632 | bytes 35684604 | solution.py:242
  1063.9 53.0 %reduce-scatter.16.cloned.1.call-done = bf16[1,512,512]{1,2,0:T(8,128)(2,1)} async-done(((bf16[1,1024,512]{1,2,0:T(8,128)(2,1)}), bf16[1,512,512]{1,2,0:T(8,128)(2,1)}) %reduce-scatter.16.cloned.1.call-update) | async-done | bytes 524304 | tf_op jit(solution)/shard_map/reduce_scatter | solution.py:253
  1120.7 18.7 %reduce-scatter.14.cloned.1.call-done = bf16[1,512,512]{1,2,0:T(8,128)(2,1)} async-done(((bf16[1,1024,512]{1,2,0:T(8,128)(2,1)}), bf16[1,512,512]{1,2,0:T(8,128)(2,1)}) %reduce-scatter.14.cloned.1.call-update) | async-done | bytes 524304 | tf_op jit(solution)/shard_map/reduce_scatter | solution.py:259
  1144.5 17.4 %reduce-scatter.18.cloned.1.call-done = bf16[1,512,512]{1,2,0:T(8,128)(2,1)} async-done(((bf16[1,1024,512]{1,2,0:T(8,128)(2,1)}), bf16[1,512,512]{1,2,0:T(8,128)(2,1)}) %reduce-scatter.18.cloned.1.call-update) | async-done | bytes 524304 | tf_op jit(solution)/shard_map/reduce_scatter | solution.py:259
  1233.1 13.6 fusion.233
  1246.8 15.5 add_convert_fusion
  1315.3 24.4 %all-reduce.8 = (f32[512]{0:T(512)}, f32[512]{0:T(512)}, f32[2048]{0:T(1024)}, f32[2048]{0:T(1024)}) all-reduce(f32[512]{0:T(512)S(1)} %add.349, f32[512]{0:T(512)S(1)} %add.350, f32[2048]{0:T(1024)S(1)} %add.351, f32[2048]{0:T(1024)S(1)} %add.352), channel_id=1, replica_groups=mesh['fsdp'=4,'ctx'=2,'tp'=4] {'fsdp','ctx'}, use_global_device_ids=true, to_apply=%region_55.56 | all-reduce | flops 5120 | bytes 40960 | tf_op jit(solution)/shard_map/psum | solution.py:360
  1347.2 152.3 %all-reduce.20.cloned.1.call-done = (bf16[1,512,2048]{2,1,0:T(8,128)(2,1)}, bf16[1,512,2048]{2,1,0:T(8,128)(2,1)}) async-done(((bf16[1,512,2048]{2,1,0:T(8,128)(2,1)}, bf16[1,512,2048]{2,1,0:T(8,128)(2,1)}), (bf16[1,512,2048]{2,1,0:T(8,128)(2,1)}, bf16[1,512,2048]{2,1,0:T(8,128)(2,1)})) %all-reduce.20.cloned.1.call-update) | async-done | bytes 4194320 | tf_op jit(solution)/shard_map/psum | solution.py:306
  1507.1 66.0 %reduce-scatter.32.cloned.1.call-done = bf16[2048,256]{1,0:T(8,128)(2,1)} async-done(((bf16[2048,2048]{1,0:T(8,128)(2,1)}), bf16[2048,256]{1,0:T(8,128)(2,1)}) %reduce-scatter.32.cloned.1.call-update) | async-done | bytes 1048592 | tf_op jit(solution)/shard_map/reduce_scatter | solution.py:356
  1575.8 72.4 %reduce-scatter.30.cloned.1.call-done = bf16[256,2048]{1,0:T(8,128)(2,1)} async-done(((bf16[2048,2048]{1,0:T(8,128)(2,1)}), bf16[256,2048]{1,0:T(8,128)(2,1)}) %reduce-scatter.30.cloned.1.call-update) | async-done | bytes 1048592 | tf_op jit(solution)/shard_map/reduce_scatter | solution.py:353
  1651.0 71.8 %reduce-scatter.28.cloned.1.call-done = bf16[256,2048]{1,0:T(8,128)(2,1)} async-done(((bf16[2048,2048]{1,0:T(8,128)(2,1)}), bf16[256,2048]{1,0:T(8,128)(2,1)}) %reduce-scatter.28.cloned.1.call-update) | async-done | bytes 1048592 | tf_op jit(solution)/shard_map/reduce_scatter | solution.py:350
  (481 shorter events, 512.5 us)
Async XLA Ops:
  7.9 62.4 %all-gather.20.cloned.1.call-start = ((), (), s32[]{:S(2)}) async-start(), calls=%async_computation.14 | async-start | bytes 2359296 | tf_op jit(solution)/shard_map/all_gather | solution.py:50
  8.7 111.7 %all-gather.14.cloned.1.call-start = ((), (), s32[]{:S(2)}) async-start(), calls=%async_computation.11 | async-start | bytes 2359296 | tf_op jit(solution)/shard_map/all_gather | solution.py:52
  9.4 129.7 %all-gather.18.cloned.1.call-start = ((), (), s32[]{:S(2)}) async-start(), calls=%async_computation.13 | async-start | bytes 1572864 | tf_op jit(solution)/shard_map/all_gather | solution.py:112
  124.9 60.8 %all-gather.32.cloned.1.call-start = ((), (), s32[]{:S(2)}) async-start(), calls=%async_computation.31 | async-start | bytes 1572864 | tf_op jit(solution)/shard_map/all_gather | solution.py:113
  129.0 80.2 %all-gather.30.cloned.1.call-start = ((), (), s32[]{:S(2)}) async-start(), calls=%async_computation.19 | async-start | bytes 1572864 | tf_op jit(solution)/shard_map/all_gather | solution.py:112
  131.6 107.7 %all-gather.22.cloned.1.call-start = ((), (), s32[]{:S(2)}) async-start(), calls=%async_computation.15 | async-start | bytes 2359296 | tf_op jit(solution)/shard_map/all_gather | solution.py:53
  132.3 269.4 %all-reduce.26.cloned.1.call-start = ((), (), s32[]{:S(2)}) async-start(), calls=%async_computation.36 | async-start | bytes 8388608 | tf_op jit(solution)/shard_map/psum | solution.py:136
  246.2 210.8 %all-gather.24.cloned.1.call-start = ((), (), s32[]{:S(2)}) async-start(), calls=%async_computation.16 | async-start | bytes 9437184 | tf_op jit(solution)/shard_map/all_gather | solution.py:54
  246.8 266.7 %all-gather.26.cloned.1.call-start = ((), (), s32[]{:S(2)}) async-start(), calls=%async_computation.17 | async-start | bytes 9437184 | tf_op jit(solution)/shard_map/all_gather | solution.py:55
  247.6 323.9 %all-gather.28.cloned.1.call-start = ((), (), s32[]{:S(2)}) async-start(), calls=%async_computation.18 | async-start | bytes 9437184 | tf_op jit(solution)/shard_map/all_gather | solution.py:56
  248.1 494.6 %all-reduce.24.cloned.1.call-start = ((), (), s32[]{:S(2)}) async-start(), calls=%async_computation.35 | async-start | bytes 8388608 | tf_op jit(solution)/shard_map/psum | solution.py:147
  587.2 381.9 %all-reduce.22.cloned.1.call-start = ((), (), s32[]{:S(2)}) async-start(), calls=%async_computation.34 | async-start | bytes 8388608 | tf_op jit(solution)/shard_map/psum | solution.py:176
  814.6 245.5 %reduce-scatter.12.cloned.1.call-start = ((), (), s32[]{:S(2)}) async-start(), calls=%async_computation.20 | async-start | bytes 1572864 | tf_op jit(solution)/shard_map/reduce_scatter | solution.py:253
  1016.1 100.8 %reduce-scatter.16.cloned.1.call-start = ((), (), s32[]{:S(2)}) async-start(), calls=%async_computation.22 | async-start | bytes 1572864 | tf_op jit(solution)/shard_map/reduce_scatter | solution.py:253
  1048.4 91.0 %reduce-scatter.14.cloned.1.call-start = ((), (), s32[]{:S(2)}) async-start(), calls=%async_computation.21 | async-start | bytes 1572864 | tf_op jit(solution)/shard_map/reduce_scatter | solution.py:259
  1049.0 112.9 %reduce-scatter.18.cloned.1.call-start = ((), (), s32[]{:S(2)}) async-start(), calls=%async_computation.23 | async-start | bytes 1572864 | tf_op jit(solution)/shard_map/reduce_scatter | solution.py:259
  1049.6 290.2 %reduce-scatter.26.cloned.1.call-start = ((), (), s32[]{:S(2)}) async-start(), calls=%async_computation.27 | async-start | bytes 2359296 | tf_op jit(solution)/shard_map/reduce_scatter | solution.py:347
  1057.1 284.5 %reduce-scatter.24.cloned.1.call-start = ((), (), s32[]{:S(2)}) async-start(), calls=%async_computation.26 | async-start | bytes 2359296 | tf_op jit(solution)/shard_map/reduce_scatter | solution.py:344
  1167.5 175.9 %reduce-scatter.22.cloned.1.call-start = ((), (), s32[]{:S(2)}) async-start(), calls=%async_computation.25 | async-start | bytes 2359296 | tf_op jit(solution)/shard_map/reduce_scatter | solution.py:341
  1214.1 131.2 %reduce-scatter.20.cloned.1.call-start = ((), (), s32[]{:S(2)}) async-start(), calls=%async_computation.24 | async-start | bytes 2359296 | tf_op jit(solution)/shard_map/reduce_scatter | solution.py:338
  1220.9 278.6 %all-reduce.20.cloned.1.call-start = ((), (), s32[]{:S(2)}) async-start(), calls=%async_computation.33 | async-start | bytes 8388608 | tf_op jit(solution)/shard_map/psum | solution.py:306
  1232.5 340.6 %reduce-scatter.32.cloned.1.call-start = ((), (), s32[]{:S(2)}) async-start(), calls=%async_computation.30 | async-start | bytes 9437184 | tf_op jit(solution)/shard_map/reduce_scatter | solution.py:356
  1262.3 385.9 %reduce-scatter.30.cloned.1.call-start = ((), (), s32[]{:S(2)}) async-start(), calls=%async_computation.29 | async-start | bytes 9437184 | tf_op jit(solution)/shard_map/reduce_scatter | solution.py:353
  1286.1 436.7 %reduce-scatter.28.cloned.1.call-start = ((), (), s32[]{:S(2)}) async-start(), calls=%async_computation.28 | async-start | bytes 9437184 | tf_op jit(solution)/shard_map/reduce_scatter | solution.py:350
  (122 other events, 2639.9 us)
Sparse Core Ops, SparseCore 0:
  9.9 30.5 all-gather.15
  42.4 27.8 all-gather.19
  72.2 27.8 all-gather.13
  141.0 21.2 all-gather.33
  164.4 21.2 all-gather.31
  187.8 21.2 all-gather.29
  211.0 28.1 all-gather.21
  246.4 155.3 all-reduce.25
  403.6 53.3 all-gather.23
  459.1 54.3 all-gather.25
  515.4 55.9 all-gather.27
  587.3 155.3 all-reduce.23
  814.7 154.3 all-reduce.21
  1016.2 43.8 reduce-scatter.11
  1062.2 54.6 reduce-scatter.15
  1141.5 20.3 reduce-scatter.17
  1165.5 41.2 reduce-scatter.25
  1209.9 41.2 reduce-scatter.23
  1254.8 41.2 reduce-scatter.21
  1299.3 41.6 reduce-scatter.19
  1344.1 155.2 all-reduce.19
  1502.8 70.2 reduce-scatter.31
  1576.9 71.2 reduce-scatter.29
  1651.5 71.2 reduce-scatter.27
  (2 shorter events, 38.8 us)
where the time goes:
time: 1740 us; the launch traced here: 1730 us
  waiting for transfers between devices  1160 us (67%)
  matrix products  306 us (18%)
  other arithmetic  101 us (6%)
  local copies, waits for them, and re-layouts  83.5 us (5%)
  blocking collectives  48.1 us (3%)
    psum x1, waiting for transfers between devices, one_micro(): lax.psum(jnp.einsum('scf,fd->scd', hidden, mat_down, preferred_element_ty...  155 us
    psum x1, waiting for transfers between devices, one_micro(): lax.psum(input_terms.astype(jnp.bfloat16), 'tp').astype(jnp.float32)  152 us
    psum x1, waiting for transfers between devices, one_micro(): lax.psum(mlp_terms.astype(jnp.bfloat16), 'tp').astype(jnp.float32)  150 us
    psum x1, waiting for transfers between devices, one_micro(): lax.psum(jnp.einsum('sce,ed->scd', head_low, mat_output, preferred_elemen...  142 us
    reduce_scatter x1, waiting for transfers between devices, per_device(): lax.psum_scatter(mat_sums[5].astype(jnp.bfloat16), ('fsdp', 'ctx'), scatt...  72.4 us
    reduce_scatter x1, waiting for transfers between devices, per_device(): lax.psum_scatter(mat_sums[4].astype(jnp.bfloat16), ('fsdp', 'ctx'), scatt...  71.8 us
    reduce_scatter x1, waiting for transfers between devices, per_device(): lax.psum_scatter(mat_sums[6].astype(jnp.bfloat16), ('fsdp', 'ctx'), scatt...  66 us
    reduce_scatter x2, waiting for transfers between devices, one_micro(): lax.psum_scatter(grad_keys_all.reshape(seq_count, full_len, local_width)....  54.5 us
  transfers between devices with their start and end apart: 26, of which 21 were waited for; matrix products, arithmetic and copies ran while one was open for 20% of the time, Pallas kernels for 0%

commit v1 on v0

v1 whole, which is shorter than its diff:
```python
import functools

import jax
import jax.numpy as jnp
from jax import lax
from jax.experimental import pallas as pl
from jax.experimental.pallas import tpu as pltpu
from jax.sharding import PartitionSpec as P

HD = 128
norm_eps = 1e-06
rope_theta = 500000.0
masked_value = -1e30
f32 = jnp.float32
bf16 = jnp.bfloat16


def dot(a, b, dims, out=f32):
    return lax.dot_general(a, b, (dims, ((), ())), preferred_element_type=f32).astype(out)


PIECE = 16
LAG = 1
CHUNK = 256


class Line:
    def __init__(self, axis, n, groups, buf, total, send, recv):
        self.axis, self.n, self.groups = axis, n, groups
        self.buf, self.total, self.send, self.recv = buf, total, send, recv
        self.i = lax.axis_index(axis)
        self.stages = 2 * n - 1

    def rows(self, group, c, count=1):
        return pl.ds(pl.multiple_of((group * self.n + c) * PIECE, PIECE), count * PIECE)

    def copy(self, way, step, group, c, source):
        rows = self.rows(group, c)
        return pltpu.make_async_remote_copy(
            src_ref=self.buf.at[source, rows],
            dst_ref=self.buf.at[0 if way == 0 else 2, rows],
            send_sem=self.send.at[way, step, group],
            recv_sem=self.recv.at[way, step, group],
            device_id={self.axis: self.i + (1 if way == 0 else -1)},
            device_id_type=pl.DeviceIdType.MESH,
        )

    def add(self, c, group, source):
        rows = self.rows(group, c)
        both = self.buf[1, rows].astype(f32) + self.buf[source, rows].astype(f32)
        self.buf[1, rows] = both.astype(bf16)

    def reduce_step(self, s, group):
        i, n = self.i, self.n

        @pl.when(i <= min(s - 1, n - 2))
        def _():
            c = n - s + i
            if s >= 2:

                @pl.when(i >= 1)
                def _():
                    self.copy(0, s - 2, group, c, 1).wait_recv()
                    self.add(c, group, 0)

            self.copy(0, s - 1, group, c, 1).start()

        @pl.when(i >= max(n - s, 1))
        def _():
            c = s + i - n
            if s >= 2:

                @pl.when(i <= n - 2)
                def _():
                    self.copy(1, s - 2, group, c, 1).wait_recv()
                    self.add(c, group, 2)

            self.copy(1, s - 1, group, c, 1).start()

    def finish(self, group, then):
        i, n = self.i, self.n
        rows = self.rows(group, i)
        self.total[...] = self.buf[1, rows].astype(f32)

        @pl.when(i >= 1)
        def _():
            self.copy(0, n - 2, group, i, 1).wait_recv()
            self.total[...] += self.buf[0, rows].astype(f32)

        @pl.when(i <= n - 2)
        def _():
            self.copy(1, n - 2, group, i, 1).wait_recv()
            self.total[...] += self.buf[2, rows].astype(f32)

        self.buf[1, rows] = then(group, self.total[...]).astype(bf16)

        @pl.when(i <= n - 2)
        def _():
            self.copy(0, n - 1, group, i, 1).start()

        @pl.when(i >= 1)
        def _():
            self.copy(1, n - 1, group, i, 1).start()

    def gather_step(self, s, group):
        i, n = self.i, self.n

        @pl.when(i >= s - 1)
        def _():
            c = i - s + 1
            self.copy(0, n + s - 3, group, c, 0).wait_recv()
            if s <= n - 1:

                @pl.when(i <= n - 2)
                def _():
                    self.copy(0, n + s - 2, group, c, 0).start()

        @pl.when(i <= n - s)
        def _():
            c = i + s - 1
            self.copy(1, n + s - 3, group, c, 2).wait_recv()
            if s <= n - 1:

                @pl.when(i >= 1)
                def _():
                    self.copy(1, n + s - 2, group, c, 2).start()

    def sent(self, group):
        i, n = self.i, self.n
        for s in range(1, n):

            @pl.when(i <= min(s - 1, n - 2))
            def _():
                self.copy(0, s - 1, group, n - s + i, 1).wait_send()

            @pl.when(i >= max(n - s, 1))
            def _():
                self.copy(1, s - 1, group, s + i - n, 1).wait_send()

            @pl.when((i >= s - 1) & (i <= n - 2))
            def _():
                self.copy(0, n + s - 2, group, i - s + 1, 1 if s == 1 else 0).wait_send()

            @pl.when((i <= n - s) & (i >= 1))
            def _():
                self.copy(1, n + s - 2, group, i + s - 1, 1 if s == 1 else 2).wait_send()

    def piece(self, group, c):
        slot = jnp.where(c < self.i, 0, jnp.where(c > self.i, 2, 1))
        return self.buf[slot, self.rows(group, c)]

    def piece_ref(self, group, c):
        slot = jnp.where(c < self.i, 0, jnp.where(c > self.i, 2, 1))
        return self.buf.at[slot, self.rows(group, c)]

    def tick(self, t, then, done):
        n = self.n

        def stage(index, body):
            group = t - index * LAG

            @pl.when((group >= 0) & (group < self.groups))
            def _():
                body(group)

        for s in range(1, n):
            stage(s - 1, functools.partial(self.reduce_step, s))
        stage(n - 1, lambda group: self.finish(group, then))
        for s in range(2, n):
            stage(n + s - 2, functools.partial(self.gather_step, s))

        def last(group):
            self.gather_step(n, group)
            self.sent(group)
            done(group)

        stage(2 * n - 2, last)

    def ticks(self):
        return self.groups + (2 * self.n - 2) * LAG


def greet(axis, n):
    i = lax.axis_index(axis)
    barrier = pltpu.get_barrier_semaphore()

    @pl.when(i >= 1)
    def _():
        pl.semaphore_signal(barrier, inc=1, device_id={axis: i - 1}, device_id_type=pl.DeviceIdType.MESH)

    @pl.when(i <= n - 2)
    def _():
        pl.semaphore_signal(barrier, inc=1, device_id={axis: i + 1}, device_id_type=pl.DeviceIdType.MESH)

    pl.semaphore_wait(barrier, jnp.minimum(i, 1) + jnp.minimum(n - 1 - i, 1))


def line_scratch(n, rows, width):
    sems = pltpu.SemaphoreType.DMA((2, 2 * n - 2, rows // (n * PIECE)))
    return [pltpu.VMEM((3, rows, width), bf16), pltpu.VMEM((PIECE, width), f32), sems, sems]


def params(collective_id):
    return pltpu.CompilerParams(
        collective_id=collective_id, has_side_effects=True, vmem_limit_bytes=60 << 20
    )


def scale_of(a):
    return lax.rsqrt(jnp.mean(a * a, axis=-1, keepdims=True) + norm_eps)


def attn_out_kernel(n, head, w_out_t, x, gain, attention, mlp_in, buf, total, send, recv):
    rows, width = x.shape
    groups = rows // (n * PIECE)
    line = Line("tp", n, groups, buf, total, send, recv)
    greet("tp", n)
    per_chunk = CHUNK // (n * PIECE)
    tile = 512

    def done(group):
        for c in range(n):
            at = line.rows(group, c)
            low = line.piece(group, c)
            attention[at] = low
            a = low.astype(f32)
            mlp_in[at] = (x[at].astype(f32) + a * scale_of(a) * gain[...]).astype(bf16)

    @pl.loop(0, line.ticks())
    def _(t):
        @pl.when((t < groups) & (lax.rem(t, per_chunk) == 0))
        def _():
            at = pl.ds(pl.multiple_of(t * n * PIECE, CHUNK), CHUNK)

            @pl.loop(0, width // tile)
            def _(j):
                cols = pl.ds(pl.multiple_of(j * tile, tile), tile)
                buf[1, at, cols] = dot(head[at], w_out_t[cols], ((1,), (1,)), bf16)

        line.tick(t, lambda group, total: total, done)


def attn_out(head, w_out_t, x, gain, n):
    rows, width = x.shape
    vmem = pl.BlockSpec(memory_space=pltpu.VMEM)
    return pl.pallas_call(
        functools.partial(attn_out_kernel, n),
        out_shape=[jax.ShapeDtypeStruct(x.shape, bf16)] * 2,
        in_specs=[vmem] * 4,
        out_specs=[vmem] * 2,
        scratch_shapes=line_scratch(n, rows, width),
        compiler_params=params(1),
        cost_estimate=pl.CostEstimate(flops=100 * 10**9, bytes_accessed=20 << 20, transcendentals=0),
        name="attn_out",
    )(head, w_out_t, x, gain)


def local_copies(pairs, sems):
    copies = [pltpu.make_async_copy(a, b, sems.at[k]) for k, (a, b) in enumerate(pairs)]
    for copy in copies:
        copy.start()
    return copies


def mlp_kernel(
    n, mlp_in, grad, attn_own, gain_m, gain_a, w_g_hbm, w_u_hbm, w_d_hbm,
    down_out, down_low_out, hidden_out, gate_out, up_out, attn_low_out, mixed_own, gain_m_sum, gain_a_sum,
    buf, total, send, recv, w_g, w_u, w_d, mlp_rows, hidden, gate_low, up_low, down_low, gate_kept, up_kept,
    ready, w_sems, io_sems, piece_sems,
):
    rows, width = grad.shape
    units = w_g.shape[1]
    groups = rows // (n * PIECE)
    per_chunk = CHUNK // (n * PIECE)
    line = Line("tp", n, groups, buf, total, send, recv)
    i = line.i
    weights = local_copies([(w_g_hbm, w_g), (w_u_hbm, w_u), (w_d_hbm, w_d)], w_sems)
    gain_m_sum[...] = jnp.zeros_like(gain_m_sum)
    gain_a_sum[...] = jnp.zeros_like(gain_a_sum)
    greet("tp", n)
    offset = per_chunk + line.stages - 1
    tile = 512

    def chunk_rows(chunk):
        return pl.ds(pl.multiple_of(chunk * CHUNK, CHUNK), CHUNK)

    def hidden_copy(chunk):
        return pltpu.make_async_copy(hidden, hidden_out.at[chunk_rows(chunk)], io_sems.at[1])

    def back_copies(chunk):
        at = chunk_rows(chunk)
        return [
            pltpu.make_async_copy(gate_low, gate_out.at[at], io_sems.at[2]),
            pltpu.make_async_copy(up_low, up_out.at[at], io_sems.at[3]),
            pltpu.make_async_copy(down_low, down_low_out.at[at], io_sems.at[4]),
        ]

    def forward(chunk, first):
        at = chunk_rows(chunk)
        fetch = pltpu.make_async_copy(mlp_in.at[at], mlp_rows, io_sems.at[0])
        fetch.start()
        if first:
            weights[0].wait()
            weights[1].wait()
        else:
            hidden_copy(chunk - 1).wait()
        fetch.wait()

        @pl.loop(0, units // tile)
        def _(j):
            cols = pl.ds(pl.multiple_of(j * tile, tile), tile)
            gate = dot(mlp_rows[...], w_g[:, cols], ((1,), (0,)))
            up = dot(mlp_rows[...], w_u[:, cols], ((1,), (0,)))
            gate_kept[at, cols] = gate.astype(bf16)
            up_kept[at, cols] = up.astype(bf16)
            hidden[:, cols] = (gate / (1.0 + jnp.exp(-gate)) * up).astype(bf16)

        hidden_copy(chunk).start()
        if first:
            weights[2].wait()

        @pl.loop(0, width // tile)
        def _(j):
            cols = pl.ds(pl.multiple_of(j * tile, tile), tile)
            buf[1, at, cols] = dot(hidden[...], w_d[cols], ((1,), (1,)), bf16)

    def backward(chunk):
        at = chunk_rows(chunk)

        @pl.loop(0, units // tile)
        def _(j):
            cols = pl.ds(pl.multiple_of(j * tile, tile), tile)
            gate = gate_kept[at, cols].astype(f32)
            sig = 1.0 / (1.0 + jnp.exp(-gate))
            grad_hidden = dot(down_low[...], w_d[:, cols], ((1,), (0,)))
            up_low[:, cols] = (grad_hidden * gate * sig).astype(bf16)
            gate_low[:, cols] = (
                grad_hidden * up_kept[at, cols].astype(f32) * sig * (1.0 + gate * (1.0 - sig))
            ).astype(bf16)

        for copy in back_copies(chunk):
            copy.start()

        @pl.loop(0, width // tile)
        def _(j):
            cols = pl.ds(pl.multiple_of(j * tile, tile), tile)
            buf[1, at, cols] = (
                dot(gate_low[...], w_g[cols], ((1,), (1,))) + dot(up_low[...], w_u[cols], ((1,), (1,)))
            ).astype(bf16)

        for copy in back_copies(chunk):
            copy.wait()

    def pieces_out(group, out):
        return local_copies([(line.piece_ref(group, c), out.at[line.rows(group, c)]) for c in range(n)], piece_sems)

    def down_done(group):
        copies = pieces_out(group, down_out)
        for c in range(n):
            at = line.rows(group, c)
            branch = line.piece(group, c).astype(f32)
            r = scale_of(branch)
            g = grad[at].astype(f32)
            scaled = g * gain_m[...]
            inner = jnp.mean(scaled * branch, axis=-1, keepdims=True)
            gain_m_sum[...] += g * branch * r
            inside = pl.ds(pl.multiple_of((lax.rem(group, per_chunk) * n + c) * PIECE, PIECE), PIECE)
            down_low[inside] = (r * scaled - branch * (r * r * r) * inner).astype(bf16)
        for copy in copies:
            copy.wait()

    def attn_grad(group, total):
        at = pl.ds(pl.multiple_of(group * PIECE, PIECE), PIECE)
        mixed = grad[line.rows(group, i)].astype(f32) + total
        mixed_own[at] = mixed
        branch = attn_own[at].astype(f32)
        r = scale_of(branch)
        scaled = mixed * gain_a[...]
        inner = jnp.mean(scaled * branch, axis=-1, keepdims=True)
        gain_a_sum[...] += mixed * branch * r
        return r * scaled - branch * (r * r * r) * inner

    def attn_done(group):
        for copy in pieces_out(group, attn_low_out):
            copy.wait()

    forward(0, True)

    @pl.loop(0, offset + line.ticks())
    def _(t):
        back = t - offset

        @pl.when((back >= 0) & (back < groups) & (lax.rem(back + groups, per_chunk) == 0))
        def _():
            @pl.when(i >= 1)
            def _():
                pl.semaphore_wait(ready.at[0], 1)

            @pl.when(i <= n - 2)
            def _():
                pl.semaphore_wait(ready.at[1], 1)

        line.tick(back, attn_grad, attn_done)
        line.tick(t, lambda group, total: total, down_done)
        after = t + 1

        @pl.when((after < groups) & (lax.rem(after, per_chunk) == 0))
        def _():
            forward(lax.div(after, per_chunk), False)

        next_back = after - offset

        @pl.when((next_back >= 0) & (next_back < groups) & (lax.rem(next_back + groups, per_chunk) == 0))
        def _():
            @pl.when(i >= 1)
            def _():
                pl.semaphore_signal(
                    ready.at[1], inc=1, device_id={"tp": i - 1}, device_id_type=pl.DeviceIdType.MESH
                )

            @pl.when(i <= n - 2)
            def _():
                pl.semaphore_signal(
                    ready.at[0], inc=1, device_id={"tp": i + 1}, device_id_type=pl.DeviceIdType.MESH
                )

            backward(lax.div(next_back, per_chunk))

    hidden_copy(rows // CHUNK - 1).wait()


def mlp(mlp_in, grad, attn_own, gain_m, gain_a, w_g, w_u, w_d, n):
    rows, width = grad.shape
    units = w_g.shape[1]
    vmem, anywhere = pl.BlockSpec(memory_space=pltpu.VMEM), pl.BlockSpec(memory_space=pl.ANY)
    acts = jax.ShapeDtypeStruct((rows, width), bf16)
    inner = jax.ShapeDtypeStruct((rows, units), bf16)
    per_piece = jax.ShapeDtypeStruct((PIECE, width), f32)
    return pl.pallas_call(
        functools.partial(mlp_kernel, n),
        out_shape=[acts, acts, inner, inner, inner, acts, jax.ShapeDtypeStruct((rows // n, width), f32), per_piece, per_piece],
        in_specs=[anywhere] + [vmem] * 4 + [anywhere] * 3,
        out_specs=[anywhere] * 6 + [vmem] * 3,
        scratch_shapes=line_scratch(n, rows, width) + [
            pltpu.VMEM(w_g.shape, bf16), pltpu.VMEM(w_u.shape, bf16), pltpu.VMEM(w_d.shape, bf16),
            pltpu.VMEM((CHUNK, width), bf16),
            pltpu.VMEM((CHUNK, units), bf16), pltpu.VMEM((CHUNK, units), bf16), pltpu.VMEM((CHUNK, units), bf16),
            pltpu.VMEM((CHUNK, width), bf16),
            pltpu.VMEM((rows, units), bf16), pltpu.VMEM((rows, units), bf16),
            pltpu.SemaphoreType.REGULAR((2,)),
            pltpu.SemaphoreType.DMA((3,)), pltpu.SemaphoreType.DMA((5,)), pltpu.SemaphoreType.DMA((n,)),
        ],
        compiler_params=params(2),
        cost_estimate=pl.CostEstimate(flops=200 * 10**9, bytes_accessed=60 << 20, transcendentals=0),
        name="mlp",
    )(mlp_in, grad, attn_own, gain_m, gain_a, w_g, w_u, w_d)


def input_grad_kernel(n, grad_qkv, w_qkv_hbm, mixed_own, grad_out, buf, total, send, recv, w_qkv, w_sem, piece_sems):
    rows, width = buf.shape[1:]
    groups = rows // (n * PIECE)
    per_chunk = CHUNK // (n * PIECE)
    line = Line("tp", n, groups, buf, total, send, recv)
    fetch = pltpu.make_async_copy(w_qkv_hbm, w_qkv, w_sem)
    fetch.start()
    greet("tp", n)
    fetch.wait()
    tile = 512

    def own(group, total):
        return total + mixed_own[pl.ds(pl.multiple_of(group * PIECE, PIECE), PIECE)]

    def done(group):
        copies = local_copies(
            [(line.piece_ref(group, c), grad_out.at[line.rows(group, c)]) for c in range(n)], piece_sems
        )
        for copy in copies:
            copy.wait()

    @pl.loop(0, line.ticks())
    def _(t):
        @pl.when((t < groups) & (lax.rem(t, per_chunk) == 0))
        def _():
            at = pl.ds(pl.multiple_of(t * n * PIECE, CHUNK), CHUNK)

            @pl.loop(0, width // tile)
            def _(j):
                cols = pl.ds(pl.multiple_of(j * tile, tile), tile)
                buf[1, at, cols] = dot(grad_qkv[at], w_qkv[cols], ((1,), (1,)), bf16)

        line.tick(t, own, done)


def input_grad(grad_qkv, w_qkv, mixed_own, n):
    rows, width = grad_qkv.shape[0], w_qkv.shape[0]
    vmem, anywhere = pl.BlockSpec(memory_space=pltpu.VMEM), pl.BlockSpec(memory_space=pl.ANY)
    return pl.pallas_call(
        functools.partial(input_grad_kernel, n),
        out_shape=jax.ShapeDtypeStruct((rows, width), bf16),
        in_specs=[vmem, anywhere, vmem],
        out_specs=anywhere,
        scratch_shapes=line_scratch(n, rows, width) + [
            pltpu.VMEM(w_qkv.shape, bf16), pltpu.SemaphoreType.DMA, pltpu.SemaphoreType.DMA((n,)),
        ],
        compiler_params=params(3),
        cost_estimate=pl.CostEstimate(flops=100 * 10**9, bytes_accessed=20 << 20, transcendentals=0),
        name="input_grad",
    )(grad_qkv, w_qkv, mixed_own)


def small_sum(values, axis):
    n = lax.axis_size(axis)
    total = values
    for k in range(1, n):
        total = total + lax.ppermute(values, axis, [(a, (a + k) % n) for a in range(n)])
    return total


def rotation_tables(positions):
    half = HD // 2
    frequency = rope_theta ** (-jnp.arange(half, dtype=f32) * 2.0 / HD)
    angles = positions.astype(f32)[:, None] * frequency[None, :]
    return jnp.cos(angles)[:, None, :], jnp.sin(angles)[:, None, :]


def rotate(values, cosine, sine):
    half = HD // 2
    first, second = values[..., :half], values[..., half:]
    return jnp.concatenate([first * cosine - second * sine, second * cosine + first * sine], axis=-1)


def per_device(
    tokens, w_query, w_key, w_value, w_output, w_gate, w_up, w_down,
    gain_query, gain_key, gain_attn, gain_mlp, cotangent,
):
    micro_count, rows, width = tokens.shape
    local = w_query.shape[1]
    heads = local // HD
    ctx = lax.axis_size("ctx")
    ctx_rank = lax.axis_index("ctx")
    tp = lax.axis_size("tp")
    tp_rank = lax.axis_index("tp")
    positions = ctx_rank * rows + jnp.arange(rows, dtype=jnp.int32)
    cosine, sine = rotation_tables(positions)
    scale = HD ** (-0.5)
    gain_q = gain_query.astype(f32)
    gain_k = gain_key.astype(f32)
    gain_a = gain_attn.astype(f32)
    gain_m = gain_mlp.astype(f32)
    xy = ("fsdp", "ctx")

    def gather(w):
        return lax.all_gather(w, xy, axis=0, tiled=True)

    w_qkv = gather(jnp.concatenate([w_query, w_key, w_value], axis=1))
    w_out_t = gather(w_output.T)
    w_g = gather(w_gate)
    w_u = gather(w_up)
    w_down_t = gather(w_down.T)

    def rms(a):
        return lax.rsqrt(jnp.mean(a * a, axis=-1, keepdims=True) + norm_eps)

    blocks = range(ctx)
    key_pos = jnp.arange(rows, dtype=jnp.int32)
    causal = key_pos[None, :] <= key_pos[:, None]

    def allowed(j):
        return causal if j == 0 else jnp.broadcast_to(ctx_rank >= j, causal.shape)

    def split_heads(a):
        return a.reshape(rows, heads, HD)

    def attend(x):
        qkv = dot(x, w_qkv, ((1,), (0,)))
        queries, key_raw = qkv[:, :local], qkv[:, local : 2 * local]
        value_low = qkv[:, 2 * local :].astype(bf16)
        squares = jnp.stack([jnp.sum(queries * queries, axis=-1), jnp.sum(key_raw * key_raw, axis=-1)])
        squares = small_sum(squares, "tp")
        rq = lax.rsqrt(squares[0] / width + norm_eps)[:, None]
        rk = lax.rsqrt(squares[1] / width + norm_eps)[:, None]
        q_low = rotate(split_heads(queries * rq * gain_q), cosine, sine).astype(bf16)
        k_low = rotate(split_heads(key_raw * rk * gain_k), cosine, sine).astype(bf16)
        keys, values = [k_low], [split_heads(value_low)]
        for j in blocks[1:]:
            pairs = [(a, a + j) for a in range(ctx - j)]
            keys.append(lax.ppermute(k_low.reshape(rows, local), "ctx", pairs).reshape(k_low.shape))
            values.append(lax.ppermute(value_low, "ctx", pairs).reshape(k_low.shape))
        scores = [
            jnp.where(
                allowed(j)[None],
                jnp.einsum("qhd,khd->hqk", q_low, keys[j], preferred_element_type=f32) * scale,
                masked_value,
            )
            for j in blocks
        ]
        top = scores[0].max(-1, keepdims=True)
        for j in blocks[1:]:
            top = jnp.maximum(top, scores[j].max(-1, keepdims=True))
        exps = [jnp.exp(a - top) for a in scores]
        total = sum(a.sum(-1, keepdims=True) for a in exps)
        exps = [a.astype(bf16) for a in exps]
        weighted = sum(
            jnp.einsum("hqk,khd->qhd", exps[j], values[j], preferred_element_type=f32) for j in blocks
        )
        inverse = 1.0 / total
        head_out = weighted * jnp.transpose(inverse, (1, 0, 2))
        head_low = head_out.reshape(rows, local).astype(bf16)
        return head_low, (queries, key_raw, rq, rk, q_low, keys, values, exps, inverse, head_out)

    def attend_back(kept, grad_heads):
        queries, key_raw, rq, rk, q_low, keys, values, exps, inverse, head_out = kept
        delta = jnp.sum(split_heads(grad_heads.astype(f32)) * head_out, axis=-1)
        delta = jnp.transpose(delta)[:, :, None]
        heads_grad = split_heads(grad_heads)
        scaled_grad = (heads_grad.astype(f32) * jnp.transpose(inverse, (1, 0, 2))).astype(bf16)
        grad_q_rot = 0.0
        key_terms, value_terms = [], []
        for j in blocks:
            grad_probs = jnp.einsum("qhd,khd->hqk", heads_grad, values[j], preferred_element_type=f32)
            grad_scores = (exps[j].astype(f32) * inverse * (grad_probs - delta)).astype(bf16)
            grad_q_rot = grad_q_rot + jnp.einsum(
                "hqk,khd->qhd", grad_scores, keys[j], preferred_element_type=f32
            )
            key_terms.append(
                jnp.einsum("hqk,qhd->khd", grad_scores, q_low, preferred_element_type=f32) * scale
            )
            value_terms.append(
                jnp.einsum("hqk,qhd->khd", exps[j], scaled_grad, preferred_element_type=f32)
            )
        grad_q_rot = grad_q_rot * scale
        grad_k_rot, grad_values = key_terms[0], value_terms[0]
        for j in blocks[1:]:
            pairs = [(a, a - j) for a in range(j, ctx)]
            back_k = lax.ppermute(key_terms[j].reshape(rows, local).astype(bf16), "ctx", pairs)
            back_v = lax.ppermute(value_terms[j].reshape(rows, local).astype(bf16), "ctx", pairs)
            grad_k_rot = grad_k_rot + split_heads(back_k).astype(f32)
            grad_values = grad_values + split_heads(back_v).astype(f32)
        value_grad = grad_values.reshape(rows, local).astype(bf16)
        grad_qn = rotate(grad_q_rot, cosine, -sine).reshape(rows, local)
        grad_kn = rotate(grad_k_rot, cosine, -sine).reshape(rows, local)
        inner = jnp.stack(
            [
                jnp.sum(grad_qn * queries * gain_q, axis=-1),
                jnp.sum(grad_kn * key_raw * gain_k, axis=-1),
            ]
        )
        inner = small_sum(inner, "tp") / width
        grad_queries = (grad_qn * rq * gain_q - queries * rq**3 * inner[0][:, None]).astype(bf16)
        grad_keys = (grad_kn * rk * gain_k - key_raw * rk**3 * inner[1][:, None]).astype(bf16)
        gain_q_term = jnp.sum(grad_qn * queries * rq, axis=0)
        gain_k_term = jnp.sum(grad_kn * key_raw * rk, axis=0)
        return jnp.concatenate([grad_queries, grad_keys, value_grad], axis=1), gain_q_term, gain_k_term

    flat = (micro_count * rows, width)
    x_all, grad_all = tokens.reshape(flat), cotangent.reshape(flat)

    def own(a):
        a = a.reshape(flat[0] // (tp * PIECE), tp, PIECE, width)
        return lax.dynamic_index_in_dim(a, tp_rank, 1, keepdims=False).reshape(flat[0] // tp, width)

    attended = [attend(tokens[m]) for m in range(micro_count)]
    head_low = jnp.concatenate([a[0] for a in attended], axis=0)
    attention, mlp_in = attn_out(head_low, w_out_t, x_all, gain_a[None], tp)
    down, down_low, hidden, gate_low, up_low, attn_low, mixed_own, gain_m_sum, gain_a_sum = mlp(
        mlp_in, grad_all, own(attention), gain_m[None], gain_a[None], w_g, w_u, w_down_t, tp
    )
    att, down = attention.astype(f32), down.astype(f32)
    out = (x_all.astype(f32) + att * rms(att) * gain_a + down * rms(down) * gain_m).astype(bf16)

    def weight_grad(left, right):
        full = dot(left, right, ((0,), (0,)), bf16)
        return lax.psum_scatter(full, xy, scatter_dimension=0, tiled=True).astype(f32)

    d_down = weight_grad(down_low, hidden).T
    d_gate = weight_grad(mlp_in, gate_low)
    d_up = weight_grad(mlp_in, up_low)
    d_out = weight_grad(attn_low, head_low).T
    grad_heads = dot(attn_low, w_out_t, ((1,), (0,)), bf16)
    back = [
        attend_back(attended[m][1], grad_heads[m * rows : (m + 1) * rows]) for m in range(micro_count)
    ]
    grad_qkv = jnp.concatenate([b[0] for b in back], axis=0)
    d_qkv = weight_grad(x_all, grad_qkv)
    grad_tokens = input_grad(grad_qkv, w_qkv, mixed_own, tp)
    gain_a_total = lax.psum(jnp.sum(gain_a_sum, axis=0), xy + ("tp",))
    gain_q_total, gain_k_total, gain_m_total = lax.psum(
        (sum(b[1] for b in back), sum(b[2] for b in back), jnp.sum(gain_m_sum, axis=0)), xy
    )
    return (
        out.reshape(tokens.shape),
        grad_tokens.reshape(tokens.shape),
        d_qkv[:, :local], d_qkv[:, local : 2 * local], d_qkv[:, 2 * local :],
        d_out, d_gate, d_up, d_down,
        gain_q_total, gain_k_total, gain_a_total, gain_m_total,
    )


def solution(mesh):
    rows, cols = P(("fsdp", "ctx"), "tp"), P("tp", ("fsdp", "ctx"))
    acts = P("fsdp", "ctx", None)
    in_specs = (acts, rows, rows, rows, cols, rows, rows, cols, P("tp"), P("tp"), P(), P(), acts)
    out_specs = (acts, acts, rows, rows, rows, cols, rows, rows, cols, P("tp"), P("tp"), P(), P())
    return jax.shard_map(
        per_device, mesh=mesh, in_specs=in_specs, out_specs=out_specs, check_vma=False
    )
```

time: 1740 us -> 962 us (0.55)
  waiting for transfers between devices: 1160 us -> 76 us
  Pallas kernels: 0 us -> 475 us
  matrix products: 306 us -> 142 us
  local copies, waits for them, and re-layouts: 83.5 us -> 61.1 us
  other arithmetic: 101 us -> 79.8 us
  starting transfers between devices: 14.1 us -> 34.6 us
  blocking collectives: 48.1 us -> 67.7 us
    psum x4 -> x0, waiting for transfers between devices: 599 us -> none  [the longest x1 155 us: one_micro(): lax.psum(jnp.einsum('scf,fd->scd', hidden, mat_down, preferred_element_ty...]
    pallas_call x0 -> x3, Pallas kernels: none -> 475 us  [the longest x1 245 us: mlp(): pl.pallas_call(functools.partial(mlp_kernel, n), out_shape=[acts, acts, i...]
    reduce_scatter x11 -> x5, waiting for transfers between devices: 301 us -> 16.6 us  [weight_grad(): lax.psum_scatter(full, xy, scatter_dimension=0, tiled=True).astype(f32)]
    all_gather x11 -> x5, waiting for transfers between devices: 258 us -> 44.2 us  [gather(): return lax.all_gather(w, xy, axis=0, tiled=True)]
    dot_general x56 -> x32, matrix products: 306 us -> 142 us  [the longest x8 86 us: dot(): lax.dot_general(a, b, (dims, ((), ())), preferred_element_type=f32)]
    ppermute x0 -> x20, starting transfers between devices: none -> 34.2 us  [the longest x12 18 us: small_sum(): lax.ppermute(values, axis, [(a, (a + k) % n) for a in range(n)])]
    psum x3 -> x2, blocking collectives: 48.1 us -> 67.7 us  [the longest x1 41.5 us: per_device(): gain_a_total = lax.psum(jnp.sum(gain_a_sum, axis=0), xy + ('tp',))]
    unnamed x253 -> x198, local copies, waits for them, and re-layouts: 37.8 us -> 21.4 us
  transfers between devices with their start and end apart: 26 -> 30, of which waited for: 21 -> 7; matrix products, arithmetic and copies ran while one was open for 20% -> 25% of each run, Pallas kernels for 0% -> 24%
where the time goes in v1:
time: 962 us; the launch traced here: 952 us
  Pallas kernels  475 us (49%)
  matrix products  142 us (15%)
  other arithmetic  79.8 us (8%)
  waiting for transfers between devices  76 us (8%)
  blocking collectives  67.7 us (7%)
  local copies, waits for them, and re-layouts  61.1 us (6%)
  starting transfers between devices  34.6 us (4%)
  between operations  16.1 us (2%)
    pallas_call x1, Pallas kernels, mlp(): pl.pallas_call(functools.partial(mlp_kernel, n), out_shape=[acts, acts, i...  245 us
    pallas_call x1, Pallas kernels, input_grad(): pl.pallas_call(functools.partial(input_grad_kernel, n), out_shape=jax.Sha...  115 us
    pallas_call x1, Pallas kernels, attn_out(): pl.pallas_call(functools.partial(attn_out_kernel, n), out_shape=[jax.Shap...  115 us
    dot_general x8, matrix products, dot(): lax.dot_general(a, b, (dims, ((), ())), preferred_element_type=f32)  86 us
    all_gather x5, waiting for transfers between devices, gather(): return lax.all_gather(w, xy, axis=0, tiled=True)  44.2 us
    psum x1, blocking collectives, per_device(): gain_a_total = lax.psum(jnp.sum(gain_a_sum, axis=0), xy + ('tp',))  41.5 us
    psum x1, blocking collectives, per_device(): lax.psum((sum((b[1] for b in back)), sum((b[2] for b in back)), jnp.sum(g...  26.3 us
    unnamed x198, local copies, waits for them, and re-layouts  21.4 us
  transfers between devices with their start and end apart: 30, of which 7 were waited for; matrix products, arithmetic and copies ran while one was open for 25% of the time, Pallas kernels for 24%

profile of v1, /device:TPU:0, one launch (start us, length us, event | category | flops | bytes accessed | tf_op | source)
XLA Modules:
  0.0 952.2 jit_solution(9055375787370774952)
XLA Ops:
  18.6 40.1 %all-gather.6.cloned.1.call-done.w_qkv_hbm = bf16[2048,1536]{1,0:T(8,128)(2,1)} async-done(((bf16[256,1536]{1,0:T(8,128)(2,1)}), bf16[2048,1536]{1,0:T(8,128)(2,1)}) %all-gather.6.cloned.1.call-update) | async-done | bytes 6291472 | tf_op jit(solution)/shard_map/all_gather | solution.py:553
  58.8 6.9 convolution_bitcast_fusion.1
  80.7 3.9 collective-permute-start.4
  94.9 3.4 fusion.88
  126.9 3.6 collective-permute-done.3
  132.4 4.2 fusion.12
  140.6 7.7 collective-permute-done.8
  158.9 114.6 %attn_out.1 = (bf16[1024,2048]{1,0:T(8,128)(2,1)}, bf16[1024,2048]{1,0:T(8,128)(2,1)}) custom-call(bf16[1024,512]{1,0:T(8,128)(2,1)} %pad_maximum_fusion.head, bf16[2048,512]{1,0:T(8,128)(2,1)} %all-gather.8.cloned.1.call-done.w_out_t, bf16[1024,2048]{1,0:T(8,128)(2,1)} %bitcast.284, f32[1,2048]{1,0:T(1,128)} %bitcast.327), custom_call_target="tpu_custom_call" | custom-call | flops 99999997952 | bytes 20971520 | tf_op jit(solution)/shard_map/attn_out/pallas_call | solution.py:246
  275.9 4.1 all-gather.12.cloned.1.call-done.w_u_hbm
  279.9 244.7 %mlp.1 = (bf16[1024,2048]{1,0:T(8,128)(2,1)}, bf16[1024,2048]{1,0:T(8,128)(2,1)}, bf16[1024,2048]{1,0:T(8,128)(2,1)}, bf16[1024,2048]{1,0:T(8,128)(2,1)}, bf16[1...) custom-call(bf16[1024,2048]{1,0:T(8,128)(2,1)} %get-tuple-element.25, ...), custom_call_target="tpu_custom_call" | custom-call | flops 199999995904 | bytes 62914560 | tf_op jit(solution)/shard_map/mlp/pallas_call | solution.py:439
  524.7 4.7 convolution_convert_fusion.5
  537.0 3.8 convolution_convert_fusion.4
  559.4 3.8 fusion.27
  623.6 24.7 %fusion.7 = bf16[2048,1536]{0,1:T(8,128)(2,1)} fusion(bf16[1024,2048]{1,0:T(8,128)(2,1)S(1)} %bitcast.285, bf16[512,512]{1,0:T(8,128)(2,1)S(1)} %copy-done.51, bf16[512,512]{1,0:T(8,128)(2,1)S(1)} %copy-done.47, bf16[512,512]{1,0:T(8,128)(2,1)S(1)} %copy-done.45, bf16[512,512]{1,0:T(8,128)(2,1)S(1)} %copy-done.49, ...), kind=kOutput, calls=%fused_computation.15 | convolution fusion | flops 6464471040 | bytes 13631488 | tf_op jit(solution)/shard_map/dot_general | solution.py:19
  648.3 14.3 %convolution_convert_fusion = bf16[2048,2048]{1,0:T(8,128)(2,1)} fusion(bf16[1024,2048]{1,0:T(8,128)(2,1)} %get-tuple-element.31, bf16[1024,2048]{1,0:T(8,128)(2,1)} %get-tuple-element.32), kind=kOutput, calls=%fused_computation.11 | convolution fusion | flops 8594128896 | bytes 16777216 | tf_op jit(solution)/shard_map/dot_general | solution.py:19
  662.7 14.4 %convolution_convert_fusion.1 = bf16[2048,2048]{1,0:T(8,128)(2,1)} fusion(bf16[1024,2048]{1,0:T(8,128)(2,1)} %get-tuple-element.25.mlp_in, bf16[1024,2048]{1,0:T(8,128)(2,1)} %get-tuple-element.30), kind=kOutput, calls=%fused_computation.12 | convolution fusion | flops 8594128896 | bytes 16777216 | tf_op jit(solution)/shard_map/dot_general | solution.py:19
  680.6 13.8 %convolution_convert_fusion.2 = bf16[2048,2048]{1,0:T(8,128)(2,1)} fusion(bf16[1024,2048]{1,0:T(8,128)(2,1)S(1)} %copy-done.94, bf16[1024,2048]{1,0:T(8,128)(2,1)} %get-tuple-element.29), kind=kOutput, calls=%fused_computation.13 | convolution fusion | flops 8594128896 | bytes 16777216 | tf_op jit(solution)/shard_map/dot_general | solution.py:19
  695.4 41.5 %psum.30 = f32[2048]{0:T(1024)} all-reduce(f32[2048]{0:T(1024)S(1)} %reduce_sum.218), channel_id=1, replica_groups=mesh['fsdp'=4,'ctx'=2,'tp'=4] {'fsdp','ctx','tp'}, use_global_device_ids=true, to_apply=%region_32.33 | all-reduce | flops 2048 | bytes 16384 | tf_op jit(solution)/shard_map/psum | solution.py:686
  740.4 6.7 fusion.4
  747.1 26.3 %all-reduce = (f32[512]{0:T(512)}, f32[512]{0:T(512)}, f32[2048]{0:T(1024)}) all-reduce(f32[512]{0:T(512)S(1)} %add.265, f32[512]{0:T(512)S(1)} %add.266, f32[2048]{0:T(1024)S(1)} %reduce_sum.219), channel_id=1, replica_groups=mesh['fsdp'=4,'ctx'=2,'tp'=4] {'fsdp','ctx'}, use_global_device_ids=true, to_apply=%region_27.28 | all-reduce | flops 3072 | bytes 24576 | tf_op jit(solution)/shard_map/psum | solution.py:687
  773.4 19.6 %maximum_maximum_fusion.grad_qkv = bf16[1024,1536]{1,0:T(8,128)(2,1)} fusion(bf16[512,512]{1,0:T(8,128)(2,1)S(1)} %copy-done.52, bf16[512,512]{1,0:T(8,128)(2,1)S(1)} %copy-done.48, bf16[512,512]{1,0:T(8,128)(2,1)S(1)} %copy-done.46, bf16[512,512]{1,0:T(8,128)(2,1)S(1)} %copy-done.50, bf16[512,512]{1,0:T(8,128)(2,1)S(1)} %copy-done.44, ...), kind=kLoop, calls=%fused_computation.42 | loop fusion | flops 18874368 | bytes 6291456 | tf_op jit(solution)/shard_map/concatenate | solution.py:683
  793.0 115.5 %input_grad.1 = bf16[1024,2048]{1,0:T(8,128)(2,1)} custom-call(bf16[1024,1536]{1,0:T(8,128)(2,1)} %maximum_maximum_fusion.grad_qkv, bf16[2048,1536]{1,0:T(8,128)(2,1)} %all-gather.6.cloned.1.call-done.w_qkv_hbm, f32[256,2048]{1,0:T(8,128)} %get-tuple-element.28.mixed_own), custom_call_target="tpu_custom_call" | custom-call | flops 99999997952 | bytes 20971520 | tf_op jit(solution)/shard_map/input_grad/pallas_call | solution.py:497
  920.8 16.5 %reduce-scatter.10.cloned.1.call-done = bf16[256,2048]{1,0:T(8,128)(2,1)} async-done(((bf16[2048,2048]{1,0:T(8,128)(2,1)}), bf16[256,2048]{1,0:T(8,128)(2,1)}) %reduce-scatter.10.cloned.1.call-update) | async-done | bytes 1048592 | tf_op jit(solution)/shard_map/reduce_scatter | solution.py:673
  940.1 4.8 copy.320
  (363 shorter events, 192.6 us)
Async XLA Ops:
  7.2 51.5 %all-gather.6.cloned.1.call-start = ((), (), s32[]{:S(2)}) async-start(), calls=%async_computation.5 | async-start | bytes 7077888 | tf_op jit(solution)/shard_map/all_gather | solution.py:553
  9.3 149.5 %all-gather.8.cloned.1.call-start = ((), (), s32[]{:S(2)}) async-start(), calls=%async_computation.6 | async-start | bytes 2359296 | tf_op jit(solution)/shard_map/all_gather | solution.py:553
  11.2 264.6 %all-gather.14.cloned.1.call-start = ((), (), s32[]{:S(2)}) async-start(), calls=%async_computation.9 | async-start | bytes 9437184 | tf_op jit(solution)/shard_map/all_gather | solution.py:553
  13.6 262.3 %all-gather.10.cloned.1.call-start = ((), (), s32[]{:S(2)}) async-start(), calls=%async_computation.7 | async-start | bytes 9437184 | tf_op jit(solution)/shard_map/all_gather | solution.py:553
  14.2 265.8 %all-gather.12.cloned.1.call-start = ((), (), s32[]{:S(2)}) async-start(), calls=%async_computation.8 | async-start | bytes 9437184 | tf_op jit(solution)/shard_map/all_gather | solution.py:553
  14.7 893.7 %reduce-scatter.8.cloned.1.call-start = ((), (), s32[]{:S(2)}) async-start(), calls=%async_computation.11 | async-start | bytes 2359296 | tf_op jit(solution)/shard_map/reduce_scatter | solution.py:673
  66.0 12.0 %collective-permute-start = (f32[2,512]{1,0:T(2,128)S(1)}, f32[2,512]{1,0:T(2,128)S(1)}, u32[]{:S(2)}, u32[]{:S(2)}) collective-permute-start(f32[2,512]{1,0:T(2,128)S(1)} %pad_maximum_fusion.4), channel_id=1, source_target_pairs={{0,1},{1,2},{2,3},{3,0},{4,5},{5,6},{6,7},{7,4},{8,9},{9,10},{10,1... | collective-permute-start | bytes 12296 | tf_op jit(solution)/shard_map/ppermute | solution.py:515
  67.5 13.2 %collective-permute-start.1 = (f32[2,512]{1,0:T(2,128)S(1)}, f32[2,512]{1,0:T(2,128)S(1)}, u32[]{:S(2)}, u32[]{:S(2)}) collective-permute-start(f32[2,512]{1,0:T(2,128)S(1)} %pad_maximum_fusion.4), channel_id=1, source_target_pairs={{0,2},{1,3},{2,0},{3,1},{4,6},{5,7},{6,4},{7,5},{8,10},{9,11},{10,... | collective-permute-start | bytes 12296 | tf_op jit(solution)/shard_map/ppermute | solution.py:515
  69.9 14.7 %collective-permute-start.2 = (f32[2,512]{1,0:T(2,128)S(1)}, f32[2,512]{1,0:T(2,128)S(1)}, u32[]{:S(2)}, u32[]{:S(2)}) collective-permute-start(f32[2,512]{1,0:T(2,128)S(1)} %pad_maximum_fusion.4), channel_id=1, source_target_pairs={{0,3},{1,0},{2,1},{3,2},{4,7},{5,4},{6,5},{7,6},{8,11},{9,8},{10,9... | collective-permute-start | bytes 12296 | tf_op jit(solution)/shard_map/ppermute | solution.py:515
  75.0 11.7 %collective-permute-start.5 = (f32[2,512]{1,0:T(2,128)S(1)}, f32[2,512]{1,0:T(2,128)S(1)}, u32[]{:S(2)}, u32[]{:S(2)}) collective-permute-start(f32[2,512]{1,0:T(2,128)S(1)} %pad_maximum_fusion.5), channel_id=1, source_target_pairs={{0,1},{1,2},{2,3},{3,0},{4,5},{5,6},{6,7},{7,4},{8,9},{9,10},{10,1... | collective-permute-start | bytes 12296 | tf_op jit(solution)/shard_map/ppermute | solution.py:515
  75.7 11.1 %collective-permute-start.6 = (f32[2,512]{1,0:T(2,128)S(1)}, f32[2,512]{1,0:T(2,128)S(1)}, u32[]{:S(2)}, u32[]{:S(2)}) collective-permute-start(f32[2,512]{1,0:T(2,128)S(1)} %pad_maximum_fusion.5), channel_id=1, source_target_pairs={{0,2},{1,3},{2,0},{3,1},{4,6},{5,7},{6,4},{7,5},{8,10},{9,11},{10,... | collective-permute-start | bytes 12296 | tf_op jit(solution)/shard_map/ppermute | solution.py:515
  80.7 56.5 %collective-permute-start.4 = (bf16[512,512]{1,0:T(8,128)(2,1)}, bf16[512,512]{1,0:T(8,128)(2,1)}, u32[]{:S(2)}, u32[]{:S(2)}) collective-permute-start(bf16[512,512]{1,0:T(8,128)(2,1)} %slice.266), channel_id=1, source_target_pairs={{0,4},{1,5},{2,6},{3,7},{8,12},{9,13},{10,14},{11,15},{16,20},{17,... | collective-permute-start | bytes 1572872 | tf_op jit(solution)/shard_map/ppermute | solution.py:588
  84.6 70.3 %collective-permute-start.9 = (bf16[512,512]{1,0:T(8,128)(2,1)}, bf16[512,512]{1,0:T(8,128)(2,1)}, u32[]{:S(2)}, u32[]{:S(2)}) collective-permute-start(bf16[512,512]{1,0:T(8,128)(2,1)} %slice.265), channel_id=1, source_target_pairs={{0,4},{1,5},{2,6},{3,7},{8,12},{9,13},{10,14},{11,15},{16,20},{17,... | collective-permute-start | bytes 1572872 | tf_op jit(solution)/shard_map/ppermute | solution.py:588
  103.2 27.4 %collective-permute-start.3 = (bf16[512,512]{0,1:T(8,128)(2,1)}, bf16[512,512]{0,1:T(8,128)(2,1)}, u32[]{:S(2)}, u32[]{:S(2)}) collective-permute-start(bf16[512,512]{0,1:T(8,128)(2,1)} %bitcast.297), channel_id=1, source_target_pairs={{0,4},{1,5},{2,6},{3,7},{8,12},{9,13},{10,14},{11,15},{16,20},{17,... | collective-permute-start | bytes 1572872 | tf_op jit(solution)/shard_map/ppermute | solution.py:587
  118.8 29.5 %collective-permute-start.8 = (bf16[512,512]{0,1:T(8,128)(2,1)}, bf16[512,512]{0,1:T(8,128)(2,1)}, u32[]{:S(2)}, u32[]{:S(2)}) collective-permute-start(bf16[512,512]{0,1:T(8,128)(2,1)} %bitcast.295), channel_id=1, source_target_pairs={{0,4},{1,5},{2,6},{3,7},{8,12},{9,13},{10,14},{11,15},{16,20},{17,... | collective-permute-start | bytes 1572872 | tf_op jit(solution)/shard_map/ppermute | solution.py:587
  557.6 27.4 %collective-permute-start.15 = (bf16[512,512]{0,1:T(8,128)(2,1)}, bf16[512,512]{0,1:T(8,128)(2,1)}, u32[]{:S(2)}, u32[]{:S(2)}) collective-permute-start(bf16[512,512]{0,1:T(8,128)(2,1)} %bitcast.296), channel_id=1, source_target_pairs={{4,0},{5,1},{6,2},{7,3},{12,8},{13,9},{14,10},{15,11},{20,16},{21,... | collective-permute-start | bytes 1572872 | tf_op jit(solution)/shard_map/ppermute | solution.py:635
  572.0 17.8 %collective-permute-start.10 = (bf16[512,512]{0,1:T(8,128)(2,1)}, bf16[512,512]{0,1:T(8,128)(2,1)}, u32[]{:S(2)}, u32[]{:S(2)}) collective-permute-start(bf16[512,512]{0,1:T(8,128)(2,1)} %bitcast.298), channel_id=1, source_target_pairs={{4,0},{5,1},{6,2},{7,3},{12,8},{13,9},{14,10},{15,11},{20,16},{21,... | collective-permute-start | bytes 1572872 | tf_op jit(solution)/shard_map/ppermute | solution.py:635
  576.7 333.8 %reduce-scatter.6.cloned.1.call-start = ((), (), s32[]{:S(2)}) async-start(), calls=%async_computation.10 | async-start | bytes 7077888 | tf_op jit(solution)/shard_map/reduce_scatter | solution.py:673
  576.8 26.1 %collective-permute-start.14 = (bf16[512,512]{0,1:T(8,128)(2,1)}, bf16[512,512]{0,1:T(8,128)(2,1)}, u32[]{:S(2)}, u32[]{:S(2)}) collective-permute-start(bf16[512,512]{0,1:T(8,128)(2,1)} %bitcast.300), channel_id=1, source_target_pairs={{4,0},{5,1},{6,2},{7,3},{12,8},{13,9},{14,10},{15,11},{20,16},{21,... | collective-permute-start | bytes 1572872 | tf_op jit(solution)/shard_map/ppermute | solution.py:636
  578.2 35.1 %collective-permute-start.19 = (bf16[512,512]{0,1:T(8,128)(2,1)}, bf16[512,512]{0,1:T(8,128)(2,1)}, u32[]{:S(2)}, u32[]{:S(2)}) collective-permute-start(bf16[512,512]{0,1:T(8,128)(2,1)} %bitcast.299), channel_id=1, source_target_pairs={{4,0},{5,1},{6,2},{7,3},{12,8},{13,9},{14,10},{15,11},{20,16},{21,... | collective-permute-start | bytes 1572872 | tf_op jit(solution)/shard_map/ppermute | solution.py:636
  608.4 11.1 %collective-permute-start.11 = (f32[2,512]{1,0:T(2,128)S(1)}, f32[2,512]{1,0:T(2,128)S(1)}, u32[]{:S(2)}, u32[]{:S(2)}) collective-permute-start(f32[2,512]{1,0:T(2,128)S(1)} %pad_maximum_fusion.6), channel_id=1, source_target_pairs={{0,1},{1,2},{2,3},{3,0},{4,5},{5,6},{6,7},{7,4},{8,9},{9,10},{10,1... | collective-permute-start | bytes 12296 | tf_op jit(solution)/shard_map/ppermute | solution.py:515
  648.3 266.4 %reduce-scatter.14.cloned.1.call-start = ((), (), s32[]{:S(2)}) async-start(), calls=%async_computation.14 | async-start | bytes 9437184 | tf_op jit(solution)/shard_map/reduce_scatter | solution.py:673
  662.7 255.3 %reduce-scatter.12.cloned.1.call-start = ((), (), s32[]{:S(2)}) async-start(), calls=%async_computation.13 | async-start | bytes 9437184 | tf_op jit(solution)/shard_map/reduce_scatter | solution.py:673
  677.1 260.2 %reduce-scatter.10.cloned.1.call-start = ((), (), s32[]{:S(2)}) async-start(), calls=%async_computation.12 | async-start | bytes 9437184 | tf_op jit(solution)/shard_map/reduce_scatter | solution.py:673
  (101 other events, 1512.9 us)
Sparse Core Ops, SparseCore 0:
  10.5 48.2 all-gather.5
  60.6 27.8 all-gather.7
  90.5 73.0 all-gather.13
  165.3 58.4 all-gather.9
  225.5 54.3 all-gather.11
  576.8 43.0 reduce-scatter.7
  648.4 63.3 reduce-scatter.5
  715.3 72.1 reduce-scatter.13
  791.4 71.2 reduce-scatter.11
  866.0 71.2 reduce-scatter.9

commit v2 on v1

--- a/solution.py
+++ b/solution.py
@@ -22,6 +22,8 @@
 PIECE = 16
 LAG = 1
 CHUNK = 256
+TILE_ROWS = 256
+TILES_PER_TICK = 3
 
 
 class Line:
@@ -180,9 +182,11 @@
         return self.groups + (2 * self.n - 2) * LAG
 
 
-def greet(axis, n):
+def greet(axis, n, others=()):
     i = lax.axis_index(axis)
     barrier = pltpu.get_barrier_semaphore()
+    for peer in others:
+        pl.semaphore_signal(barrier, inc=1, device_id=peer, device_id_type=pl.DeviceIdType.MESH)
 
     @pl.when(i >= 1)
     def _():
@@ -192,7 +196,7 @@
     def _():
         pl.semaphore_signal(barrier, inc=1, device_id={axis: i + 1}, device_id_type=pl.DeviceIdType.MESH)
 
-    pl.semaphore_wait(barrier, jnp.minimum(i, 1) + jnp.minimum(n - 1 - i, 1))
+    pl.semaphore_wait(barrier, len(others) + jnp.minimum(i, 1) + jnp.minimum(n - 1 - i, 1))
 
 
 def line_scratch(n, rows, width):
@@ -202,7 +206,7 @@
 
 def params(collective_id):
     return pltpu.CompilerParams(
-        collective_id=collective_id, has_side_effects=True, vmem_limit_bytes=60 << 20
+        collective_id=collective_id, has_side_effects=True, vmem_limit_bytes=63 << 20
     )
 
 
@@ -264,9 +268,9 @@
 
 def mlp_kernel(
     n, mlp_in, grad, attn_own, gain_m, gain_a, w_g_hbm, w_u_hbm, w_d_hbm,
-    down_out, down_low_out, hidden_out, gate_out, up_out, attn_low_out, mixed_own, gain_m_sum, gain_a_sum,
-    buf, total, send, recv, w_g, w_u, w_d, mlp_rows, hidden, gate_low, up_low, down_low, gate_kept, up_kept,
-    ready, w_sems, io_sems, piece_sems,
+    down_out, hidden_out, attn_low_out, weights_out, mixed_own, gain_m_sum, gain_a_sum,
+    buf, total, send, recv, w_g, w_u, w_d, mlp_rows, hidden, down_low, gate, up, tiles,
+    ready, w_sems, io_sems, piece_sems, tile_sems,
 ):
     rows, width = grad.shape
     units = w_g.shape[1]
@@ -287,14 +291,6 @@
     def hidden_copy(chunk):
         return pltpu.make_async_copy(hidden, hidden_out.at[chunk_rows(chunk)], io_sems.at[1])
 
-    def back_copies(chunk):
-        at = chunk_rows(chunk)
-        return [
-            pltpu.make_async_copy(gate_low, gate_out.at[at], io_sems.at[2]),
-            pltpu.make_async_copy(up_low, up_out.at[at], io_sems.at[3]),
-            pltpu.make_async_copy(down_low, down_low_out.at[at], io_sems.at[4]),
-        ]
-
     def forward(chunk, first):
         at = chunk_rows(chunk)
         fetch = pltpu.make_async_copy(mlp_in.at[at], mlp_rows, io_sems.at[0])
@@ -309,11 +305,11 @@
         @pl.loop(0, units // tile)
         def _(j):
             cols = pl.ds(pl.multiple_of(j * tile, tile), tile)
-            gate = dot(mlp_rows[...], w_g[:, cols], ((1,), (0,)))
-            up = dot(mlp_rows[...], w_u[:, cols], ((1,), (0,)))
-            gate_kept[at, cols] = gate.astype(bf16)
-            up_kept[at, cols] = up.astype(bf16)
-            hidden[:, cols] = (gate / (1.0 + jnp.exp(-gate)) * up).astype(bf16)
+            gate_proj = dot(mlp_rows[...], w_g[:, cols], ((1,), (0,)))
+            up_proj = dot(mlp_rows[...], w_u[:, cols], ((1,), (0,)))
+            gate[at, cols] = gate_proj.astype(bf16)
+            up[at, cols] = up_proj.astype(bf16)
+            hidden[:, cols] = (gate_proj / (1.0 + jnp.exp(-gate_proj)) * up_proj).astype(bf16)
 
         hidden_copy(chunk).start()
         if first:
@@ -330,26 +326,61 @@
         @pl.loop(0, units // tile)
         def _(j):
             cols = pl.ds(pl.multiple_of(j * tile, tile), tile)
-            gate = gate_kept[at, cols].astype(f32)
-            sig = 1.0 / (1.0 + jnp.exp(-gate))
-            grad_hidden = dot(down_low[...], w_d[:, cols], ((1,), (0,)))
-            up_low[:, cols] = (grad_hidden * gate * sig).astype(bf16)
-            gate_low[:, cols] = (
-                grad_hidden * up_kept[at, cols].astype(f32) * sig * (1.0 + gate * (1.0 - sig))
-            ).astype(bf16)
-
-        for copy in back_copies(chunk):
-            copy.start()
+            gate_proj, up_proj = gate[at, cols].astype(f32), up[at, cols].astype(f32)
+            sig = 1.0 / (1.0 + jnp.exp(-gate_proj))
+            grad_hidden = dot(down_low[at], w_d[:, cols], ((1,), (0,)))
+            up[at, cols] = (grad_hidden * gate_proj * sig).astype(bf16)
+            gate[at, cols] = (grad_hidden * up_proj * sig * (1.0 + gate_proj * (1.0 - sig))).astype(bf16)
 
         @pl.loop(0, width // tile)
         def _(j):
             cols = pl.ds(pl.multiple_of(j * tile, tile), tile)
             buf[1, at, cols] = (
-                dot(gate_low[...], w_g[cols], ((1,), (1,))) + dot(up_low[...], w_u[cols], ((1,), (1,)))
+                dot(gate[at], w_g[cols], ((1,), (1,))) + dot(up[at], w_u[cols], ((1,), (1,)))
             ).astype(bf16)
 
-        for copy in back_copies(chunk):
-            copy.wait()
+    whole = pl.ds(0, rows)
+    late_in = [(hidden_out, w_g.at[whole]), (mlp_in, w_u.at[whole])]
+    per_part = width // TILE_ROWS
+
+    def tile_copy(k, slot):
+        part, block = lax.div(k, per_part), lax.rem(k, per_part)
+        return pltpu.make_async_copy(
+            tiles.at[slot],
+            weights_out.at[
+                pl.ds(pl.multiple_of(block * TILE_ROWS, TILE_ROWS), TILE_ROWS),
+                pl.ds(pl.multiple_of(part * units, units), units),
+            ],
+            tile_sems.at[slot],
+        )
+
+    def weight_tile(k):
+        slot = lax.rem(k, 2)
+        block = pl.ds(pl.multiple_of(lax.rem(k, per_part) * TILE_ROWS, TILE_ROWS), TILE_ROWS)
+
+        @pl.when(k >= 2)
+        def _():
+            tile_copy(k - 2, slot).wait()
+
+        def fill(left, right):
+            @pl.loop(0, units // tile)
+            def _(j):
+                cols = pl.ds(pl.multiple_of(j * tile, tile), tile)
+                tiles[slot, :, cols] = dot(left[whole, block], right[whole, cols], ((0,), (0,)), bf16)
+
+        @pl.when(k < per_part)
+        def _():
+            fill(down_low, w_g)
+
+        @pl.when((k >= per_part) & (k < 2 * per_part))
+        def _():
+            fill(w_u, gate)
+
+        @pl.when(k >= 2 * per_part)
+        def _():
+            fill(w_u, up)
+
+        tile_copy(k, slot).start()
 
     def pieces_out(group, out):
         return local_copies([(line.piece_ref(group, c), out.at[line.rows(group, c)]) for c in range(n)], piece_sems)
@@ -364,8 +395,7 @@
             scaled = g * gain_m[...]
             inner = jnp.mean(scaled * branch, axis=-1, keepdims=True)
             gain_m_sum[...] += g * branch * r
-            inside = pl.ds(pl.multiple_of((lax.rem(group, per_chunk) * n + c) * PIECE, PIECE), PIECE)
-            down_low[inside] = (r * scaled - branch * (r * r * r) * inner).astype(bf16)
+            down_low[at] = (r * scaled - branch * (r * r * r) * inner).astype(bf16)
         for copy in copies:
             copy.wait()
 
@@ -426,7 +456,27 @@
 
             backward(lax.div(next_back, per_chunk))
 
-    hidden_copy(rows // CHUNK - 1).wait()
+        first_tick = offset + groups - per_chunk
+
+        @pl.when(after == first_tick)
+        def _():
+            hidden_copy(rows // CHUNK - 1).wait()
+            local_copies(late_in, w_sems)
+
+        @pl.when(t == first_tick)
+        def _():
+            for k, (source, target) in enumerate(late_in):
+                pltpu.make_async_copy(source, target, w_sems.at[k]).wait()
+
+        for m in range(TILES_PER_TICK):
+            k = (t - first_tick) * TILES_PER_TICK + m
+
+            @pl.when((k >= 0) & (k < 3 * per_part))
+            def _():
+                weight_tile(k)
+
+    for k in (3 * per_part - 2, 3 * per_part - 1):
+        tile_copy(k, k % 2).wait()
 
 
 def mlp(mlp_in, grad, attn_own, gain_m, gain_a, w_g, w_u, w_d, n):
@@ -438,17 +488,20 @@
     per_piece = jax.ShapeDtypeStruct((PIECE, width), f32)
     return pl.pallas_call(
         functools.partial(mlp_kernel, n),
-        out_shape=[acts, acts, inner, inner, inner, acts, jax.ShapeDtypeStruct((rows // n, width), f32), per_piece, per_piece],
+        out_shape=[
+            acts, inner, acts, jax.ShapeDtypeStruct((width, 3 * units), bf16),
+            jax.ShapeDtypeStruct((rows // n, width), f32), per_piece, per_piece,
+        ],
         in_specs=[anywhere] + [vmem] * 4 + [anywhere] * 3,
-        out_specs=[anywhere] * 6 + [vmem] * 3,
+        out_specs=[anywhere] * 4 + [vmem] * 3,
         scratch_shapes=line_scratch(n, rows, width) + [
             pltpu.VMEM(w_g.shape, bf16), pltpu.VMEM(w_u.shape, bf16), pltpu.VMEM(w_d.shape, bf16),
-            pltpu.VMEM((CHUNK, width), bf16),
-            pltpu.VMEM((CHUNK, units), bf16), pltpu.VMEM((CHUNK, units), bf16), pltpu.VMEM((CHUNK, units), bf16),
-            pltpu.VMEM((CHUNK, width), bf16),
+            pltpu.VMEM((CHUNK, width), bf16), pltpu.VMEM((CHUNK, units), bf16), pltpu.VMEM((rows, width), bf16),
             pltpu.VMEM((rows, units), bf16), pltpu.VMEM((rows, units), bf16),
+            pltpu.VMEM((2, TILE_ROWS, units), bf16),
             pltpu.SemaphoreType.REGULAR((2,)),
-            pltpu.SemaphoreType.DMA((3,)), pltpu.SemaphoreType.DMA((5,)), pltpu.SemaphoreType.DMA((n,)),
+            pltpu.SemaphoreType.DMA((3,)), pltpu.SemaphoreType.DMA((2,)), pltpu.SemaphoreType.DMA((n,)),
+            pltpu.SemaphoreType.DMA((2,)),
         ],
         compiler_params=params(2),
         cost_estimate=pl.CostEstimate(flops=200 * 10**9, bytes_accessed=60 << 20, transcendentals=0),
@@ -456,14 +509,102 @@
     )(mlp_in, grad, attn_own, gain_m, gain_a, w_g, w_u, w_d)
 
 
-def input_grad_kernel(n, grad_qkv, w_qkv_hbm, mixed_own, grad_out, buf, total, send, recv, w_qkv, w_sem, piece_sems):
+class Owners:
+    def __init__(self, n_xy, full, pair_in, peer_in, result, pair_sems, peer_sems):
+        n_fsdp, self.n_ctx = n_xy
+        self.chips = n_fsdp // 2
+        self.full, self.pair_in, self.peer_in, self.result = full, pair_in, peer_in, result
+        self.pair_sems, self.peer_sems = pair_sems, peer_sems
+        fsdp = lax.axis_index("fsdp")
+        self.core = lax.rem(fsdp, 2)
+        self.ctx = lax.axis_index("ctx")
+        self.place = lax.div(fsdp, 2) * self.n_ctx + self.ctx
+        self.block = full.shape[0] // (n_fsdp * self.n_ctx)
+
+    def pair_copy(self, chip):
+        there = 1 - self.core
+        span = self.n_ctx * self.block
+        rows = pl.ds(pl.multiple_of((2 * chip + there) * span, span), span)
+        return pltpu.make_async_remote_copy(
+            src_ref=self.full.at[rows], dst_ref=self.pair_in.at[pl.ds(chip * span, span)],
+            send_sem=self.pair_sems.at[0, chip], recv_sem=self.pair_sems.at[1, chip],
+            device_id={"fsdp": 2 * lax.div(lax.axis_index("fsdp"), 2) + there}, device_id_type=pl.DeviceIdType.MESH,
+        )
+
+    def peer_copy(self, k):
+        place = lax.rem(self.place + k, self.chips * self.n_ctx)
+        return pltpu.make_async_remote_copy(
+            src_ref=self.pair_in.at[self.block_rows(place)], dst_ref=self.peer_in.at[k - 1],
+            send_sem=self.peer_sems.at[0, k - 1], recv_sem=self.peer_sems.at[1, k - 1],
+            device_id={"fsdp": 2 * lax.div(place, self.n_ctx) + self.core, "ctx": lax.rem(place, self.n_ctx)},
+            device_id_type=pl.DeviceIdType.MESH,
+        )
+
+    def block_rows(self, place):
+        return pl.ds(pl.multiple_of(place * self.block, self.block), self.block)
+
+    def start(self):
+        for chip in range(self.chips):
+            self.pair_copy(chip).start()
+
+    def pass_on(self):
+        span = self.n_ctx * self.block
+        for chip in range(self.chips):
+            self.pair_copy(chip).wait_recv()
+            rows = pl.ds(chip * span, span)
+            mine = pl.ds(pl.multiple_of((2 * chip + self.core) * span, span), span)
+            self.pair_in[rows] = (self.pair_in[rows].astype(f32) + self.full[mine].astype(f32)).astype(bf16)
+        for k in range(1, self.chips * self.n_ctx):
+            self.peer_copy(k).start()
+
+    def end(self):
+        self.result[...] = self.pair_in[self.block_rows(self.place)].astype(f32)
+        for k in range(1, self.chips * self.n_ctx):
+            self.peer_copy(k).wait()
+            self.result[...] += self.peer_in[k - 1].astype(f32)
+        for chip in range(self.chips):
+            self.pair_copy(chip).wait_send()
+
+
+def owners_scratch(n_xy, shape):
+    n_fsdp, n_ctx = n_xy
+    peers = n_fsdp // 2 * n_ctx - 1
+    block = shape[0] // (n_fsdp * n_ctx)
+    return [
+        pltpu.VMEM((shape[0] // 2, shape[1]), bf16), pltpu.VMEM((peers, block, shape[1]), bf16),
+        pltpu.SemaphoreType.DMA((2, n_fsdp // 2)), pltpu.SemaphoreType.DMA((2, peers)),
+    ]
+
+
+def input_grad_kernel(
+    n, n_xy, grad_qkv, w_qkv_hbm, mixed_own, gains, weights, grad_out, gains_sum, weights_own,
+    buf, total, send, recv, w_qkv, w_sem, piece_sems, gains_theirs, gain_send, gain_recv,
+    pair_in, peer_in, pair_sems, peer_sems,
+):
     rows, width = buf.shape[1:]
     groups = rows // (n * PIECE)
     per_chunk = CHUNK // (n * PIECE)
     line = Line("tp", n, groups, buf, total, send, recv)
     fetch = pltpu.make_async_copy(w_qkv_hbm, w_qkv, w_sem)
     fetch.start()
-    greet("tp", n)
+    n_fsdp, n_ctx = n_xy
+    place = lax.axis_index("fsdp") * n_ctx + lax.axis_index("ctx")
+    others = []
+    for k in range(1, n_fsdp * n_ctx):
+        peer = lax.rem(place + k, n_fsdp * n_ctx)
+        others.append({"fsdp": lax.div(peer, n_ctx), "ctx": lax.rem(peer, n_ctx)})
+    greet("tp", n, others)
+    gain_copies = [
+        pltpu.make_async_remote_copy(
+            src_ref=gains, dst_ref=gains_theirs.at[k], send_sem=gain_send.at[k], recv_sem=gain_recv.at[k],
+            device_id=peer, device_id_type=pl.DeviceIdType.MESH,
+        )
+        for k, peer in enumerate(others)
+    ]
+    for copy in gain_copies:
+        copy.start()
+    owners = Owners(n_xy, weights, pair_in, peer_in, weights_own, pair_sems, peer_sems)
+    owners.start()
     fetch.wait()
     tile = 512
 
@@ -490,43 +631,426 @@
 
         line.tick(t, own, done)
 
-
-def input_grad(grad_qkv, w_qkv, mixed_own, n):
+        @pl.when(t == 2)
+        def _():
+            owners.pass_on()
+
+    owners.end()
+    gains_sum[...] = gains[...]
+    for k, copy in enumerate(gain_copies):
+        copy.wait()
+        gains_sum[...] += gains_theirs[k]
+
+
+def input_grad(grad_qkv, w_qkv, mixed_own, gains, weights, n, n_xy):
     rows, width = grad_qkv.shape[0], w_qkv.shape[0]
+    peers = n_xy[0] * n_xy[1] - 1
     vmem, anywhere = pl.BlockSpec(memory_space=pltpu.VMEM), pl.BlockSpec(memory_space=pl.ANY)
     return pl.pallas_call(
-        functools.partial(input_grad_kernel, n),
-        out_shape=jax.ShapeDtypeStruct((rows, width), bf16),
-        in_specs=[vmem, anywhere, vmem],
-        out_specs=anywhere,
+        functools.partial(input_grad_kernel, n, n_xy),
+        out_shape=[
+            jax.ShapeDtypeStruct((rows, width), bf16), jax.ShapeDtypeStruct(gains.shape, f32),
+            jax.ShapeDtypeStruct((weights.shape[0] // (n_xy[0] * n_xy[1]), weights.shape[1]), f32),
+        ],
+        in_specs=[vmem, anywhere, vmem, vmem, vmem],
+        out_specs=[anywhere, vmem, vmem],
         scratch_shapes=line_scratch(n, rows, width) + [
             pltpu.VMEM(w_qkv.shape, bf16), pltpu.SemaphoreType.DMA, pltpu.SemaphoreType.DMA((n,)),
-        ],
+            pltpu.VMEM((peers,) + gains.shape, f32), pltpu.SemaphoreType.DMA((peers,)), pltpu.SemaphoreType.DMA((peers,)),
+        ] + owners_scratch(n_xy, weights.shape),
         compiler_params=params(3),
         cost_estimate=pl.CostEstimate(flops=100 * 10**9, bytes_accessed=20 << 20, transcendentals=0),
         name="input_grad",
-    )(grad_qkv, w_qkv, mixed_own)
-
-
-def small_sum(values, axis):
-    n = lax.axis_size(axis)
-    total = values
-    for k in range(1, n):
-        total = total + lax.ppermute(values, axis, [(a, (a + k) % n) for a in range(n)])
-    return total
+    )(grad_qkv, w_qkv, mixed_own, gains, weights)
+
+
+def peers_of(axis, n):
+    i = lax.axis_index(axis)
+    return [(k - 1, lax.rem(i + k, n)) for k in range(1, n)]
+
+
+def meet(axes):
+    barrier = pltpu.get_barrier_semaphore()
+    count = 0
+    for axis, n in axes:
+        for _, peer in peers_of(axis, n):
+            pl.semaphore_signal(barrier, inc=1, device_id={axis: peer}, device_id_type=pl.DeviceIdType.MESH)
+            count += 1
+    pl.semaphore_wait(barrier, count)
+
+
+def swap(axis, n, pairs, send, recv):
+    copies = []
+    for k, (mine, theirs) in enumerate(pairs):
+        for slot, peer in peers_of(axis, n):
+            copy = pltpu.make_async_remote_copy(
+                src_ref=mine, dst_ref=theirs.at[slot],
+                send_sem=send.at[k, slot], recv_sem=recv.at[k, slot],
+                device_id={axis: peer}, device_id_type=pl.DeviceIdType.MESH,
+            )
+            copy.start()
+            copies.append(copy)
+    for copy in copies:
+        copy.wait()
+
+
+def lanes_to_rows(columns):
+    return jnp.transpose(columns)[:8]
+
+
+def rows_to_lanes(packed):
+    rows = packed.shape[1]
+    return jnp.transpose(jnp.concatenate([packed, jnp.zeros((120, rows), f32)], axis=0))
+
+
+def two_lanes(first, second):
+    lane = lax.broadcasted_iota(jnp.int32, (first.shape[0], 128), 1)
+    return jnp.where(lane == 0, first, jnp.where(lane == 1, second, 0.0))
+
+
+def turn(values, cosine, sine):
+    return values * cosine + pltpu.roll(values, HD // 2, 1) * sine
+
+
+def heads_loop(heads, body):
+    @pl.loop(0, heads)
+    def _(h):
+        body(h, lambda part, width: pl.ds(pl.multiple_of(part * width + h * HD, HD), HD))
+
+
+def attend_kernel(
+    n_tp, n_ctx, seqs, x, w_qkv, gain_q, gain_k, cosine, sine,
+    raw, low, prev, head_low, head_out, stats,
+    sums, theirs, kv_send, kv_recv, sum_send, sum_recv,
+):
+    rows_all, width = x.shape
+    rows = rows_all // seqs
+    local = w_qkv.shape[1] // 3
+    heads = local // HD
+    me = lax.axis_index("ctx")
+    scale = HD ** (-0.5)
+    meet([("tp", n_tp), ("ctx", n_ctx)])
+    step = min(256, rows)
+
+    def chunks(body):
+        @pl.loop(0, rows_all // step)
+        def _(k):
+            body(pl.ds(pl.multiple_of(k * step, step), step), pl.ds(pl.multiple_of(lax.rem(k, rows // step) * step, step), step))
+
+    for j in range(1, n_ctx):
+
+        @pl.when(me < j)
+        def _():
+            prev[j - 1] = jnp.zeros(prev.shape[1:], bf16)
+
+    def kv_copy(j, part, seq):
+        at = pl.ds(seq * rows, rows)
+        return pltpu.make_async_remote_copy(
+            src_ref=low.at[at, pl.ds((1 + part) * local, local)],
+            dst_ref=prev.at[j - 1, at, pl.ds(part * local, local)],
+            send_sem=kv_send.at[j - 1, part, seq], recv_sem=kv_recv.at[j - 1, part, seq],
+            device_id={"ctx": lax.rem(me + j, n_ctx)}, device_id_type=pl.DeviceIdType.MESH,
+        )
+
+    def kv_each(method, part, seq, here):
+        for j in range(1, n_ctx):
+
+            @pl.when((me >= j) if here else (me + j < n_ctx))
+            def _():
+                getattr(kv_copy(j, part, seq), method)()
+
+    def value_chunk(at, _):
+        low[at, 2 * local :] = dot(x[at], w_qkv[:, 2 * local :], ((1,), (0,)), bf16)
+
+    chunks(value_chunk)
+    for seq in range(seqs):
+        kv_each("start", 1, seq, False)
+
+    def raw_chunk(at, _):
+        q = dot(x[at], w_qkv[:, :local], ((1,), (0,)))
+        raw[at, :local] = q
+        k = dot(x[at], w_qkv[:, local : 2 * local], ((1,), (0,)))
+        raw[at, local:] = k
+        both = two_lanes(jnp.sum(q * q, axis=-1, keepdims=True), jnp.sum(k * k, axis=-1, keepdims=True))
+        sums[:, at] = lanes_to_rows(both)
+
+    chunks(raw_chunk)
+    swap("tp", n_tp, [(sums, theirs)], sum_send, sum_recv)
+    total = sums[...]
+    for slot in range(n_tp - 1):
+        total = total + theirs[slot]
+    stats[...] = rows_to_lanes(lax.rsqrt(total / width + norm_eps))
+
+    def turned(part, gain):
+        def chunk(at, pos):
+            r = stats[at, part : part + 1]
+            for h in range(heads):
+                cols = pl.ds(part * local + h * HD, HD)
+                v = raw[at, cols] * r * gain[:, h * HD : (h + 1) * HD]
+                low[at, cols] = turn(v, cosine[pos], sine[pos]).astype(bf16)
+
+        chunks(chunk)
+
+    turned(1, gain_k)
+    for seq in range(seqs):
+        kv_each("start", 0, seq, False)
+    turned(0, gain_q)
+    lane = lax.broadcasted_iota(jnp.int32, (step, 128), 1)
+
+    for seq in range(seqs):
+        for part in range(2):
+            kv_each("wait_recv", part, seq, True)
+        seq_rows = pl.ds(seq * rows, rows)
+
+        def one_head(h, cols, seq=seq, seq_rows=seq_rows):
+            for tile in range(rows // step):
+                at = pl.ds(seq * rows + tile * step, step)
+                q = low[at, cols(0, local)]
+                seen = (tile + 1) * step
+                own = pl.ds(seq * rows, seen)
+                s = dot(q, low[own, cols(1, local)], ((1,), (1,))) * scale
+                i_pos = lax.broadcasted_iota(jnp.int32, (step, seen), 0) + tile * step
+                j_pos = lax.broadcasted_iota(jnp.int32, (step, seen), 1)
+                scores = [jnp.where(j_pos <= i_pos, s, masked_value)]
+                values = [low[own, cols(2, local)]]
+                for j in range(1, n_ctx):
+                    s = dot(q, prev[j - 1, seq_rows, cols(0, local)], ((1,), (1,))) * scale
+                    scores.append(jnp.where(me >= j, s, masked_value))
+                    values.append(prev[j - 1, seq_rows, cols(1, local)])
+                top = scores[0].max(-1, keepdims=True)
+                for s in scores[1:]:
+                    top = jnp.maximum(top, s.max(-1, keepdims=True))
+                total, weighted = 0.0, 0.0
+                for s, v in zip(scores, values):
+                    e = jnp.exp(s - top)
+                    total = total + e.sum(-1, keepdims=True)
+                    weighted = weighted + dot(e.astype(bf16), v, ((1,), (0,)))
+                out = weighted / total
+                head_out[at, cols(0, local)] = out
+                head_low[at, cols(0, local)] = out.astype(bf16)
+                stats[at] = jnp.where(lane == h + 2, top + jnp.log(total), stats[at])
+
+        heads_loop(heads, one_head)
+
+    for seq in range(seqs):
+        for part in range(2):
+            kv_each("wait_send", part, seq, False)
+
+
+def attend(x, w_qkv, gain_q, gain_k, cosine, sine, seqs, n_tp, n_ctx):
+    rows, width = x.shape
+    local = w_qkv.shape[1] // 3
+    vmem = pl.BlockSpec(memory_space=pltpu.VMEM)
+    shape = jax.ShapeDtypeStruct
+    kv_sems = pltpu.SemaphoreType.DMA((max(n_ctx - 1, 1), 2, seqs))
+    sum_sems = pltpu.SemaphoreType.DMA((1, n_tp - 1))
+    return pl.pallas_call(
+        functools.partial(attend_kernel, n_tp, n_ctx, seqs),
+        out_shape=[
+            shape((rows, 2 * local), f32), shape((rows, 3 * local), bf16),
+            shape((max(n_ctx - 1, 1), rows, 2 * local), bf16),
+            shape((rows, local), bf16), shape((rows, local), f32), shape((rows, 128), f32),
+        ],
+        in_specs=[vmem] * 6,
+        out_specs=[vmem] * 6,
+        scratch_shapes=[
+            pltpu.VMEM((8, rows), f32), pltpu.VMEM((n_tp - 1, 8, rows), f32),
+            kv_sems, kv_sems, sum_sems, sum_sems,
+        ],
+        compiler_params=params(4),
+        cost_estimate=pl.CostEstimate(flops=50 * 10**9, bytes_accessed=30 << 20, transcendentals=0),
+        name="attend",
+    )(x, w_qkv, gain_q, gain_k, cosine, sine)
+
+
+def attend_back_kernel(
+    n_tp, n_ctx, seqs, attn_low, w_out_t, raw, low, prev, head_out, stats, x, head_low, gain_q, gain_k, cosine, sine, gain_a,
+    grad_qkv, gain_qk_sum, gain_a_sum, weights_out,
+    grad_heads, grad_q, grad_kv, out_kv, in_kv, sums, theirs, gain_theirs, kv_send, kv_recv, sum_send, sum_recv,
+):
+    rows_all, width = attn_low.shape
+    rows = rows_all // seqs
+    local = w_out_t.shape[1]
+    heads = local // HD
+    me = lax.axis_index("ctx")
+    scale = HD ** (-0.5)
+    meet([("tp", n_tp), ("ctx", n_ctx)])
+    step = min(256, rows)
+
+    def chunks(body):
+        @pl.loop(0, rows_all // step)
+        def _(k):
+            body(pl.ds(pl.multiple_of(k * step, step), step), pl.ds(pl.multiple_of(lax.rem(k, rows // step) * step, step), step))
+
+    def heads_chunk(at, _):
+        grad_heads[at] = dot(attn_low[at], w_out_t[...], ((1,), (0,)), bf16)
+
+    chunks(heads_chunk)
+    grad_q[...] = jnp.zeros_like(grad_q)
+    grad_kv[...] = jnp.zeros_like(grad_kv)
+
+    def kv_copy(j, seq):
+        at = pl.ds(seq * rows, rows)
+        return pltpu.make_async_remote_copy(
+            src_ref=out_kv.at[j - 1, at], dst_ref=in_kv.at[j - 1, at],
+            send_sem=kv_send.at[j - 1, seq], recv_sem=kv_recv.at[j - 1, seq],
+            device_id={"ctx": lax.rem(me + n_ctx - j, n_ctx)}, device_id_type=pl.DeviceIdType.MESH,
+        )
+
+    def lane_of(at, index):
+        lane = lax.broadcasted_iota(jnp.int32, (step, 128), 1)
+        return jnp.sum(jnp.where(lane == index, stats[at], 0.0), axis=-1, keepdims=True)
+
+    def block(h, cols, at, keys, values, mask):
+        q, g = low[at, cols(0, local)], grad_heads[at, cols(0, local)]
+        delta = jnp.sum(g.astype(f32) * head_out[at, cols(0, local)], axis=-1, keepdims=True)
+        s = dot(q, keys, ((1,), (1,))) * scale
+        p = jnp.exp(s - lane_of(at, h + 2))
+        if mask is not None:
+            p = jnp.where(mask, p, 0.0)
+        dp = dot(g, values, ((1,), (1,)))
+        ds = (p * (dp - delta)).astype(bf16)
+        grad_q[at, cols(0, local)] += dot(ds, keys, ((1,), (0,))) * scale
+        return dot(ds, q, ((0,), (0,))) * scale, dot(p.astype(bf16), g, ((0,), (0,)))
+
+    for j in range(1, n_ctx):
+
+        @pl.when(me >= j)
+        def _():
+            for seq in range(seqs):
+                seq_rows = pl.ds(seq * rows, rows)
+
+                def one_head(h, cols):
+                    keys, values = prev[j - 1, seq_rows, cols(0, local)], prev[j - 1, seq_rows, cols(1, local)]
+                    dk, dv = 0.0, 0.0
+                    for tile in range(rows // step):
+                        at = pl.ds(seq * rows + tile * step, step)
+                        k_term, v_term = block(h, cols, at, keys, values, None)
+                        dk, dv = dk + k_term, dv + v_term
+                    out_kv[j - 1, seq_rows, cols(0, local)] = dk.astype(bf16)
+                    out_kv[j - 1, seq_rows, cols(1, local)] = dv.astype(bf16)
+
+                heads_loop(heads, one_head)
+                kv_copy(j, seq).start()
+
+    for seq in range(seqs):
+
+        def one_head(h, cols):
+            for tile in range(rows // step):
+                at = pl.ds(seq * rows + tile * step, step)
+                seen = (tile + 1) * step
+                own = pl.ds(seq * rows, seen)
+                i_pos = lax.broadcasted_iota(jnp.int32, (step, seen), 0) + tile * step
+                j_pos = lax.broadcasted_iota(jnp.int32, (step, seen), 1)
+                k_term, v_term = block(
+                    h, cols, at, low[own, cols(1, local)], low[own, cols(2, local)], j_pos <= i_pos
+                )
+                grad_kv[own, cols(0, local)] += k_term
+                grad_kv[own, cols(1, local)] += v_term
+
+        heads_loop(heads, one_head)
+
+    def weight_rows(left, right, cols):
+        @pl.loop(0, width // step)
+        def _(k):
+            at = pl.ds(pl.multiple_of(k * step, step), step)
+            weights_out[at, cols] = dot(left[:, at], right[...], ((0,), (0,)), bf16)
+
+    weight_rows(attn_low, head_low, pl.ds(3 * local, local))
+
+    for j in range(1, n_ctx):
+        for seq in range(seqs):
+
+            @pl.when(me + j < n_ctx)
+            def _():
+                kv_copy(j, seq).wait_recv()
+                at = pl.ds(seq * rows, rows)
+                grad_kv[at] += in_kv[j - 1, at].astype(f32)
+
+    def turned(at, pos, part, ref, gain):
+        inner = 0.0
+        for h in range(heads):
+            cols = pl.ds(h * HD, HD)
+            d = turn(ref[at, cols], cosine[pos], -sine[pos])
+            ref[at, cols] = d
+            weighted = d * raw[at, pl.ds(part * local + h * HD, HD)] * gain[:, h * HD : (h + 1) * HD]
+            inner = inner + jnp.sum(weighted, axis=-1, keepdims=True)
+        return inner
+
+    def inner_chunk(at, pos):
+        both = two_lanes(
+            turned(at, pos, 0, grad_q, gain_q), turned(at, pos, 1, grad_kv, gain_k)
+        )
+        sums[:, at] = lanes_to_rows(both)
+
+    chunks(inner_chunk)
+    swap("tp", n_tp, [(sums, theirs), (gain_a, gain_theirs)], sum_send, sum_recv)
+    total, gain_total = sums[...], gain_a[...]
+    for slot in range(n_tp - 1):
+        total = total + theirs[slot]
+        gain_total = gain_total + gain_theirs[slot]
+    gain_a_sum[...] = gain_total
+    sums[...] = total / width
+    gain_qk_sum[...] = jnp.zeros_like(gain_qk_sum)
+
+    def out_chunk(at, _):
+        inner = rows_to_lanes(sums[:, at])
+        for part, ref, gain in ((0, grad_q, gain_q), (1, grad_kv, gain_k)):
+            cols = pl.ds(part * local, local)
+            r = stats[at, part : part + 1]
+            d, v = ref[at, :local], raw[at, cols]
+            grad_qkv[at, cols] = (d * r * gain[...] - v * (r * r * r) * inner[:, part : part + 1]).astype(bf16)
+            gain_qk_sum[part : part + 1] += jnp.sum(d * v * r, axis=0, keepdims=True)
+        grad_qkv[at, 2 * local :] = grad_kv[at, local:].astype(bf16)
+
+    chunks(out_chunk)
+    weight_rows(x, grad_qkv, pl.ds(0, 3 * local))
+
+    for j in range(1, n_ctx):
+        for seq in range(seqs):
+
+            @pl.when(me >= j)
+            def _():
+                kv_copy(j, seq).wait_send()
+
+
+def attend_back(
+    attn_low, w_out_t, raw, low, prev, head_out, stats, x, head_low, gain_q, gain_k, cosine, sine, gain_a, seqs, n_tp, n_ctx
+):
+    rows, width = attn_low.shape
+    local = w_out_t.shape[1]
+    vmem = pl.BlockSpec(memory_space=pltpu.VMEM)
+    shape = jax.ShapeDtypeStruct
+    blocks = max(n_ctx - 1, 1)
+    kv_sems = pltpu.SemaphoreType.DMA((blocks, seqs))
+    sum_sems = pltpu.SemaphoreType.DMA((2, n_tp - 1))
+    return pl.pallas_call(
+        functools.partial(attend_back_kernel, n_tp, n_ctx, seqs),
+        out_shape=[
+            shape((rows, 3 * local), bf16), shape((8, local), f32), shape(gain_a.shape, f32),
+            shape((width, 4 * local), bf16),
+        ],
+        in_specs=[vmem] * 14,
+        out_specs=[vmem] * 4,
+        scratch_shapes=[
+            pltpu.VMEM((rows, local), bf16), pltpu.VMEM((rows, local), f32), pltpu.VMEM((rows, 2 * local), f32),
+            pltpu.VMEM((blocks, rows, 2 * local), bf16), pltpu.VMEM((blocks, rows, 2 * local), bf16),
+            pltpu.VMEM((8, rows), f32), pltpu.VMEM((n_tp - 1, 8, rows), f32),
+            pltpu.VMEM((n_tp - 1,) + gain_a.shape, f32),
+            kv_sems, kv_sems, sum_sems, sum_sems,
+        ],
+        compiler_params=params(5),
+        cost_estimate=pl.CostEstimate(flops=60 * 10**9, bytes_accessed=30 << 20, transcendentals=0),
+        name="attend_back",
+    )(attn_low, w_out_t, raw, low, prev, head_out, stats, x, head_low, gain_q, gain_k, cosine, sine, gain_a)
 
 
 def rotation_tables(positions):
     half = HD // 2
     frequency = rope_theta ** (-jnp.arange(half, dtype=f32) * 2.0 / HD)
     angles = positions.astype(f32)[:, None] * frequency[None, :]
-    return jnp.cos(angles)[:, None, :], jnp.sin(angles)[:, None, :]
-
-
-def rotate(values, cosine, sine):
-    half = HD // 2
-    first, second = values[..., :half], values[..., half:]
-    return jnp.concatenate([first * cosine - second * sine, second * cosine + first * sine], axis=-1)
+    cosine, sine = jnp.cos(angles), jnp.sin(angles)
+    return jnp.concatenate([cosine, cosine], axis=1), jnp.concatenate([-sine, sine], axis=1)
 
 
 def per_device(
@@ -535,14 +1059,12 @@
 ):
     micro_count, rows, width = tokens.shape
     local = w_query.shape[1]
-    heads = local // HD
     ctx = lax.axis_size("ctx")
     ctx_rank = lax.axis_index("ctx")
     tp = lax.axis_size("tp")
     tp_rank = lax.axis_index("tp")
     positions = ctx_rank * rows + jnp.arange(rows, dtype=jnp.int32)
     cosine, sine = rotation_tables(positions)
-    scale = HD ** (-0.5)
     gain_q = gain_query.astype(f32)
     gain_k = gain_key.astype(f32)
     gain_a = gain_attn.astype(f32)
@@ -561,97 +1083,6 @@
     def rms(a):
         return lax.rsqrt(jnp.mean(a * a, axis=-1, keepdims=True) + norm_eps)
 
-    blocks = range(ctx)
-    key_pos = jnp.arange(rows, dtype=jnp.int32)
-    causal = key_pos[None, :] <= key_pos[:, None]
-
-    def allowed(j):
-        return causal if j == 0 else jnp.broadcast_to(ctx_rank >= j, causal.shape)
-
-    def split_heads(a):
-        return a.reshape(rows, heads, HD)
-
-    def attend(x):
-        qkv = dot(x, w_qkv, ((1,), (0,)))
-        queries, key_raw = qkv[:, :local], qkv[:, local : 2 * local]
-        value_low = qkv[:, 2 * local :].astype(bf16)
-        squares = jnp.stack([jnp.sum(queries * queries, axis=-1), jnp.sum(key_raw * key_raw, axis=-1)])
-        squares = small_sum(squares, "tp")
-        rq = lax.rsqrt(squares[0] / width + norm_eps)[:, None]
-        rk = lax.rsqrt(squares[1] / width + norm_eps)[:, None]
-        q_low = rotate(split_heads(queries * rq * gain_q), cosine, sine).astype(bf16)
-        k_low = rotate(split_heads(key_raw * rk * gain_k), cosine, sine).astype(bf16)
-        keys, values = [k_low], [split_heads(value_low)]
-        for j in blocks[1:]:
-            pairs = [(a, a + j) for a in range(ctx - j)]
-            keys.append(lax.ppermute(k_low.reshape(rows, local), "ctx", pairs).reshape(k_low.shape))
-            values.append(lax.ppermute(value_low, "ctx", pairs).reshape(k_low.shape))
-        scores = [
-            jnp.where(
-                allowed(j)[None],
-                jnp.einsum("qhd,khd->hqk", q_low, keys[j], preferred_element_type=f32) * scale,
-                masked_value,
-            )
-            for j in blocks
-        ]
-        top = scores[0].max(-1, keepdims=True)
-        for j in blocks[1:]:
-            top = jnp.maximum(top, scores[j].max(-1, keepdims=True))
-        exps = [jnp.exp(a - top) for a in scores]
-        total = sum(a.sum(-1, keepdims=True) for a in exps)
-        exps = [a.astype(bf16) for a in exps]
-        weighted = sum(
-            jnp.einsum("hqk,khd->qhd", exps[j], values[j], preferred_element_type=f32) for j in blocks
-        )
-        inverse = 1.0 / total
-        head_out = weighted * jnp.transpose(inverse, (1, 0, 2))
-        head_low = head_out.reshape(rows, local).astype(bf16)
-        return head_low, (queries, key_raw, rq, rk, q_low, keys, values, exps, inverse, head_out)
-
-    def attend_back(kept, grad_heads):
-        queries, key_raw, rq, rk, q_low, keys, values, exps, inverse, head_out = kept
-        delta = jnp.sum(split_heads(grad_heads.astype(f32)) * head_out, axis=-1)
-        delta = jnp.transpose(delta)[:, :, None]
-        heads_grad = split_heads(grad_heads)
-        scaled_grad = (heads_grad.astype(f32) * jnp.transpose(inverse, (1, 0, 2))).astype(bf16)
-        grad_q_rot = 0.0
-        key_terms, value_terms = [], []
-        for j in blocks:
-            grad_probs = jnp.einsum("qhd,khd->hqk", heads_grad, values[j], preferred_element_type=f32)
-            grad_scores = (exps[j].astype(f32) * inverse * (grad_probs - delta)).astype(bf16)
-            grad_q_rot = grad_q_rot + jnp.einsum(
-                "hqk,khd->qhd", grad_scores, keys[j], preferred_element_type=f32
-            )
-            key_terms.append(
-                jnp.einsum("hqk,qhd->khd", grad_scores, q_low, preferred_element_type=f32) * scale
-            )
-            value_terms.append(
-                jnp.einsum("hqk,qhd->khd", exps[j], scaled_grad, preferred_element_type=f32)
-            )
-        grad_q_rot = grad_q_rot * scale
-        grad_k_rot, grad_values = key_terms[0], value_terms[0]
-        for j in blocks[1:]:
-            pairs = [(a, a - j) for a in range(j, ctx)]
-            back_k = lax.ppermute(key_terms[j].reshape(rows, local).astype(bf16), "ctx", pairs)
-            back_v = lax.ppermute(value_terms[j].reshape(rows, local).astype(bf16), "ctx", pairs)
-            grad_k_rot = grad_k_rot + split_heads(back_k).astype(f32)
-            grad_values = grad_values + split_heads(back_v).astype(f32)
-        value_grad = grad_values.reshape(rows, local).astype(bf16)
-        grad_qn = rotate(grad_q_rot, cosine, -sine).reshape(rows, local)
-        grad_kn = rotate(grad_k_rot, cosine, -sine).reshape(rows, local)
-        inner = jnp.stack(
-            [
-                jnp.sum(grad_qn * queries * gain_q, axis=-1),
-                jnp.sum(grad_kn * key_raw * gain_k, axis=-1),
-            ]
-        )
-        inner = small_sum(inner, "tp") / width
-        grad_queries = (grad_qn * rq * gain_q - queries * rq**3 * inner[0][:, None]).astype(bf16)
-        grad_keys = (grad_kn * rk * gain_k - key_raw * rk**3 * inner[1][:, None]).astype(bf16)
-        gain_q_term = jnp.sum(grad_qn * queries * rq, axis=0)
-        gain_k_term = jnp.sum(grad_kn * key_raw * rk, axis=0)
-        return jnp.concatenate([grad_queries, grad_keys, value_grad], axis=1), gain_q_term, gain_k_term
-
     flat = (micro_count * rows, width)
     x_all, grad_all = tokens.reshape(flat), cotangent.reshape(flat)
 
@@ -659,40 +1090,39 @@
         a = a.reshape(flat[0] // (tp * PIECE), tp, PIECE, width)
         return lax.dynamic_index_in_dim(a, tp_rank, 1, keepdims=False).reshape(flat[0] // tp, width)
 
-    attended = [attend(tokens[m]) for m in range(micro_count)]
-    head_low = jnp.concatenate([a[0] for a in attended], axis=0)
+    tables = (gain_q[None], gain_k[None], cosine, sine)
+    raw, low, prev, head_low, head_out, stats = attend(x_all, w_qkv, *tables, micro_count, tp, ctx)
     attention, mlp_in = attn_out(head_low, w_out_t, x_all, gain_a[None], tp)
-    down, down_low, hidden, gate_low, up_low, attn_low, mixed_own, gain_m_sum, gain_a_sum = mlp(
+    down, _, attn_low, mlp_weights, mixed_own, gain_m_sum, gain_a_sum = mlp(
         mlp_in, grad_all, own(attention), gain_m[None], gain_a[None], w_g, w_u, w_down_t, tp
     )
     att, down = attention.astype(f32), down.astype(f32)
     out = (x_all.astype(f32) + att * rms(att) * gain_a + down * rms(down) * gain_m).astype(bf16)
 
-    def weight_grad(left, right):
-        full = dot(left, right, ((0,), (0,)), bf16)
+    def scatter(full):
         return lax.psum_scatter(full, xy, scatter_dimension=0, tiled=True).astype(f32)
 
-    d_down = weight_grad(down_low, hidden).T
-    d_gate = weight_grad(mlp_in, gate_low)
-    d_up = weight_grad(mlp_in, up_low)
-    d_out = weight_grad(attn_low, head_low).T
-    grad_heads = dot(attn_low, w_out_t, ((1,), (0,)), bf16)
-    back = [
-        attend_back(attended[m][1], grad_heads[m * rows : (m + 1) * rows]) for m in range(micro_count)
-    ]
-    grad_qkv = jnp.concatenate([b[0] for b in back], axis=0)
-    d_qkv = weight_grad(x_all, grad_qkv)
-    grad_tokens = input_grad(grad_qkv, w_qkv, mixed_own, tp)
-    gain_a_total = lax.psum(jnp.sum(gain_a_sum, axis=0), xy + ("tp",))
-    gain_q_total, gain_k_total, gain_m_total = lax.psum(
-        (sum(b[1] for b in back), sum(b[2] for b in back), jnp.sum(gain_m_sum, axis=0)), xy
+    units = w_gate.shape[1]
+    d_mlp = scatter(mlp_weights)
+    d_down, d_gate, d_up = d_mlp[:, :units].T, d_mlp[:, units : 2 * units], d_mlp[:, 2 * units :]
+    gain_a_own = jnp.sum(gain_a_sum, axis=0).reshape(8, width // 8)
+    grad_qkv, gain_qk_sum, gain_a_tp, attn_weights = attend_back(
+        attn_low, w_out_t, raw, low, prev, head_out, stats, x_all, head_low, *tables, gain_a_own, micro_count, tp, ctx
     )
+    gains = jnp.concatenate(
+        [gain_qk_sum[0], gain_qk_sum[1], gain_a_tp.reshape(width), jnp.sum(gain_m_sum, axis=0)]
+    ).reshape(8, (local + width) // 4)
+    grad_tokens, gains, d_attn = input_grad(
+        grad_qkv, w_qkv, mixed_own, gains, attn_weights, tp, (lax.axis_size("fsdp"), lax.axis_size("ctx"))
+    )
+    gains = gains.reshape(2 * (local + width))
     return (
         out.reshape(tokens.shape),
         grad_tokens.reshape(tokens.shape),
-        d_qkv[:, :local], d_qkv[:, local : 2 * local], d_qkv[:, 2 * local :],
-        d_out, d_gate, d_up, d_down,
-        gain_q_total, gain_k_total, gain_a_total, gain_m_total,
+        d_attn[:, :local], d_attn[:, local : 2 * local], d_attn[:, 2 * local : 3 * local],
+        d_attn[:, 3 * local :].T, d_gate, d_up, d_down,
+        gains[:local], gains[local : 2 * local],
+        gains[2 * local : 2 * local + width], gains[2 * local + width :],
     )
 
 

time: 962 us -> 797 us (0.83)
  Pallas kernels: 475 us -> 673 us
  matrix products: 142 us -> 0 us
  blocking collectives: 67.7 us -> 0 us
  other arithmetic: 79.8 us -> 22.6 us
  local copies, waits for them, and re-layouts: 61.1 us -> 24.3 us
  starting transfers between devices: 34.6 us -> 0.24 us
  waiting for transfers between devices: 76 us -> 62.4 us
    pallas_call x2 -> x4, Pallas kernels: 360 us -> 558 us  [the longest x1 269 us: mlp(): pl.pallas_call(functools.partial(mlp_kernel, n), out_shape=[acts, inner,...]
    dot_general x32 -> x0, matrix products: 142 us -> none  [the longest x8 86 us: dot(): lax.dot_general(a, b, (dims, ((), ())), preferred_element_type=f32)]
    psum x2 -> x0, blocking collectives: 67.7 us -> none  [the longest x1 41.5 us: per_device(): gain_a_total = lax.psum(jnp.sum(gain_a_sum, axis=0), xy + ('tp',))]
    ppermute x20 -> x0, starting transfers between devices: 34.2 us -> none  [the longest x12 18 us: small_sum(): lax.ppermute(values, axis, [(a, (a + k) % n) for a in range(n)])]
    concatenate x4 -> x2, other arithmetic: 23.9 us -> 1.01 us  [the longest x1 1 us: rotation_tables(): jnp.concatenate([cosine, cosine], axis=1)]
    convert_element_type x10 -> x0, local copies, waits for them, and re-layouts: 17.3 us -> none  [the longest x2 4.51 us: attend_back(): grad_k_rot = grad_k_rot + split_heads(back_k).astype(f32)]
    all_gather x5, waiting for transfers between devices: 44.2 us -> 61.3 us  [gather(): return lax.all_gather(w, xy, axis=0, tiled=True)]
    reduce_scatter x5 -> x1, waiting for transfers between devices: 16.6 us -> 0.01 us  [scatter(): lax.psum_scatter(full, xy, scatter_dimension=0, tiled=True).astype(f32)]
  transfers between devices with their start and end apart: 30 -> 6, of which waited for: 7 -> 2; matrix products, arithmetic and copies ran while one was open for 25% -> 4% of each run, Pallas kernels for 24% -> 51%
where the time goes in v2:
time: 797 us
  Pallas kernels  673 us (84%)
  waiting for transfers between devices  62.4 us (8%)
  local copies, waits for them, and re-layouts  24.3 us (3%)
  other arithmetic  22.6 us (3%)
  between operations  14.3 us (2%)
    pallas_call x1, Pallas kernels, mlp(): pl.pallas_call(functools.partial(mlp_kernel, n), out_shape=[acts, inner,...  269 us
    pallas_call x1, Pallas kernels, input_grad(): pl.pallas_call(functools.partial(input_grad_kernel, n, n_xy), out_shape=[...  120 us
    pallas_call x1, Pallas kernels, attn_out(): pl.pallas_call(functools.partial(attn_out_kernel, n), out_shape=[jax.Shap...  115 us
    pallas_call x1, Pallas kernels, attend_back(): pl.pallas_call(functools.partial(attend_back_kernel, n_tp, n_ctx, seqs),...  88.9 us
    pallas_call x1, Pallas kernels, attend(): pl.pallas_call(functools.partial(attend_kernel, n_tp, n_ctx, seqs), out_s...  80 us
    all_gather x5, waiting for transfers between devices, gather(): return lax.all_gather(w, xy, axis=0, tiled=True)  61.3 us
  transfers between devices with their start and end apart: 6, of which 2 were waited for; matrix products, arithmetic and copies ran while one was open for 4% of the time, Pallas kernels for 51%

profile of v2, /device:TPU:0, one launch (start us, length us, event | category | flops | bytes accessed | tf_op | source)
XLA Modules:
  0.0 796.5 jit_solution(16430120976167029494)
XLA Ops:
  7.3 2.0 pad_maximum_fusion
  9.4 1.8 copy.26
  11.3 2.3 copy.28
  17.2 1.0 fusion.7
  18.2 1.0 pad_maximum_fusion.1
  19.2 39.6 %all-gather.6.cloned.1.call-done.w_qkv.w_qkv_hbm = bf16[2048,1536]{1,0:T(8,128)(2,1)} async-done(((bf16[256,1536]{1,0:T(8,128)(2,1)}), bf16[2048,1536]{1,0:T(8,128)(2,1)}) %all-gather.6.cloned.1.call-update) | async-done | bytes 6291472 | tf_op jit(solution)/shard_map/all_gather | solution.py:1075
  58.8 80.0 %attend.1 = (f32[1024,1024]{1,0:T(8,128)}, bf16[1024,1536]{1,0:T(8,128)(2,1)}, bf16[1,1024,1024]{2,1,0:T(8,128)(2,1)}, bf16[1024,512]{1,0:T(8,128)(2,1)}, f32[1024,512]{1,0:T(8,128)}, /*index=5*/f32[1024,128]{1,0:T(8,128)}) custom-call(bf16[1024,2048]{1,0:T(8,128)(2,1)} %bitcast.24, bf16[2048,1536]{1,0:T(8,128)(2,1)} %all-gather.6.cloned.1.call-done.w_qkv.w_qkv_hbm, ...), custom_call_target="tpu_custom_call" | custom-call | flops 49999998976 | bytes 31457280 | tf_op jit(solution)/shard_map/attend/pallas_call | solution.py:847
  138.8 115.0 %attn_out.1 = (bf16[1024,2048]{1,0:T(8,128)(2,1)}, bf16[1024,2048]{1,0:T(8,128)(2,1)}) custom-call(bf16[1024,512]{1,0:T(8,128)(2,1)} %get-tuple-element.34.head.head_low, bf16[2048,512]{1,0:T(8,128)(2,1)} %all-gather.8.cloned.1.call-done.w_out_t, bf16[1024,2048]{1,0:T(8,128)(2,1)} %bitcast.25, f32[1,2048]{1,0:T(1,128)} %bitcast.32), custom_call_target="tpu_custom_call" | custom-call | flops 99999997952 | bytes 20971520 | tf_op jit(solution)/shard_map/attn_out/pallas_call | solution.py:250
  253.8 2.3 constant_dynamic-slice_fusion
  256.1 21.6 %all-gather.12.cloned.1.call-done.w_u_hbm = bf16[2048,2048]{1,0:T(8,128)(2,1)} async-done(((bf16[256,2048]{1,0:T(8,128)(2,1)}), bf16[2048,2048]{1,0:T(8,128)(2,1)}) %all-gather.12.cloned.1.call-update) | async-done | bytes 8388624 | tf_op jit(solution)/shard_map/all_gather | solution.py:1075
  277.7 268.7 %mlp.1 = (bf16[1024,2048]{1,0:T(8,128)(2,1)}, bf16[1024,2048]{1,0:T(8,128)(2,1)}, bf16[1024,2048]{1,0:T(8,128)(2,1)}, bf16[2048,6144]{1,0:T(8,128)(2,1)}, f32[25...) custom-call(bf16[1024,2048]{1,0:T(8,128)(2,1)} %get-tuple-element.36.mlp_in, bf16[1024,2048]{1,0:T(8,128)(2,1)} %bitcast.43, ...), custom_call_target="tpu_custom_call" | custom-call | flops 199999995904 | bytes 62914560 | tf_op jit(solution)/shard_map/mlp/pallas_call | solution.py:489
  546.5 3.1 fusion
  550.8 88.9 %attend_back.1 = (bf16[1024,1536]{1,0:T(8,128)(2,1)}, f32[8,512]{1,0:T(8,128)}, f32[8,256]{1,0:T(8,128)}, bf16[2048,2048]{1,0:T(8,128)(2,1)}) custom-call(bf16[1024,2048]{1,0:T(8,128)(2,1)} %get-tuple-element.38.attn_low, bf16[2048,512]{1,0:T(8,128)(2,1)} %all-gather.8.cloned.1.call-done.w_out_t, f32[1024,1024]{1,0:T(8,128)} %get-tuple-element.39.raw, ...), custom_call_target="tpu_custom_call" | custom-call | flops 60000002048 | bytes 31457280 | tf_op jit(solution)/shard_map/attend_back/pallas_call | solution.py:1027
  641.8 120.1 %input_grad.1 = (bf16[1024,2048]{1,0:T(8,128)(2,1)}, f32[8,640]{1,0:T(8,128)}, f32[256,2048]{1,0:T(8,128)}) custom-call(bf16[1024,1536]{1,0:T(8,128)(2,1)} %get-tuple-element.45.grad_qkv, bf16[2048,1536]{1,0:T(8,128)(2,1)} %all-gather.6.cloned.1.call-done.w_qkv.w_qkv_hbm, f32[256,2048]{1,0:T(8,128)} %get-tuple-element.46.mixed_own, f32[8,640]{1,0:T(8,128)} %reshape.93.gains, ...), custom_call_target="tpu_custom_call" | custom-call | flops 99999997952 | bytes 20971520 | tf_op jit(solution)/shard_map/input_grad/pallas_call | solution.py:649
  762.0 2.7 slice_bitcast_fusion.1
  764.7 1.0 copy.29
  766.3 3.4 fusion.5
  770.3 6.5 fusion.4
  776.8 2.6 convert_element_type.37
  779.4 1.5 slice_bitcast_fusion
  781.0 3.0 copy.30
  784.0 2.7 fusion.8
  786.6 1.0 copy-done.2
  787.7 2.0 copy.34
  (59 shorter events, 8.4 us)
Async XLA Ops:
  7.2 7.6 copy-start.11
  7.2 8.2 %copy-start.12 = (bf16[512]{0:T(512)(128)(2,1)S(1)}, bf16[512]{0:T(512)(128)(2,1)}, u32[]{:S(2)}) copy-start(bf16[512]{0:T(512)(128)(2,1)} %param.22) | copy-start | bytes 3076
  7.2 8.8 %copy-start.9 = (bf16[2048]{0:T(1024)(128)(2,1)S(1)}, bf16[2048]{0:T(1024)(128)(2,1)}, u32[]{:S(2)}) copy-start(bf16[2048]{0:T(1024)(128)(2,1)} %param.23) | copy-start | bytes 12292
  7.2 9.4 %copy-start.10 = (bf16[2048]{0:T(1024)(128)(2,1)S(1)}, bf16[2048]{0:T(1024)(128)(2,1)}, u32[]{:S(2)}) copy-start(bf16[2048]{0:T(1024)(128)(2,1)} %param.24) | copy-start | bytes 12292
  7.2 51.5 %all-gather.6.cloned.1.call-start = ((), (), s32[]{:S(2)}) async-start(), calls=%async_computation.1 | async-start | bytes 7077888 | tf_op jit(solution)/shard_map/all_gather | solution.py:1075
  9.3 129.4 %all-gather.8.cloned.1.call-start = ((), (), s32[]{:S(2)}) async-start(), calls=%async_computation.2 | async-start | bytes 2359296 | tf_op jit(solution)/shard_map/all_gather | solution.py:1075
  11.2 244.9 %all-gather.14.cloned.1.call-start = ((), (), s32[]{:S(2)}) async-start(), calls=%async_computation.5 | async-start | bytes 9437184 | tf_op jit(solution)/shard_map/all_gather | solution.py:1075
  13.5 242.5 %all-gather.10.cloned.1.call-start = ((), (), s32[]{:S(2)}) async-start(), calls=%async_computation.3 | async-start | bytes 9437184 | tf_op jit(solution)/shard_map/all_gather | solution.py:1075
  14.1 263.6 %all-gather.12.cloned.1.call-start = ((), (), s32[]{:S(2)}) async-start(), calls=%async_computation.4 | async-start | bytes 9437184 | tf_op jit(solution)/shard_map/all_gather | solution.py:1075
  14.7 762.0 %reduce-scatter.2.cloned.1.call-start = ((), (), s32[]{:S(2)}) async-start(), calls=%async_computation.6 | async-start | bytes 28311552 | tf_op jit(solution)/shard_map/reduce_scatter | solution.py:1103
  546.5 3.7 copy-start.4
  550.8 89.6 %copy-start.3 = (f32[16,2048]{1,0:T(8,128)S(1)}, f32[16,2048]{1,0:T(8,128)}, u32[]{:S(2)}) copy-start(f32[16,2048]{1,0:T(8,128)} %get-tuple-element.49) | copy-start | bytes 393220
  761.9 3.8 copy-start.7
  762.0 8.3 %copy-start.5 = (f32[2048]{0:T(1024)S(1)}, f32[2048]{0:T(1024)}, u32[]{:S(2)}) copy-start(f32[2048]{0:T(1024)} %convert_element_type.32) | copy-start | bytes 24580
  762.0 8.3 %copy-start.6 = (f32[2048]{0:T(1024)S(1)}, f32[2048]{0:T(1024)}, u32[]{:S(2)}) copy-start(f32[2048]{0:T(1024)} %convert_element_type.34) | copy-start | bytes 24580
  762.0 8.3 %copy-start.8 = (f32[1024]{0:T(1024)S(1)}, f32[1024]{0:T(1024)}, u32[]{:S(2)}) copy-start(f32[1024]{0:T(1024)} %add_rsqrt_fusion.1) | copy-start | bytes 12292
  765.7 4.6 copy-start
  779.4 4.6 copy-start.1
  784.0 3.7 copy-start.2
Sparse Core Ops, SparseCore 0:
  10.5 48.2 all-gather.5
  61.2 32.8 all-gather.7
  96.6 68.7 all-gather.13
  167.1 54.3 all-gather.9
  223.3 54.3 all-gather.11
  546.6 201.5 reduce-scatter.1

commit v3 on v2

--- a/solution.py
+++ b/solution.py
@@ -2,6 +2,7 @@
 
 import jax
 import jax.numpy as jnp
+import numpy as np
 from jax import lax
 from jax.experimental import pallas as pl
 from jax.experimental.pallas import tpu as pltpu
@@ -23,6 +24,8 @@
 LAG = 1
 CHUNK = 256
 TILE_ROWS = 256
+TILE_COLUMNS = 2048
+MLP_TILE = 1024
 TILES_PER_TICK = 3
 
 
@@ -214,51 +217,6 @@
     return lax.rsqrt(jnp.mean(a * a, axis=-1, keepdims=True) + norm_eps)
 
 
-def attn_out_kernel(n, head, w_out_t, x, gain, attention, mlp_in, buf, total, send, recv):
-    rows, width = x.shape
-    groups = rows // (n * PIECE)
-    line = Line("tp", n, groups, buf, total, send, recv)
-    greet("tp", n)
-    per_chunk = CHUNK // (n * PIECE)
-    tile = 512
-
-    def done(group):
-        for c in range(n):
-            at = line.rows(group, c)
-            low = line.piece(group, c)
-            attention[at] = low
-            a = low.astype(f32)
-            mlp_in[at] = (x[at].astype(f32) + a * scale_of(a) * gain[...]).astype(bf16)
-
-    @pl.loop(0, line.ticks())
-    def _(t):
-        @pl.when((t < groups) & (lax.rem(t, per_chunk) == 0))
-        def _():
-            at = pl.ds(pl.multiple_of(t * n * PIECE, CHUNK), CHUNK)
-
-            @pl.loop(0, width // tile)
-            def _(j):
-                cols = pl.ds(pl.multiple_of(j * tile, tile), tile)
-                buf[1, at, cols] = dot(head[at], w_out_t[cols], ((1,), (1,)), bf16)
-
-        line.tick(t, lambda group, total: total, done)
-
-
-def attn_out(head, w_out_t, x, gain, n):
-    rows, width = x.shape
-    vmem = pl.BlockSpec(memory_space=pltpu.VMEM)
-    return pl.pallas_call(
-        functools.partial(attn_out_kernel, n),
-        out_shape=[jax.ShapeDtypeStruct(x.shape, bf16)] * 2,
-        in_specs=[vmem] * 4,
-        out_specs=[vmem] * 2,
-        scratch_shapes=line_scratch(n, rows, width),
-        compiler_params=params(1),
-        cost_estimate=pl.CostEstimate(flops=100 * 10**9, bytes_accessed=20 << 20, transcendentals=0),
-        name="attn_out",
-    )(head, w_out_t, x, gain)
-
-
 def local_copies(pairs, sems):
     copies = [pltpu.make_async_copy(a, b, sems.at[k]) for k, (a, b) in enumerate(pairs)]
     for copy in copies:
@@ -269,8 +227,8 @@
 def mlp_kernel(
     n, mlp_in, grad, attn_own, gain_m, gain_a, w_g_hbm, w_u_hbm, w_d_hbm,
     down_out, hidden_out, attn_low_out, weights_out, mixed_own, gain_m_sum, gain_a_sum,
-    buf, total, send, recv, w_g, w_u, w_d, mlp_rows, hidden, down_low, gate, up, tiles,
-    ready, w_sems, io_sems, piece_sems, tile_sems,
+    buf, total, send, recv, w_g, w_u, w_d, mlp_rows, hidden, down_low, gate, up,
+    ready, w_sems, io_sems, piece_sems, tile_sems, gain_m_acc, gain_a_acc,
 ):
     rows, width = grad.shape
     units = w_g.shape[1]
@@ -278,12 +236,24 @@
     per_chunk = CHUNK // (n * PIECE)
     line = Line("tp", n, groups, buf, total, send, recv)
     i = line.i
-    weights = local_copies([(w_g_hbm, w_g), (w_u_hbm, w_u), (w_d_hbm, w_d)], w_sems)
-    gain_m_sum[...] = jnp.zeros_like(gain_m_sum)
-    gain_a_sum[...] = jnp.zeros_like(gain_a_sum)
+    tile = MLP_TILE
+
+    def weight_copies(j):
+        cols = pl.ds(pl.multiple_of(j * tile, tile), tile)
+        return [
+            pltpu.make_async_copy(w_g_hbm.at[:, cols], w_g.at[:, cols], w_sems.at[0, j]),
+            pltpu.make_async_copy(w_u_hbm.at[:, cols], w_u.at[:, cols], w_sems.at[1, j]),
+        ]
+
+    for j in range(units // tile):
+        for copy in weight_copies(j):
+            copy.start()
+    down_weights = pltpu.make_async_copy(w_d_hbm, w_d, w_sems.at[2, 0])
+    down_weights.start()
+    gain_m_acc[...] = jnp.zeros_like(gain_m_acc)
+    gain_a_acc[...] = jnp.zeros_like(gain_a_acc)
     greet("tp", n)
-    offset = per_chunk + line.stages - 1
-    tile = 512
+    offset = per_chunk + line.stages
 
     def chunk_rows(chunk):
         return pl.ds(pl.multiple_of(chunk * CHUNK, CHUNK), CHUNK)
@@ -291,19 +261,19 @@
     def hidden_copy(chunk):
         return pltpu.make_async_copy(hidden, hidden_out.at[chunk_rows(chunk)], io_sems.at[1])
 
-    def forward(chunk, first):
+    def forward(chunk, first=False):
         at = chunk_rows(chunk)
         fetch = pltpu.make_async_copy(mlp_in.at[at], mlp_rows, io_sems.at[0])
         fetch.start()
-        if first:
-            weights[0].wait()
-            weights[1].wait()
-        else:
+        if not first:
             hidden_copy(chunk - 1).wait()
         fetch.wait()
 
         @pl.loop(0, units // tile)
         def _(j):
+            if first:
+                for copy in weight_copies(j):
+                    copy.wait()
             cols = pl.ds(pl.multiple_of(j * tile, tile), tile)
             gate_proj = dot(mlp_rows[...], w_g[:, cols], ((1,), (0,)))
             up_proj = dot(mlp_rows[...], w_u[:, cols], ((1,), (0,)))
@@ -312,8 +282,9 @@
             hidden[:, cols] = (gate_proj / (1.0 + jnp.exp(-gate_proj)) * up_proj).astype(bf16)
 
         hidden_copy(chunk).start()
-        if first:
-            weights[2].wait()
+
+    def forward_down(chunk):
+        at = chunk_rows(chunk)
 
         @pl.loop(0, width // tile)
         def _(j):
@@ -332,6 +303,9 @@
             up[at, cols] = (grad_hidden * gate_proj * sig).astype(bf16)
             gate[at, cols] = (grad_hidden * up_proj * sig * (1.0 + gate_proj * (1.0 - sig))).astype(bf16)
 
+    def backward_in(chunk):
+        at = chunk_rows(chunk)
+
         @pl.loop(0, width // tile)
         def _(j):
             cols = pl.ds(pl.multiple_of(j * tile, tile), tile)
@@ -346,7 +320,7 @@
     def tile_copy(k, slot):
         part, block = lax.div(k, per_part), lax.rem(k, per_part)
         return pltpu.make_async_copy(
-            tiles.at[slot],
+            w_d.at[pl.ds(pl.multiple_of(slot * TILE_ROWS, TILE_ROWS), TILE_ROWS)],
             weights_out.at[
                 pl.ds(pl.multiple_of(block * TILE_ROWS, TILE_ROWS), TILE_ROWS),
                 pl.ds(pl.multiple_of(part * units, units), units),
@@ -363,10 +337,12 @@
             tile_copy(k - 2, slot).wait()
 
         def fill(left, right):
-            @pl.loop(0, units // tile)
+            @pl.loop(0, units // TILE_COLUMNS)
             def _(j):
-                cols = pl.ds(pl.multiple_of(j * tile, tile), tile)
-                tiles[slot, :, cols] = dot(left[whole, block], right[whole, cols], ((0,), (0,)), bf16)
+                cols = pl.ds(pl.multiple_of(j * TILE_COLUMNS, TILE_COLUMNS), TILE_COLUMNS)
+                w_d[pl.ds(pl.multiple_of(slot * TILE_ROWS, TILE_ROWS), TILE_ROWS), cols] = dot(
+                    left[whole, block], right[whole, cols], ((0,), (0,)), bf16
+                )
 
         @pl.when(k < per_part)
         def _():
@@ -381,6 +357,19 @@
             fill(w_u, up)
 
         tile_copy(k, slot).start()
+
+    def let_in():
+        @pl.when(i >= 1)
+        def _():
+            pl.semaphore_signal(
+                ready.at[1], inc=1, device_id={"tp": i - 1}, device_id_type=pl.DeviceIdType.MESH
+            )
+
+        @pl.when(i <= n - 2)
+        def _():
+            pl.semaphore_signal(
+                ready.at[0], inc=1, device_id={"tp": i + 1}, device_id_type=pl.DeviceIdType.MESH
+            )
 
     def pieces_out(group, out):
         return local_copies([(line.piece_ref(group, c), out.at[line.rows(group, c)]) for c in range(n)], piece_sems)
@@ -394,7 +383,7 @@
             g = grad[at].astype(f32)
             scaled = g * gain_m[...]
             inner = jnp.mean(scaled * branch, axis=-1, keepdims=True)
-            gain_m_sum[...] += g * branch * r
+            gain_m_acc[...] += g * branch * r
             down_low[at] = (r * scaled - branch * (r * r * r) * inner).astype(bf16)
         for copy in copies:
             copy.wait()
@@ -407,7 +396,7 @@
         r = scale_of(branch)
         scaled = mixed * gain_a[...]
         inner = jnp.mean(scaled * branch, axis=-1, keepdims=True)
-        gain_a_sum[...] += mixed * branch * r
+        gain_a_acc[...] += mixed * branch * r
         return r * scaled - branch * (r * r * r) * inner
 
     def attn_done(group):
@@ -415,6 +404,8 @@
             copy.wait()
 
     forward(0, True)
+    down_weights.wait()
+    forward_down(0)
 
     @pl.loop(0, offset + line.ticks())
     def _(t):
@@ -432,41 +423,37 @@
 
         line.tick(back, attn_grad, attn_done)
         line.tick(t, lambda group, total: total, down_done)
-        after = t + 1
-
-        @pl.when((after < groups) & (lax.rem(after, per_chunk) == 0))
-        def _():
-            forward(lax.div(after, per_chunk), False)
-
-        next_back = after - offset
-
-        @pl.when((next_back >= 0) & (next_back < groups) & (lax.rem(next_back + groups, per_chunk) == 0))
-        def _():
-            @pl.when(i >= 1)
+        for ahead, work in ((2, forward), (1, forward_down)):
+            due = t + ahead
+
+            @pl.when((due >= per_chunk) & (due < groups) & (lax.rem(due, per_chunk) == 0))
             def _():
-                pl.semaphore_signal(
-                    ready.at[1], inc=1, device_id={"tp": i - 1}, device_id_type=pl.DeviceIdType.MESH
-                )
-
-            @pl.when(i <= n - 2)
+                work(lax.div(due, per_chunk))
+
+        for ahead, work in ((2, backward), (1, backward_in)):
+            due = t + ahead - offset
+
+            @pl.when((due >= 0) & (due < groups) & (lax.rem(due + groups, per_chunk) == 0))
             def _():
-                pl.semaphore_signal(
-                    ready.at[0], inc=1, device_id={"tp": i + 1}, device_id_type=pl.DeviceIdType.MESH
-                )
-
-            backward(lax.div(next_back, per_chunk))
+                if ahead == 1:
+                    let_in()
+                work(lax.div(due, per_chunk))
 
         first_tick = offset + groups - per_chunk
 
-        @pl.when(after == first_tick)
+        def late_copies():
+            return [pltpu.make_async_copy(a, b, io_sems.at[k]) for k, (a, b) in enumerate(late_in)]
+
+        @pl.when(t == first_tick - 1)
         def _():
             hidden_copy(rows // CHUNK - 1).wait()
-            local_copies(late_in, w_sems)
+            for copy in late_copies():
+                copy.start()
 
         @pl.when(t == first_tick)
         def _():
-            for k, (source, target) in enumerate(late_in):
-                pltpu.make_async_copy(source, target, w_sems.at[k]).wait()
+            for copy in late_copies():
+                copy.wait()
 
         for m in range(TILES_PER_TICK):
             k = (t - first_tick) * TILES_PER_TICK + m
@@ -477,6 +464,8 @@
 
     for k in (3 * per_part - 2, 3 * per_part - 1):
         tile_copy(k, k % 2).wait()
+    gain_m_sum[...] = jnp.sum(gain_m_acc[...], axis=0, keepdims=True)
+    gain_a_sum[...] = jnp.sum(gain_a_acc[...], axis=0, keepdims=True)
 
 
 def mlp(mlp_in, grad, attn_own, gain_m, gain_a, w_g, w_u, w_d, n):
@@ -485,12 +474,12 @@
     vmem, anywhere = pl.BlockSpec(memory_space=pltpu.VMEM), pl.BlockSpec(memory_space=pl.ANY)
     acts = jax.ShapeDtypeStruct((rows, width), bf16)
     inner = jax.ShapeDtypeStruct((rows, units), bf16)
-    per_piece = jax.ShapeDtypeStruct((PIECE, width), f32)
+    gain_shape = jax.ShapeDtypeStruct((1, width), f32)
     return pl.pallas_call(
         functools.partial(mlp_kernel, n),
         out_shape=[
             acts, inner, acts, jax.ShapeDtypeStruct((width, 3 * units), bf16),
-            jax.ShapeDtypeStruct((rows // n, width), f32), per_piece, per_piece,
+            jax.ShapeDtypeStruct((rows // n, width), f32), gain_shape, gain_shape,
         ],
         in_specs=[anywhere] + [vmem] * 4 + [anywhere] * 3,
         out_specs=[anywhere] * 4 + [vmem] * 3,
@@ -498,10 +487,10 @@
             pltpu.VMEM(w_g.shape, bf16), pltpu.VMEM(w_u.shape, bf16), pltpu.VMEM(w_d.shape, bf16),
             pltpu.VMEM((CHUNK, width), bf16), pltpu.VMEM((CHUNK, units), bf16), pltpu.VMEM((rows, width), bf16),
             pltpu.VMEM((rows, units), bf16), pltpu.VMEM((rows, units), bf16),
-            pltpu.VMEM((2, TILE_ROWS, units), bf16),
             pltpu.SemaphoreType.REGULAR((2,)),
-            pltpu.SemaphoreType.DMA((3,)), pltpu.SemaphoreType.DMA((2,)), pltpu.SemaphoreType.DMA((n,)),
+            pltpu.SemaphoreType.DMA((3, units // 512)), pltpu.SemaphoreType.DMA((2,)), pltpu.SemaphoreType.DMA((n,)),
             pltpu.SemaphoreType.DMA((2,)),
+            pltpu.VMEM((PIECE, width), f32), pltpu.VMEM((PIECE, width), f32),
         ],
         compiler_params=params(2),
         cost_estimate=pl.CostEstimate(flops=200 * 10**9, bytes_accessed=60 << 20, transcendentals=0),
@@ -577,7 +566,7 @@
 
 
 def input_grad_kernel(
-    n, n_xy, grad_qkv, w_qkv_hbm, mixed_own, gains, weights, grad_out, gains_sum, weights_own,
+    n, n_xy, grad_qkv, w_full_hbm, mixed_own, gains, weights, grad_out, gains_sum, weights_own,
     buf, total, send, recv, w_qkv, w_sem, piece_sems, gains_theirs, gain_send, gain_recv,
     pair_in, peer_in, pair_sems, peer_sems,
 ):
@@ -585,7 +574,7 @@
     groups = rows // (n * PIECE)
     per_chunk = CHUNK // (n * PIECE)
     line = Line("tp", n, groups, buf, total, send, recv)
-    fetch = pltpu.make_async_copy(w_qkv_hbm, w_qkv, w_sem)
+    fetch = pltpu.make_async_copy(w_full_hbm.at[:, pl.ds(0, w_qkv.shape[1])], w_qkv, w_sem)
     fetch.start()
     n_fsdp, n_ctx = n_xy
     place = lax.axis_index("fsdp") * n_ctx + lax.axis_index("ctx")
@@ -642,8 +631,8 @@
         gains_sum[...] += gains_theirs[k]
 
 
-def input_grad(grad_qkv, w_qkv, mixed_own, gains, weights, n, n_xy):
-    rows, width = grad_qkv.shape[0], w_qkv.shape[0]
+def input_grad(grad_qkv, w_full, mixed_own, gains, weights, n, n_xy):
+    rows, width = grad_qkv.shape[0], w_full.shape[0]
     peers = n_xy[0] * n_xy[1] - 1
     vmem, anywhere = pl.BlockSpec(memory_space=pltpu.VMEM), pl.BlockSpec(memory_space=pl.ANY)
     return pl.pallas_call(
@@ -655,13 +644,13 @@
         in_specs=[vmem, anywhere, vmem, vmem, vmem],
         out_specs=[anywhere, vmem, vmem],
         scratch_shapes=line_scratch(n, rows, width) + [
-            pltpu.VMEM(w_qkv.shape, bf16), pltpu.SemaphoreType.DMA, pltpu.SemaphoreType.DMA((n,)),
+            pltpu.VMEM((width, grad_qkv.shape[1]), bf16), pltpu.SemaphoreType.DMA, pltpu.SemaphoreType.DMA((n,)),
             pltpu.VMEM((peers,) + gains.shape, f32), pltpu.SemaphoreType.DMA((peers,)), pltpu.SemaphoreType.DMA((peers,)),
         ] + owners_scratch(n_xy, weights.shape),
         compiler_params=params(3),
         cost_estimate=pl.CostEstimate(flops=100 * 10**9, bytes_accessed=20 << 20, transcendentals=0),
         name="input_grad",
-    )(grad_qkv, w_qkv, mixed_own, gains, weights)
+    )(grad_qkv, w_full, mixed_own, gains, weights)
 
 
 def peers_of(axis, n):
@@ -669,9 +658,11 @@
     return [(k - 1, lax.rem(i + k, n)) for k in range(1, n)]
 
 
-def meet(axes):
+def meet(axes, others=()):
     barrier = pltpu.get_barrier_semaphore()
-    count = 0
+    count = len(others)
+    for peer in others:
+        pl.semaphore_signal(barrier, inc=1, device_id=peer, device_id_type=pl.DeviceIdType.MESH)
     for axis, n in axes:
         for _, peer in peers_of(axis, n):
             pl.semaphore_signal(barrier, inc=1, device_id={axis: peer}, device_id_type=pl.DeviceIdType.MESH)
@@ -718,24 +709,124 @@
         body(h, lambda part, width: pl.ds(pl.multiple_of(part * width + h * HD, HD), HD))
 
 
-def attend_kernel(
-    n_tp, n_ctx, seqs, x, w_qkv, gain_q, gain_k, cosine, sine,
-    raw, low, prev, head_low, head_out, stats,
-    sums, theirs, kv_send, kv_recv, sum_send, sum_recv,
+class Gather:
+    def __init__(self, n_xy, parts, full, local_sems, sems):
+        n_fsdp, self.n_ctx = n_xy
+        self.chips = n_fsdp // 2
+        self.parts, self.full, self.local_sems, self.sems = parts, full, local_sems, sems
+        fsdp = lax.axis_index("fsdp")
+        self.chip, self.core = lax.div(fsdp, 2), lax.rem(fsdp, 2)
+        self.ctx = lax.axis_index("ctx")
+        self.block = parts[0].shape[0]
+
+    def place(self, part, chip, core, ctx):
+        columns = self.parts[part].shape[1]
+        first = sum(p.shape[1] for p in self.parts[:part])
+        row = ((2 * chip + core) * self.n_ctx + ctx) * self.block
+        return self.full.at[pl.ds(pl.multiple_of(row, self.block), self.block), pl.ds(first, columns)]
+
+    def send(self, part, slot, source, target, device):
+        return pltpu.make_async_remote_copy(
+            src_ref=source, dst_ref=target,
+            send_sem=self.sems.at[0, part, slot], recv_sem=self.sems.at[1, part, slot],
+            device_id=device, device_id_type=pl.DeviceIdType.MESH,
+        )
+
+    def keep(self, part):
+        return pltpu.make_async_copy(
+            self.parts[part], self.place(part, self.chip, self.core, self.ctx), self.local_sems.at[part]
+        )
+
+    def to_ctx(self, part, k):
+        target = self.place(part, self.chip, self.core, self.ctx)
+        return self.send(part, k - 1, self.parts[part], target, {"ctx": lax.rem(self.ctx + k, self.n_ctx)})
+
+    def to_chip(self, part, c, k):
+        ctx = lax.rem(self.ctx + self.n_ctx - c, self.n_ctx)
+        target = self.place(part, self.chip, self.core, ctx)
+        source = self.parts[part] if c == 0 else target
+        slot = self.n_ctx - 1 + c * (self.chips - 1) + k - 1
+        chip = lax.rem(self.chip + k, self.chips)
+        return self.send(part, slot, source, target, {"fsdp": 2 * chip + self.core})
+
+    def to_core(self, part, c, k):
+        ctx = lax.rem(self.ctx + self.n_ctx - c, self.n_ctx)
+        chip = lax.rem(self.chip + self.chips - k, self.chips)
+        target = self.place(part, chip, self.core, ctx)
+        source = self.parts[part] if c == 0 and k == 0 else target
+        slot = self.n_ctx - 1 + self.n_ctx * (self.chips - 1) + c * self.chips + k
+        return self.send(part, slot, source, target, {"fsdp": 2 * self.chip + 1 - self.core})
+
+    def slots(self):
+        return self.n_ctx - 1 + self.n_ctx * (self.chips - 1) + self.n_ctx * self.chips
+
+    def start(self, part):
+        self.keep(part).start()
+        for k in range(1, self.n_ctx):
+            self.to_ctx(part, k).start()
+        for k in range(1, self.chips):
+            self.to_chip(part, 0, k).start()
+        self.to_core(part, 0, 0).start()
+
+    def pass_on(self, part):
+        for c in range(1, self.n_ctx):
+            self.to_ctx(part, c).wait_recv()
+            for k in range(1, self.chips):
+                self.to_chip(part, c, k).start()
+            self.to_core(part, c, 0).start()
+        for c in range(self.n_ctx):
+            for k in range(1, self.chips):
+                self.to_chip(part, c, k).wait_recv()
+                self.to_core(part, c, k).start()
+
+    def end(self, part):
+        for c in range(self.n_ctx):
+            for k in range(self.chips):
+                self.to_core(part, c, k).wait_recv()
+        self.keep(part).wait()
+
+    def sent(self, part):
+        for k in range(1, self.n_ctx):
+            self.to_ctx(part, k).wait_send()
+        for c in range(self.n_ctx):
+            for k in range(1, self.chips):
+                self.to_chip(part, c, k).wait_send()
+            for k in range(self.chips):
+                self.to_core(part, c, k).wait_send()
+
+
+def front_kernel(
+    n_tp, n_xy, seqs, x_hbm, w_q, w_k, w_v, w_o, gain_q, gain_k, gain_a, cosine, sine,
+    raw_out, low_out, prev_out, head_low_out, stats_out, attention_out, mlp_in_out, w_out, attn_own_out,
+    buf, total, send, recv, x, w, raw, low, prev, head_low, stats, mlp_in, attn_own,
+    sums, theirs, kv_send, kv_recv, sum_send, sum_recv, w_local_sems, w_sems, io_sems, piece_sems, group_sems,
 ):
+    n_ctx = n_xy[1]
     rows_all, width = x.shape
     rows = rows_all // seqs
-    local = w_qkv.shape[1] // 3
+    local = w_q.shape[1]
     heads = local // HD
     me = lax.axis_index("ctx")
     scale = HD ** (-0.5)
-    meet([("tp", n_tp), ("ctx", n_ctx)])
     step = min(256, rows)
+    fetch_x = pltpu.make_async_copy(x_hbm, x, io_sems.at[0])
+    fetch_x.start()
+    gather = Gather(n_xy, [w_v, w_k, w_q, w_o], w, w_local_sems, w_sems)
+    value_at, key_at, query_at, out_at = 0, local, 2 * local, 3 * local
+    fsdp = lax.axis_index("fsdp")
+    meet(
+        [("tp", n_tp), ("ctx", n_ctx)],
+        [{"fsdp": 2 * lax.div(fsdp, 2) + 1 - lax.rem(fsdp, 2)}]
+        + [{"fsdp": lax.rem(fsdp + 2 * k, n_xy[0])} for k in range(1, n_xy[0] // 2)],
+    )
+    for part in range(4):
+        gather.start(part)
 
     def chunks(body):
         @pl.loop(0, rows_all // step)
         def _(k):
-            body(pl.ds(pl.multiple_of(k * step, step), step), pl.ds(pl.multiple_of(lax.rem(k, rows // step) * step, step), step))
+            at = pl.ds(pl.multiple_of(k * step, step), step)
+            body(at, pl.ds(pl.multiple_of(me * rows + lax.rem(k, rows // step) * step, step), step))
 
     for j in range(1, n_ctx):
 
@@ -759,27 +850,44 @@
             def _():
                 getattr(kv_copy(j, part, seq), method)()
 
+    gather.pass_on(0)
+    gather.pass_on(1)
+    gather.end(0)
+    fetch_x.wait()
+
     def value_chunk(at, _):
-        low[at, 2 * local :] = dot(x[at], w_qkv[:, 2 * local :], ((1,), (0,)), bf16)
+        low[at, 2 * local :] = dot(x[at], w[:, value_at : value_at + local], ((1,), (0,)), bf16)
 
     chunks(value_chunk)
     for seq in range(seqs):
         kv_each("start", 1, seq, False)
-
-    def raw_chunk(at, _):
-        q = dot(x[at], w_qkv[:, :local], ((1,), (0,)))
-        raw[at, :local] = q
-        k = dot(x[at], w_qkv[:, local : 2 * local], ((1,), (0,)))
-        raw[at, local:] = k
-        both = two_lanes(jnp.sum(q * q, axis=-1, keepdims=True), jnp.sum(k * k, axis=-1, keepdims=True))
-        sums[:, at] = lanes_to_rows(both)
-
-    chunks(raw_chunk)
+    gather.pass_on(2)
+    gather.end(1)
+
+    def raw_chunk(part, first):
+        def chunk(at, _):
+            v = dot(x[at], w[:, first : first + local], ((1,), (0,)))
+            raw[at, part * local : (part + 1) * local] = v
+            square = jnp.sum(v * v, axis=-1, keepdims=True)
+            lane = lax.broadcasted_iota(jnp.int32, (step, 128), 1)
+            stats[at] = jnp.where(lane == part, square, stats[at] if part == 0 else 0.0)
+
+        chunks(chunk)
+
+    raw_chunk(1, key_at)
+    gather.pass_on(3)
+    gather.end(2)
+    raw_chunk(0, query_at)
+
+    def sums_chunk(at, _):
+        sums[:, at] = lanes_to_rows(stats[at])
+
+    chunks(sums_chunk)
     swap("tp", n_tp, [(sums, theirs)], sum_send, sum_recv)
-    total = sums[...]
+    square_sums = sums[...]
     for slot in range(n_tp - 1):
-        total = total + theirs[slot]
-    stats[...] = rows_to_lanes(lax.rsqrt(total / width + norm_eps))
+        square_sums = square_sums + theirs[slot]
+    stats[...] = rows_to_lanes(lax.rsqrt(square_sums / width + norm_eps))
 
     def turned(part, gain):
         def chunk(at, pos):
@@ -797,12 +905,12 @@
     turned(0, gain_q)
     lane = lax.broadcasted_iota(jnp.int32, (step, 128), 1)
 
-    for seq in range(seqs):
+    def attention(seq):
         for part in range(2):
             kv_each("wait_recv", part, seq, True)
         seq_rows = pl.ds(seq * rows, rows)
 
-        def one_head(h, cols, seq=seq, seq_rows=seq_rows):
+        def one_head(h, cols):
             for tile in range(rows // step):
                 at = pl.ds(seq * rows + tile * step, step)
                 q = low[at, cols(0, local)]
@@ -825,52 +933,129 @@
                     e = jnp.exp(s - top)
                     total = total + e.sum(-1, keepdims=True)
                     weighted = weighted + dot(e.astype(bf16), v, ((1,), (0,)))
-                out = weighted / total
-                head_out[at, cols(0, local)] = out
-                head_low[at, cols(0, local)] = out.astype(bf16)
+                head_low[at, cols(0, local)] = (weighted / total).astype(bf16)
                 stats[at] = jnp.where(lane == h + 2, top + jnp.log(total), stats[at])
 
         heads_loop(heads, one_head)
 
+    attention(0)
+    gather.end(3)
+
+    groups = rows_all // (n_tp * PIECE)
+    line = Line("tp", n_tp, groups, buf, total, send, recv)
+    per_chunk, per_seq = step // (n_tp * PIECE), rows // (n_tp * PIECE)
+    tile = 512
+
+    def group_rows(group):
+        return pl.ds(pl.multiple_of(group * n_tp * PIECE, n_tp * PIECE), n_tp * PIECE)
+
+    def mlp_copy(group):
+        at = group_rows(group)
+        return pltpu.make_async_copy(mlp_in.at[at], mlp_in_out.at[at], group_sems.at[group])
+
+    def own(group, total):
+        attn_own[pl.ds(pl.multiple_of(group * PIECE, PIECE), PIECE)] = total.astype(bf16)
+        return total
+
+    def done(group):
+        copies = local_copies(
+            [(line.piece_ref(group, c), attention_out.at[line.rows(group, c)]) for c in range(n_tp)], piece_sems
+        )
+        for c in range(n_tp):
+            at = line.rows(group, c)
+            a = line.piece(group, c).astype(f32)
+            mlp_in[at] = (x[at].astype(f32) + a * scale_of(a) * gain_a[...]).astype(bf16)
+        mlp_copy(group).start()
+        for copy in copies:
+            copy.wait()
+
+    saves = [
+        (raw, raw_out), (low, low_out), (prev, prev_out), (head_low, head_low_out), (stats, stats_out), (w, w_out),
+    ]
+
+    @pl.loop(0, line.ticks())
+    def _(t):
+        @pl.when((t < groups) & (lax.rem(t, per_chunk) == 0))
+        def _():
+            at = pl.ds(pl.multiple_of(t * n_tp * PIECE, step), step)
+
+            @pl.loop(0, width // tile)
+            def _(j):
+                cols = pl.ds(pl.multiple_of(j * tile, tile), tile)
+                buf[1, at, cols] = dot(head_low[at], w[cols, out_at : out_at + local], ((1,), (1,)), bf16)
+
+        line.tick(t, own, done)
+        for seq in range(1, seqs):
+
+            @pl.when(t == seq * per_seq - 1)
+            def _():
+                attention(seq)
+
+        @pl.when(t == (seqs - 1) * per_seq)
+        def _():
+            for k, (source, target) in enumerate(saves):
+                pltpu.make_async_copy(source, target, io_sems.at[k]).start()
+
+    own_out = pltpu.make_async_copy(attn_own, attn_own_out, piece_sems.at[0])
+    own_out.start()
+    for k, (source, target) in enumerate(saves):
+        pltpu.make_async_copy(source, target, io_sems.at[k]).wait()
+    own_out.wait()
+
+    @pl.loop(0, groups)
+    def _(group):
+        mlp_copy(group).wait()
+
+    for part in range(4):
+        gather.sent(part)
     for seq in range(seqs):
         for part in range(2):
             kv_each("wait_send", part, seq, False)
 
 
-def attend(x, w_qkv, gain_q, gain_k, cosine, sine, seqs, n_tp, n_ctx):
+def front(x, w_q, w_k, w_v, w_o, gain_q, gain_k, gain_a, cosine, sine, seqs, n_tp, n_xy):
     rows, width = x.shape
-    local = w_qkv.shape[1] // 3
-    vmem = pl.BlockSpec(memory_space=pltpu.VMEM)
+    local = w_q.shape[1]
+    n_fsdp, n_ctx = n_xy
+    chips = n_fsdp // 2
+    vmem, anywhere = pl.BlockSpec(memory_space=pltpu.VMEM), pl.BlockSpec(memory_space=pl.ANY)
     shape = jax.ShapeDtypeStruct
-    kv_sems = pltpu.SemaphoreType.DMA((max(n_ctx - 1, 1), 2, seqs))
-    sum_sems = pltpu.SemaphoreType.DMA((1, n_tp - 1))
+    dma = pltpu.SemaphoreType.DMA
+    saved = [
+        shape((rows, 2 * local), f32), shape((rows, 3 * local), bf16),
+        shape((max(n_ctx - 1, 1), rows, 2 * local), bf16),
+        shape((rows, local), bf16), shape((rows, 128), f32),
+    ]
+    acts, full = shape(x.shape, bf16), shape((width, 4 * local), bf16)
+    vmem_of = [pltpu.VMEM(a.shape, a.dtype) for a in saved]
+    slots = n_ctx - 1 + n_ctx * (chips - 1) + n_ctx * chips
+    kv_sems, sum_sems = dma((max(n_ctx - 1, 1), 2, seqs)), dma((1, n_tp - 1))
     return pl.pallas_call(
-        functools.partial(attend_kernel, n_tp, n_ctx, seqs),
-        out_shape=[
-            shape((rows, 2 * local), f32), shape((rows, 3 * local), bf16),
-            shape((max(n_ctx - 1, 1), rows, 2 * local), bf16),
-            shape((rows, local), bf16), shape((rows, local), f32), shape((rows, 128), f32),
+        functools.partial(front_kernel, n_tp, n_xy, seqs),
+        out_shape=saved + [acts, acts, full, shape((rows // n_tp, width), bf16)],
+        in_specs=[anywhere] + [vmem] * 9,
+        out_specs=[anywhere] * 9,
+        scratch_shapes=line_scratch(n_tp, rows, width) + [
+            pltpu.VMEM(x.shape, bf16), pltpu.VMEM(full.shape, bf16), *vmem_of, pltpu.VMEM(x.shape, bf16),
+            pltpu.VMEM((rows // n_tp, width), bf16),
+            pltpu.VMEM((8, rows), f32), pltpu.VMEM((n_tp - 1, 8, rows), f32),
+            kv_sems, kv_sems, sum_sems, sum_sems, dma((4,)), dma((2, 4, slots)), dma((7,)), dma((n_tp,)),
+            dma((rows // (n_tp * PIECE),)),
         ],
-        in_specs=[vmem] * 6,
-        out_specs=[vmem] * 6,
-        scratch_shapes=[
-            pltpu.VMEM((8, rows), f32), pltpu.VMEM((n_tp - 1, 8, rows), f32),
-            kv_sems, kv_sems, sum_sems, sum_sems,
-        ],
-        compiler_params=params(4),
-        cost_estimate=pl.CostEstimate(flops=50 * 10**9, bytes_accessed=30 << 20, transcendentals=0),
-        name="attend",
-    )(x, w_qkv, gain_q, gain_k, cosine, sine)
+        compiler_params=params(1),
+        cost_estimate=pl.CostEstimate(flops=150 * 10**9, bytes_accessed=30 << 20, transcendentals=0),
+        name="front",
+    )(x, w_q, w_k, w_v, w_o, gain_q, gain_k, gain_a, cosine, sine)
 
 
 def attend_back_kernel(
-    n_tp, n_ctx, seqs, attn_low, w_out_t, raw, low, prev, head_out, stats, x, head_low, gain_q, gain_k, cosine, sine, gain_a,
+    n_tp, n_ctx, seqs, attn_low, w_full, raw, low, prev, stats, x, head_low, gain_q, gain_k, cosine, sine, gain_a,
     grad_qkv, gain_qk_sum, gain_a_sum, weights_out,
     grad_heads, grad_q, grad_kv, out_kv, in_kv, sums, theirs, gain_theirs, kv_send, kv_recv, sum_send, sum_recv,
 ):
     rows_all, width = attn_low.shape
     rows = rows_all // seqs
-    local = w_out_t.shape[1]
+    local = head_low.shape[1]
     heads = local // HD
     me = lax.axis_index("ctx")
     scale = HD ** (-0.5)
@@ -880,10 +1065,11 @@
     def chunks(body):
         @pl.loop(0, rows_all // step)
         def _(k):
-            body(pl.ds(pl.multiple_of(k * step, step), step), pl.ds(pl.multiple_of(lax.rem(k, rows // step) * step, step), step))
+            at = pl.ds(pl.multiple_of(k * step, step), step)
+            body(at, pl.ds(pl.multiple_of(me * rows + lax.rem(k, rows // step) * step, step), step))
 
     def heads_chunk(at, _):
-        grad_heads[at] = dot(attn_low[at], w_out_t[...], ((1,), (0,)), bf16)
+        grad_heads[at] = dot(attn_low[at], w_full[:, 3 * local :], ((1,), (0,)), bf16)
 
     chunks(heads_chunk)
     grad_q[...] = jnp.zeros_like(grad_q)
@@ -903,7 +1089,7 @@
 
     def block(h, cols, at, keys, values, mask):
         q, g = low[at, cols(0, local)], grad_heads[at, cols(0, local)]
-        delta = jnp.sum(g.astype(f32) * head_out[at, cols(0, local)], axis=-1, keepdims=True)
+        delta = jnp.sum(g.astype(f32) * head_low[at, cols(0, local)].astype(f32), axis=-1, keepdims=True)
         s = dot(q, keys, ((1,), (1,))) * scale
         p = jnp.exp(s - lane_of(at, h + 2))
         if mask is not None:
@@ -996,12 +1182,13 @@
     def out_chunk(at, _):
         inner = rows_to_lanes(sums[:, at])
         for part, ref, gain in ((0, grad_q, gain_q), (1, grad_kv, gain_k)):
-            cols = pl.ds(part * local, local)
             r = stats[at, part : part + 1]
-            d, v = ref[at, :local], raw[at, cols]
-            grad_qkv[at, cols] = (d * r * gain[...] - v * (r * r * r) * inner[:, part : part + 1]).astype(bf16)
+            d, v = ref[at, :local], raw[at, pl.ds(part * local, local)]
+            grad_qkv[at, pl.ds((2 - part) * local, local)] = (
+                d * r * gain[...] - v * (r * r * r) * inner[:, part : part + 1]
+            ).astype(bf16)
             gain_qk_sum[part : part + 1] += jnp.sum(d * v * r, axis=0, keepdims=True)
-        grad_qkv[at, 2 * local :] = grad_kv[at, local:].astype(bf16)
+        grad_qkv[at, :local] = grad_kv[at, local:].astype(bf16)
 
     chunks(out_chunk)
     weight_rows(x, grad_qkv, pl.ds(0, 3 * local))
@@ -1015,10 +1202,10 @@
 
 
 def attend_back(
-    attn_low, w_out_t, raw, low, prev, head_out, stats, x, head_low, gain_q, gain_k, cosine, sine, gain_a, seqs, n_tp, n_ctx
+    attn_low, w_full, raw, low, prev, stats, x, head_low, gain_q, gain_k, cosine, sine, gain_a, seqs, n_tp, n_ctx
 ):
     rows, width = attn_low.shape
-    local = w_out_t.shape[1]
+    local = head_low.shape[1]
     vmem = pl.BlockSpec(memory_space=pltpu.VMEM)
     shape = jax.ShapeDtypeStruct
     blocks = max(n_ctx - 1, 1)
@@ -1030,7 +1217,7 @@
             shape((rows, 3 * local), bf16), shape((8, local), f32), shape(gain_a.shape, f32),
             shape((width, 4 * local), bf16),
         ],
-        in_specs=[vmem] * 14,
+        in_specs=[vmem] * 13,
         out_specs=[vmem] * 4,
         scratch_shapes=[
             pltpu.VMEM((rows, local), bf16), pltpu.VMEM((rows, local), f32), pltpu.VMEM((rows, 2 * local), f32),
@@ -1042,15 +1229,18 @@
         compiler_params=params(5),
         cost_estimate=pl.CostEstimate(flops=60 * 10**9, bytes_accessed=30 << 20, transcendentals=0),
         name="attend_back",
-    )(attn_low, w_out_t, raw, low, prev, head_out, stats, x, head_low, gain_q, gain_k, cosine, sine, gain_a)
-
-
-def rotation_tables(positions):
+    )(attn_low, w_full, raw, low, prev, stats, x, head_low, gain_q, gain_k, cosine, sine, gain_a)
+
+
+def rotation_tables(length):
     half = HD // 2
-    frequency = rope_theta ** (-jnp.arange(half, dtype=f32) * 2.0 / HD)
-    angles = positions.astype(f32)[:, None] * frequency[None, :]
-    cosine, sine = jnp.cos(angles), jnp.sin(angles)
-    return jnp.concatenate([cosine, cosine], axis=1), jnp.concatenate([-sine, sine], axis=1)
+    frequency = rope_theta ** (-np.arange(half) * 2.0 / HD)
+    angles = np.arange(length)[:, None] * frequency[None, :]
+    cosine, sine = np.cos(angles), np.sin(angles)
+    return (
+        jnp.asarray(np.concatenate([cosine, cosine], axis=1), f32),
+        jnp.asarray(np.concatenate([-sine, sine], axis=1), f32),
+    )
 
 
 def per_device(
@@ -1060,11 +1250,8 @@
     micro_count, rows, width = tokens.shape
     local = w_query.shape[1]
     ctx = lax.axis_size("ctx")
-    ctx_rank = lax.axis_index("ctx")
     tp = lax.axis_size("tp")
-    tp_rank = lax.axis_index("tp")
-    positions = ctx_rank * rows + jnp.arange(rows, dtype=jnp.int32)
-    cosine, sine = rotation_tables(positions)
+    cosine, sine = rotation_tables(rows * ctx)
     gain_q = gain_query.astype(f32)
     gain_k = gain_key.astype(f32)
     gain_a = gain_attn.astype(f32)
@@ -1074,8 +1261,6 @@
     def gather(w):
         return lax.all_gather(w, xy, axis=0, tiled=True)
 
-    w_qkv = gather(jnp.concatenate([w_query, w_key, w_value], axis=1))
-    w_out_t = gather(w_output.T)
     w_g = gather(w_gate)
     w_u = gather(w_up)
     w_down_t = gather(w_down.T)
@@ -1086,15 +1271,14 @@
     flat = (micro_count * rows, width)
     x_all, grad_all = tokens.reshape(flat), cotangent.reshape(flat)
 
-    def own(a):
-        a = a.reshape(flat[0] // (tp * PIECE), tp, PIECE, width)
-        return lax.dynamic_index_in_dim(a, tp_rank, 1, keepdims=False).reshape(flat[0] // tp, width)
-
     tables = (gain_q[None], gain_k[None], cosine, sine)
-    raw, low, prev, head_low, head_out, stats = attend(x_all, w_qkv, *tables, micro_count, tp, ctx)
-    attention, mlp_in = attn_out(head_low, w_out_t, x_all, gain_a[None], tp)
+    n_xy = (lax.axis_size("fsdp"), ctx)
+    raw, low, prev, head_low, stats, attention, mlp_in, w_full, attn_own = front(
+        x_all, w_query, w_key, w_value, w_output.T, gain_q[None], gain_k[None], gain_a[None], cosine, sine,
+        micro_count, tp, n_xy
+    )
     down, _, attn_low, mlp_weights, mixed_own, gain_m_sum, gain_a_sum = mlp(
-        mlp_in, grad_all, own(attention), gain_m[None], gain_a[None], w_g, w_u, w_down_t, tp
+        mlp_in, grad_all, attn_own, gain_m[None], gain_a[None], w_g, w_u, w_down_t, tp
     )
     att, down = attention.astype(f32), down.astype(f32)
     out = (x_all.astype(f32) + att * rms(att) * gain_a + down * rms(down) * gain_m).astype(bf16)
@@ -1105,21 +1289,20 @@
     units = w_gate.shape[1]
     d_mlp = scatter(mlp_weights)
     d_down, d_gate, d_up = d_mlp[:, :units].T, d_mlp[:, units : 2 * units], d_mlp[:, 2 * units :]
-    gain_a_own = jnp.sum(gain_a_sum, axis=0).reshape(8, width // 8)
     grad_qkv, gain_qk_sum, gain_a_tp, attn_weights = attend_back(
-        attn_low, w_out_t, raw, low, prev, head_out, stats, x_all, head_low, *tables, gain_a_own, micro_count, tp, ctx
+        attn_low, w_full, raw, low, prev, stats, x_all, head_low, *tables, gain_a_sum, micro_count, tp, ctx
     )
     gains = jnp.concatenate(
-        [gain_qk_sum[0], gain_qk_sum[1], gain_a_tp.reshape(width), jnp.sum(gain_m_sum, axis=0)]
+        [gain_qk_sum[0], gain_qk_sum[1], gain_a_tp[0], gain_m_sum[0]]
     ).reshape(8, (local + width) // 4)
     grad_tokens, gains, d_attn = input_grad(
-        grad_qkv, w_qkv, mixed_own, gains, attn_weights, tp, (lax.axis_size("fsdp"), lax.axis_size("ctx"))
+        grad_qkv, w_full, mixed_own, gains, attn_weights, tp, n_xy
     )
     gains = gains.reshape(2 * (local + width))
     return (
         out.reshape(tokens.shape),
         grad_tokens.reshape(tokens.shape),
-        d_attn[:, :local], d_attn[:, local : 2 * local], d_attn[:, 2 * local : 3 * local],
+        d_attn[:, 2 * local : 3 * local], d_attn[:, local : 2 * local], d_attn[:, :local],
         d_attn[:, 3 * local :].T, d_gate, d_up, d_down,
         gains[:local], gains[local : 2 * local],
         gains[2 * local : 2 * local + width], gains[2 * local + width :],

time: 797 us -> 743 us (0.932)
  waiting for transfers between devices: 62.4 us -> 1.47 us
    all_gather x5 -> x3, waiting for transfers between devices: 61.3 us -> 0.06 us  [gather(): return lax.all_gather(w, xy, axis=0, tiled=True)]
    pallas_call x1, Pallas kernels: 269 us -> 237 us  [mlp(): pl.pallas_call(functools.partial(mlp_kernel, n), out_shape=[acts, inner,...]
    pallas_call x2 -> x1, Pallas kernels: 195 us -> 217 us  [front(): pl.pallas_call(functools.partial(front_kernel, n_tp, n_xy, seqs), out_sha...]
    pallas_call x1, Pallas kernels: 88.9 us -> 106 us  [attend_back(): pl.pallas_call(functools.partial(attend_back_kernel, n_tp, n_ctx, seqs),...]
  transfers between devices with their start and end apart: 6 -> 4, of which waited for: 2 -> 0; matrix products, arithmetic and copies ran while one was open for 4% -> 3% of each run, Pallas kernels for 51% -> 60%
where the time goes in v3:
time: 743 us; the launch traced here: 735 us
  Pallas kernels  680 us (92%)
  local copies, waits for them, and re-layouts  19.8 us (3%)
  other arithmetic  19.2 us (3%)
  between operations  14.4 us (2%)
    pallas_call x1, Pallas kernels, mlp(): pl.pallas_call(functools.partial(mlp_kernel, n), out_shape=[acts, inner,...  237 us
    pallas_call x1, Pallas kernels, front(): pl.pallas_call(functools.partial(front_kernel, n_tp, n_xy, seqs), out_sha...  217 us
    pallas_call x1, Pallas kernels, input_grad(): pl.pallas_call(functools.partial(input_grad_kernel, n, n_xy), out_shape=[...  120 us
    pallas_call x1, Pallas kernels, attend_back(): pl.pallas_call(functools.partial(attend_back_kernel, n_tp, n_ctx, seqs),...  106 us
  transfers between devices with their start and end apart: 4, of which 0 were waited for; matrix products, arithmetic and copies ran while one was open for 3% of the time, Pallas kernels for 60%

profile of v3, /device:TPU:0, one launch (start us, length us, event | category | flops | bytes accessed | tf_op | source)
XLA Modules:
  0.0 734.9 jit_solution(4461561659249815613)
XLA Ops:
  7.3 2.3 copy.29
  9.7 0.7 all-gather.4.cloned.1.call-update
  10.4 0.7 all-gather.6.cloned.1.call-update
  12.9 0.8 copy.28
  14.4 217.1 %front.1 = (f32[1024,1024]{1,0:T(8,128)}, bf16[1024,1536]{1,0:T(8,128)(2,1)}, bf16[1,1024,1024]{2,1,0:T(8,128)(2,1)}, bf16[1024,512]{1,0:T(8,128)(2,1)}, f32[102...) custom-call(bf16[1024,2048]{1,0:T(8,128)(2,1)} %bitcast.19, ...), custom_call_target="tpu_custom_call" | custom-call | flops 149999992832 | bytes 31457280 | tf_op jit(solution)/shard_map/front/pallas_call | solution.py:1033
  231.6 236.9 %mlp.1 = (bf16[1024,2048]{1,0:T(8,128)(2,1)}, bf16[1024,2048]{1,0:T(8,128)(2,1)}, bf16[1024,2048]{1,0:T(8,128)(2,1)}, bf16[2048,6144]{1,0:T(8,128)(2,1)}, f32[25...) custom-call(bf16[1024,2048]{1,0:T(8,128)(2,1)} %get-tuple-element.36.mlp_in, bf16[1024,2048]{1,0:T(8,128)(2,1)} %bitcast.36, ...), custom_call_target="tpu_custom_call" | custom-call | flops 199999995904 | bytes 62914560 | tf_op jit(solution)/shard_map/mlp/pallas_call | solution.py:478
  468.5 3.1 fusion
  471.6 0.6 add_rsqrt_fusion.1
  472.2 106.2 %attend_back.1 = (bf16[1024,1536]{1,0:T(8,128)(2,1)}, f32[8,512]{1,0:T(8,128)}, f32[1,2048]{1,0:T(1,128)}, bf16[2048,2048]{1,0:T(8,128)(2,1)}) custom-call(bf16[1024,2048]{1,0:T(8,128)(2,1)} %get-tuple-element.39.attn_low, bf16[2048,2048]{1,0:T(8,128)(2,1)} %get-tuple-element.40.w_full.w_full_hbm, f32[1024,1024]{1,0:T(8,128)} %get-tuple-element.41.raw, ...), custom_call_target="tpu_custom_call" | custom-call | flops 60000002048 | bytes 31457280 | tf_op jit(solution)/shard_map/attend_back/pallas_call | solution.py:1214
  578.4 0.8 fusion.10
  579.2 0.7 pad_maximum_fusion
  579.9 0.6 reshape.65.gains
  580.5 119.7 %input_grad.1 = (bf16[1024,2048]{1,0:T(8,128)(2,1)}, f32[8,640]{1,0:T(8,128)}, f32[256,2048]{1,0:T(8,128)}) custom-call(bf16[1024,1536]{1,0:T(8,128)(2,1)} %get-tuple-element.47.grad_qkv, bf16[2048,2048]{1,0:T(8,128)(2,1)} %get-tuple-element.40.w_full.w_full_hbm, f32[256,2048]{1,0:T(8,128)} %get-tuple-element.48.mixed_own, f32[8,640]{1,0:T(8,128)} %reshape.65.gains, ...), custom_call_target="tpu_custom_call" | custom-call | flops 99999997952 | bytes 20971520 | tf_op jit(solution)/shard_map/input_grad/pallas_call | solution.py:638
  700.3 2.7 slice_bitcast_fusion.1
  703.0 1.0 copy.30
  704.6 3.4 fusion.5
  707.9 0.6 fusion.8
  708.6 6.5 fusion.4
  715.0 2.6 convert_element_type.29
  717.7 1.5 slice_bitcast_fusion
  719.2 3.0 copy.31
  722.3 2.7 fusion.7
  724.9 1.0 copy-done.2
  726.0 2.0 copy.33
  (42 shorter events, 3.3 us)
Async XLA Ops:
  7.2 4.0 copy-start.9
  7.2 4.6 copy-start.11
  7.2 5.1 copy-start.12
  7.2 5.7 copy-start.3
  7.2 6.5 copy-start.10
  7.2 224.3 %all-gather.8.cloned.1.call-start = ((), (), s32[]{:S(2)}) async-start(), calls=%async_computation.3 | async-start | bytes 9437184 | tf_op jit(solution)/shard_map/all_gather | solution.py:1262
  9.6 221.9 %all-gather.4.cloned.1.call-start = ((), (), s32[]{:S(2)}) async-start(), calls=%async_computation.1 | async-start | bytes 9437184 | tf_op jit(solution)/shard_map/all_gather | solution.py:1262
  10.4 221.2 %all-gather.6.cloned.1.call-start = ((), (), s32[]{:S(2)}) async-start(), calls=%async_computation.2 | async-start | bytes 9437184 | tf_op jit(solution)/shard_map/all_gather | solution.py:1262
  11.1 703.9 %reduce-scatter.2.cloned.1.call-start = ((), (), s32[]{:S(2)}) async-start(), calls=%async_computation.4 | async-start | bytes 28311552 | tf_op jit(solution)/shard_map/reduce_scatter | solution.py:1287
  472.2 107.0 %copy-start.8 = (f32[1,2048]{1,0:T(1,128)S(1)}, f32[1,2048]{1,0:T(1,128)}, u32[]{:S(2)}) copy-start(f32[1,2048]{1,0:T(1,128)} %get-tuple-element.51) | copy-start | bytes 24580
  700.2 3.8 copy-start.6
  700.2 8.3 %copy-start.4 = (f32[2048]{0:T(1024)S(1)}, f32[2048]{0:T(1024)}, u32[]{:S(2)}) copy-start(f32[2048]{0:T(1024)} %convert_element_type.24) | copy-start | bytes 24580
  700.2 8.3 %copy-start.5 = (f32[2048]{0:T(1024)S(1)}, f32[2048]{0:T(1024)}, u32[]{:S(2)}) copy-start(f32[2048]{0:T(1024)} %convert_element_type.26) | copy-start | bytes 24580
  700.3 8.3 %copy-start.7 = (f32[1024]{0:T(1024)S(1)}, f32[1024]{0:T(1024)}, u32[]{:S(2)}) copy-start(f32[1024]{0:T(1024)} %add_rsqrt_fusion.1) | copy-start | bytes 12292
  704.0 4.6 copy-start.1
  717.7 4.6 copy-start
  722.3 3.7 copy-start.2
Sparse Core Ops, SparseCore 0:
  10.5 85.1 all-gather.7
  97.6 65.6 all-gather.3
  165.2 57.6 all-gather.5
  468.6 219.0 reduce-scatter.1

commit v4 on v3

--- a/solution.py
+++ b/solution.py
@@ -24,7 +24,10 @@
 LAG = 1
 CHUNK = 256
 TILE_ROWS = 256
+EXTRA = 4
 TILE_COLUMNS = 2048
+WEIGHT_ROWS = 256
+WEIGHT_TILES = 2
 MLP_TILE = 1024
 TILES_PER_TICK = 3
 
@@ -253,7 +256,7 @@
     gain_m_acc[...] = jnp.zeros_like(gain_m_acc)
     gain_a_acc[...] = jnp.zeros_like(gain_a_acc)
     greet("tp", n)
-    offset = per_chunk + line.stages
+    offset = per_chunk + line.stages + EXTRA
 
     def chunk_rows(chunk):
         return pl.ds(pl.multiple_of(chunk * CHUNK, CHUNK), CHUNK)
@@ -496,161 +499,6 @@
         cost_estimate=pl.CostEstimate(flops=200 * 10**9, bytes_accessed=60 << 20, transcendentals=0),
         name="mlp",
     )(mlp_in, grad, attn_own, gain_m, gain_a, w_g, w_u, w_d)
-
-
-class Owners:
-    def __init__(self, n_xy, full, pair_in, peer_in, result, pair_sems, peer_sems):
-        n_fsdp, self.n_ctx = n_xy
-        self.chips = n_fsdp // 2
-        self.full, self.pair_in, self.peer_in, self.result = full, pair_in, peer_in, result
-        self.pair_sems, self.peer_sems = pair_sems, peer_sems
-        fsdp = lax.axis_index("fsdp")
-        self.core = lax.rem(fsdp, 2)
-        self.ctx = lax.axis_index("ctx")
-        self.place = lax.div(fsdp, 2) * self.n_ctx + self.ctx
-        self.block = full.shape[0] // (n_fsdp * self.n_ctx)
-
-    def pair_copy(self, chip):
-        there = 1 - self.core
-        span = self.n_ctx * self.block
-        rows = pl.ds(pl.multiple_of((2 * chip + there) * span, span), span)
-        return pltpu.make_async_remote_copy(
-            src_ref=self.full.at[rows], dst_ref=self.pair_in.at[pl.ds(chip * span, span)],
-            send_sem=self.pair_sems.at[0, chip], recv_sem=self.pair_sems.at[1, chip],
-            device_id={"fsdp": 2 * lax.div(lax.axis_index("fsdp"), 2) + there}, device_id_type=pl.DeviceIdType.MESH,
-        )
-
-    def peer_copy(self, k):
-        place = lax.rem(self.place + k, self.chips * self.n_ctx)
-        return pltpu.make_async_remote_copy(
-            src_ref=self.pair_in.at[self.block_rows(place)], dst_ref=self.peer_in.at[k - 1],
-            send_sem=self.peer_sems.at[0, k - 1], recv_sem=self.peer_sems.at[1, k - 1],
-            device_id={"fsdp": 2 * lax.div(place, self.n_ctx) + self.core, "ctx": lax.rem(place, self.n_ctx)},
-            device_id_type=pl.DeviceIdType.MESH,
-        )
-
-    def block_rows(self, place):
-        return pl.ds(pl.multiple_of(place * self.block, self.block), self.block)
-
-    def start(self):
-        for chip in range(self.chips):
-            self.pair_copy(chip).start()
-
-    def pass_on(self):
-        span = self.n_ctx * self.block
-        for chip in range(self.chips):
-            self.pair_copy(chip).wait_recv()
-            rows = pl.ds(chip * span, span)
-            mine = pl.ds(pl.multiple_of((2 * chip + self.core) * span, span), span)
-            self.pair_in[rows] = (self.pair_in[rows].astype(f32) + self.full[mine].astype(f32)).astype(bf16)
-        for k in range(1, self.chips * self.n_ctx):
-            self.peer_copy(k).start()
-
-    def end(self):
-        self.result[...] = self.pair_in[self.block_rows(self.place)].astype(f32)
-        for k in range(1, self.chips * self.n_ctx):
-            self.peer_copy(k).wait()
-            self.result[...] += self.peer_in[k - 1].astype(f32)
-        for chip in range(self.chips):
-            self.pair_copy(chip).wait_send()
-
-
-def owners_scratch(n_xy, shape):
-    n_fsdp, n_ctx = n_xy
-    peers = n_fsdp // 2 * n_ctx - 1
-    block = shape[0] // (n_fsdp * n_ctx)
-    return [
-        pltpu.VMEM((shape[0] // 2, shape[1]), bf16), pltpu.VMEM((peers, block, shape[1]), bf16),
-        pltpu.SemaphoreType.DMA((2, n_fsdp // 2)), pltpu.SemaphoreType.DMA((2, peers)),
-    ]
-
-
-def input_grad_kernel(
-    n, n_xy, grad_qkv, w_full_hbm, mixed_own, gains, weights, grad_out, gains_sum, weights_own,
-    buf, total, send, recv, w_qkv, w_sem, piece_sems, gains_theirs, gain_send, gain_recv,
-    pair_in, peer_in, pair_sems, peer_sems,
-):
-    rows, width = buf.shape[1:]
-    groups = rows // (n * PIECE)
-    per_chunk = CHUNK // (n * PIECE)
-    line = Line("tp", n, groups, buf, total, send, recv)
-    fetch = pltpu.make_async_copy(w_full_hbm.at[:, pl.ds(0, w_qkv.shape[1])], w_qkv, w_sem)
-    fetch.start()
-    n_fsdp, n_ctx = n_xy
-    place = lax.axis_index("fsdp") * n_ctx + lax.axis_index("ctx")
-    others = []
-    for k in range(1, n_fsdp * n_ctx):
-        peer = lax.rem(place + k, n_fsdp * n_ctx)
-        others.append({"fsdp": lax.div(peer, n_ctx), "ctx": lax.rem(peer, n_ctx)})
-    greet("tp", n, others)
-    gain_copies = [
-        pltpu.make_async_remote_copy(
-            src_ref=gains, dst_ref=gains_theirs.at[k], send_sem=gain_send.at[k], recv_sem=gain_recv.at[k],
-            device_id=peer, device_id_type=pl.DeviceIdType.MESH,
-        )
-        for k, peer in enumerate(others)
-    ]
-    for copy in gain_copies:
-        copy.start()
-    owners = Owners(n_xy, weights, pair_in, peer_in, weights_own, pair_sems, peer_sems)
-    owners.start()
-    fetch.wait()
-    tile = 512
-
-    def own(group, total):
-        return total + mixed_own[pl.ds(pl.multiple_of(group * PIECE, PIECE), PIECE)]
-
-    def done(group):
-        copies = local_copies(
-            [(line.piece_ref(group, c), grad_out.at[line.rows(group, c)]) for c in range(n)], piece_sems
-        )
-        for copy in copies:
-            copy.wait()
-
-    @pl.loop(0, line.ticks())
-    def _(t):
-        @pl.when((t < groups) & (lax.rem(t, per_chunk) == 0))
-        def _():
-            at = pl.ds(pl.multiple_of(t * n * PIECE, CHUNK), CHUNK)
-
-            @pl.loop(0, width // tile)
-            def _(j):
-                cols = pl.ds(pl.multiple_of(j * tile, tile), tile)
-                buf[1, at, cols] = dot(grad_qkv[at], w_qkv[cols], ((1,), (1,)), bf16)
-
-        line.tick(t, own, done)
-
-        @pl.when(t == 2)
-        def _():
-            owners.pass_on()
-
-    owners.end()
-    gains_sum[...] = gains[...]
-    for k, copy in enumerate(gain_copies):
-        copy.wait()
-        gains_sum[...] += gains_theirs[k]
-
-
-def input_grad(grad_qkv, w_full, mixed_own, gains, weights, n, n_xy):
-    rows, width = grad_qkv.shape[0], w_full.shape[0]
-    peers = n_xy[0] * n_xy[1] - 1
-    vmem, anywhere = pl.BlockSpec(memory_space=pltpu.VMEM), pl.BlockSpec(memory_space=pl.ANY)
-    return pl.pallas_call(
-        functools.partial(input_grad_kernel, n, n_xy),
-        out_shape=[
-            jax.ShapeDtypeStruct((rows, width), bf16), jax.ShapeDtypeStruct(gains.shape, f32),
-            jax.ShapeDtypeStruct((weights.shape[0] // (n_xy[0] * n_xy[1]), weights.shape[1]), f32),
-        ],
-        in_specs=[vmem, anywhere, vmem, vmem, vmem],
-        out_specs=[anywhere, vmem, vmem],
-        scratch_shapes=line_scratch(n, rows, width) + [
-            pltpu.VMEM((width, grad_qkv.shape[1]), bf16), pltpu.SemaphoreType.DMA, pltpu.SemaphoreType.DMA((n,)),
-            pltpu.VMEM((peers,) + gains.shape, f32), pltpu.SemaphoreType.DMA((peers,)), pltpu.SemaphoreType.DMA((peers,)),
-        ] + owners_scratch(n_xy, weights.shape),
-        compiler_params=params(3),
-        cost_estimate=pl.CostEstimate(flops=100 * 10**9, bytes_accessed=20 << 20, transcendentals=0),
-        name="input_grad",
-    )(grad_qkv, w_full, mixed_own, gains, weights)
 
 
 def peers_of(axis, n):
@@ -1048,37 +896,147 @@
     )(x, w_q, w_k, w_v, w_o, gain_q, gain_k, gain_a, cosine, sine)
 
 
-def attend_back_kernel(
-    n_tp, n_ctx, seqs, attn_low, w_full, raw, low, prev, stats, x, head_low, gain_q, gain_k, cosine, sine, gain_a,
-    grad_qkv, gain_qk_sum, gain_a_sum, weights_out,
-    grad_heads, grad_q, grad_kv, out_kv, in_kv, sums, theirs, gain_theirs, kv_send, kv_recv, sum_send, sum_recv,
+class Owners:
+    def __init__(self, n_xy, full, first, columns, pair_in, peer_in, stage, stage_sem, pair_sems, peer_sems):
+        n_fsdp, self.n_ctx = n_xy
+        self.chips = n_fsdp // 2
+        self.first, self.columns = first, columns
+        self.full, self.pair_in, self.peer_in = full, pair_in, peer_in
+        self.stage, self.stage_sem = stage, stage_sem
+        self.pair_sems, self.peer_sems = pair_sems, peer_sems
+        fsdp = lax.axis_index("fsdp")
+        self.chip, self.core = lax.div(fsdp, 2), lax.rem(fsdp, 2)
+        self.place = self.chip * self.n_ctx + lax.axis_index("ctx")
+        self.block = full.shape[0] // (n_fsdp * self.n_ctx)
+        self.span = self.n_ctx * self.block
+
+    def cols(self):
+        return pl.ds(self.first, self.columns)
+
+    def pair_copy(self, chip):
+        there = 1 - self.core
+        rows = pl.ds(pl.multiple_of((2 * chip + there) * self.span, self.span), self.span)
+        return pltpu.make_async_remote_copy(
+            src_ref=self.full.at[rows, self.cols()],
+            dst_ref=self.pair_in.at[pl.ds(chip * self.span, self.span), self.cols()],
+            send_sem=self.pair_sems.at[0, chip], recv_sem=self.pair_sems.at[1, chip],
+            device_id={"fsdp": 2 * self.chip + there}, device_id_type=pl.DeviceIdType.MESH,
+        )
+
+    def peer_copy(self, k):
+        place = lax.rem(self.place + k, self.chips * self.n_ctx)
+        return pltpu.make_async_remote_copy(
+            src_ref=self.pair_in.at[self.block_rows(place), self.cols()],
+            dst_ref=self.peer_in.at[k - 1, :, self.cols()],
+            send_sem=self.peer_sems.at[0, k - 1], recv_sem=self.peer_sems.at[1, k - 1],
+            device_id={"fsdp": 2 * lax.div(place, self.n_ctx) + self.core, "ctx": lax.rem(place, self.n_ctx)},
+            device_id_type=pl.DeviceIdType.MESH,
+        )
+
+    def block_rows(self, place):
+        return pl.ds(pl.multiple_of(place * self.block, self.block), self.block)
+
+    def start(self):
+        for chip in range(self.chips):
+            self.pair_copy(chip).start()
+
+    def pass_on(self):
+        unit = min(self.span, self.stage.shape[0])
+        for chip in range(self.chips):
+            for u in range(self.span // unit):
+                mine = pl.multiple_of((2 * chip + self.core) * self.span + u * unit, unit)
+                fetch = pltpu.make_async_copy(
+                    self.full.at[pl.ds(mine, unit), self.cols()],
+                    self.stage.at[pl.ds(0, unit), pl.ds(0, self.columns)], self.stage_sem,
+                )
+                fetch.start()
+                if u == 0:
+                    self.pair_copy(chip).wait_recv()
+                fetch.wait()
+                rows = pl.ds(chip * self.span + u * unit, unit)
+                both = self.pair_in[rows, self.cols()].astype(f32) + self.stage[:unit, : self.columns].astype(f32)
+                self.pair_in[rows, self.cols()] = both.astype(bf16)
+        for k in range(1, self.chips * self.n_ctx):
+            self.peer_copy(k).start()
+
+    def end(self, result, width):
+        for k in range(1, self.chips * self.n_ctx):
+            self.peer_copy(k).wait()
+        for part in range(self.first // width, (self.first + self.columns) // width):
+            cols = pl.ds(part * width, width)
+            sums = self.pair_in[self.block_rows(self.place), cols].astype(f32)
+            for k in range(1, self.chips * self.n_ctx):
+                sums = sums + self.peer_in[k - 1, :, cols].astype(f32)
+            result[part * self.block : (part + 1) * self.block] = sums
+        for chip in range(self.chips):
+            self.pair_copy(chip).wait_send()
+
+
+def back_kernel(
+    n_tp, n_xy, seqs,
+    attn_low_hbm, w_hbm, raw_hbm, low_hbm, prev_hbm, head_low_hbm, stats_hbm, x_hbm, mixed_own_hbm,
+    attention_hbm, down_hbm, gain_q, gain_k, gain_a, gain_m, gain_a_own, gain_m_own, cosine, sine,
+    grad_out, out_out, gains_sum, weights_own, weights_out,
+    buf, total, send, recv, w, raw, low, kv, in_kv, head_low, stats, x, mixed_own, grad_heads, grad_q, grad_kv,
+    grad_qkv, tiles, pair_in, peer_in, branches, outs, gains, gains_theirs, gain_qk,
+    sums, theirs, gain_theirs, load_sems, kv_send, kv_recv, sum_send, sum_recv, tile_sems, stage_sem,
+    pair_sems, peer_sems, gain_send, gain_recv, piece_sems, branch_sems, out_sems,
 ):
-    rows_all, width = attn_low.shape
+    n_fsdp, n_ctx = n_xy
+    rows_all, width = x.shape
     rows = rows_all // seqs
     local = head_low.shape[1]
     heads = local // HD
     me = lax.axis_index("ctx")
     scale = HD ** (-0.5)
-    meet([("tp", n_tp), ("ctx", n_ctx)])
     step = min(256, rows)
-
-    def chunks(body):
-        @pl.loop(0, rows_all // step)
+    out_at = 3 * local
+    groups = rows_all // (n_tp * PIECE)
+    line = Line("tp", n_tp, groups, buf, total, send, recv)
+    per_chunk, per_seq = step // (n_tp * PIECE), rows // (n_tp * PIECE)
+    attn_low = buf.at[1]
+    qkv_cols, out_cols = pl.ds(0, out_at), pl.ds(out_at, local)
+    loads = local_copies(
+        [
+            (attn_low_hbm, attn_low), (w_hbm.at[:, out_cols], w.at[:, out_cols]), (prev_hbm, kv), (low_hbm, low),
+            (head_low_hbm, head_low), (stats_hbm, stats), (raw_hbm, raw), (x_hbm, x),
+            (w_hbm.at[:, qkv_cols], w.at[:, qkv_cols]), (mixed_own_hbm, mixed_own),
+        ],
+        load_sems,
+    )
+    place = lax.axis_index("fsdp") * n_ctx + me
+    others = []
+    for k in range(1, n_fsdp * n_ctx):
+        peer = lax.rem(place + k, n_fsdp * n_ctx)
+        others.append({"fsdp": lax.div(peer, n_ctx), "ctx": lax.rem(peer, n_ctx)})
+    meet([("tp", n_tp)], others)
+
+    def chunks(body, seq=None):
+        count = rows_all if seq is None else rows
+        first = 0 if seq is None else seq * rows
+
+        @pl.loop(0, count // step)
         def _(k):
-            at = pl.ds(pl.multiple_of(k * step, step), step)
+            at = pl.ds(pl.multiple_of(first + k * step, step), step)
             body(at, pl.ds(pl.multiple_of(me * rows + lax.rem(k, rows // step) * step, step), step))
 
+    loads[0].wait()
+    loads[1].wait()
+
     def heads_chunk(at, _):
-        grad_heads[at] = dot(attn_low[at], w_full[:, 3 * local :], ((1,), (0,)), bf16)
+        grad_heads[at] = dot(attn_low[at], w[:, out_cols], ((1,), (0,)), bf16)
 
     chunks(heads_chunk)
     grad_q[...] = jnp.zeros_like(grad_q)
     grad_kv[...] = jnp.zeros_like(grad_kv)
+    gain_qk[...] = jnp.zeros_like(gain_qk)
+    for load in loads[2:6]:
+        load.wait()
 
     def kv_copy(j, seq):
         at = pl.ds(seq * rows, rows)
         return pltpu.make_async_remote_copy(
-            src_ref=out_kv.at[j - 1, at], dst_ref=in_kv.at[j - 1, at],
+            src_ref=kv.at[j - 1, at], dst_ref=in_kv.at[j - 1, at],
             send_sem=kv_send.at[j - 1, seq], recv_sem=kv_recv.at[j - 1, seq],
             device_id={"ctx": lax.rem(me + n_ctx - j, n_ctx)}, device_id_type=pl.DeviceIdType.MESH,
         )
@@ -1107,14 +1065,14 @@
                 seq_rows = pl.ds(seq * rows, rows)
 
                 def one_head(h, cols):
-                    keys, values = prev[j - 1, seq_rows, cols(0, local)], prev[j - 1, seq_rows, cols(1, local)]
+                    keys, values = kv[j - 1, seq_rows, cols(0, local)], kv[j - 1, seq_rows, cols(1, local)]
                     dk, dv = 0.0, 0.0
                     for tile in range(rows // step):
                         at = pl.ds(seq * rows + tile * step, step)
                         k_term, v_term = block(h, cols, at, keys, values, None)
                         dk, dv = dk + k_term, dv + v_term
-                    out_kv[j - 1, seq_rows, cols(0, local)] = dk.astype(bf16)
-                    out_kv[j - 1, seq_rows, cols(1, local)] = dv.astype(bf16)
+                    kv[j - 1, seq_rows, cols(0, local)] = dk.astype(bf16)
+                    kv[j - 1, seq_rows, cols(1, local)] = dv.astype(bf16)
 
                 heads_loop(heads, one_head)
                 kv_copy(j, seq).start()
@@ -1136,22 +1094,48 @@
 
         heads_loop(heads, one_head)
 
-    def weight_rows(left, right, cols):
-        @pl.loop(0, width // step)
-        def _(k):
-            at = pl.ds(pl.multiple_of(k * step, step), step)
-            weights_out[at, cols] = dot(left[:, at], right[...], ((0,), (0,)), bf16)
-
-    weight_rows(attn_low, head_low, pl.ds(3 * local, local))
-
-    for j in range(1, n_ctx):
-        for seq in range(seqs):
-
-            @pl.when(me + j < n_ctx)
-            def _():
-                kv_copy(j, seq).wait_recv()
-                at = pl.ds(seq * rows, rows)
-                grad_kv[at] += in_kv[j - 1, at].astype(f32)
+    blocks = width // WEIGHT_ROWS
+
+    def tile_copy(k, slot, first, columns):
+        return pltpu.make_async_copy(
+            tiles.at[slot, :, pl.ds(0, columns)],
+            weights_out.at[
+                pl.ds(pl.multiple_of(k * WEIGHT_ROWS, WEIGHT_ROWS), WEIGHT_ROWS), pl.ds(first, columns)
+            ],
+            tile_sems.at[slot],
+        )
+
+    def weight_tile(k, left, right, first, columns):
+        slot = lax.rem(k, 2)
+
+        @pl.when(k >= 2)
+        def _():
+            tile_copy(k - 2, slot, first, columns).wait()
+
+        at = pl.ds(pl.multiple_of(k * WEIGHT_ROWS, WEIGHT_ROWS), WEIGHT_ROWS)
+        tiles[slot, :, :columns] = dot(left[:, at], right[...], ((0,), (0,)), bf16)
+        tile_copy(k, slot, first, columns).start()
+
+    def tiles_end(first, columns):
+        for k in (blocks - 2, blocks - 1):
+            tile_copy(k, k % 2, first, columns).wait()
+
+    def owners(index, first, columns):
+        return Owners(
+            n_xy, weights_out, first, columns, pair_in, peer_in, low, stage_sem,
+            pair_sems.at[index], peer_sems.at[index],
+        )
+
+    owners_out, owners_qkv = owners(0, out_at, local), owners(1, 0, out_at)
+
+    @pl.loop(0, blocks)
+    def _(k):
+        weight_tile(k, attn_low, head_low, out_at, local)
+
+    tiles_end(out_at, local)
+    owners_out.start()
+    for load in loads[6:]:
+        load.wait()
 
     def turned(at, pos, part, ref, gain):
         inner = 0.0
@@ -1163,36 +1147,163 @@
             inner = inner + jnp.sum(weighted, axis=-1, keepdims=True)
         return inner
 
-    def inner_chunk(at, pos):
-        both = two_lanes(
-            turned(at, pos, 0, grad_q, gain_q), turned(at, pos, 1, grad_kv, gain_k)
+    def norm_back(seq):
+        for j in range(1, n_ctx):
+
+            @pl.when(me + j < n_ctx)
+            def _():
+                kv_copy(j, seq).wait_recv()
+                at = pl.ds(seq * rows, rows)
+                grad_kv[at] += in_kv[j - 1, at].astype(f32)
+
+        def inner_chunk(at, pos):
+            both = two_lanes(turned(at, pos, 0, grad_q, gain_q), turned(at, pos, 1, grad_kv, gain_k))
+            sums[:, at] = lanes_to_rows(both)
+
+        chunks(inner_chunk, seq)
+        seq_rows = pl.ds(seq * rows, rows)
+        pairs = [(sums.at[:, seq_rows], theirs.at[:, :, seq_rows])]
+        if seq == 0:
+            pairs.append((gain_a_own, gain_theirs))
+        swap("tp", n_tp, pairs, sum_send.at[seq], sum_recv.at[seq])
+        inner_sums = sums[:, seq_rows]
+        for slot in range(n_tp - 1):
+            inner_sums = inner_sums + theirs[slot, :, seq_rows]
+        sums[:, seq_rows] = inner_sums / width
+
+        def out_chunk(at, _):
+            inner = rows_to_lanes(sums[:, at])
+            for part, ref, gain in ((0, grad_q, gain_q), (1, grad_kv, gain_k)):
+                r = stats[at, part : part + 1]
+                d, v = ref[at, :local], raw[at, pl.ds(part * local, local)]
+                grad_qkv[at, pl.ds((2 - part) * local, local)] = (
+                    d * r * gain[...] - v * (r * r * r) * inner[:, part : part + 1]
+                ).astype(bf16)
+                gain_qk[part : part + 1] += jnp.sum(d * v * r, axis=0, keepdims=True)
+            grad_qkv[at, :local] = grad_kv[at, local:].astype(bf16)
+
+        chunks(out_chunk, seq)
+
+    def gain_copies():
+        return [
+            pltpu.make_async_remote_copy(
+                src_ref=gains, dst_ref=gains_theirs.at[k], send_sem=gain_send.at[k], recv_sem=gain_recv.at[k],
+                device_id=peer, device_id_type=pl.DeviceIdType.MESH,
+            )
+            for k, peer in enumerate(others)
+        ]
+
+    def send_gains():
+        gains[:, :local] = gain_qk[0:1]
+        gains[:, local : 2 * local] = gain_qk[1:2]
+        gain_total = gain_a_own[...]
+        for slot in range(n_tp - 1):
+            gain_total = gain_total + gain_theirs[slot]
+        gains[:, 2 * local : 2 * local + width] = gain_total
+        gains[:, 2 * local + width :] = gain_m_own[...]
+        for copy in gain_copies():
+            copy.start()
+
+    norm_back(0)
+    if seqs == 1:
+        send_gains()
+
+    span = n_tp * PIECE
+
+    def group_rows(group):
+        return pl.ds(pl.multiple_of(group * span, span), span)
+
+    def branch_copies(group):
+        at, slot = group_rows(group), lax.rem(group, 4)
+        return [
+            pltpu.make_async_copy(attention_hbm.at[at], branches.at[slot, 0], branch_sems.at[slot, 0]),
+            pltpu.make_async_copy(down_hbm.at[at], branches.at[slot, 1], branch_sems.at[slot, 1]),
+        ]
+
+    def out_copy(group):
+        slot = lax.rem(group, 2)
+        return pltpu.make_async_copy(outs.at[slot], out_out.at[group_rows(group)], out_sems.at[slot])
+
+    def own(group, total):
+        for copy in branch_copies(group):
+            copy.start()
+        return total + mixed_own[pl.ds(pl.multiple_of(group * PIECE, PIECE), PIECE)]
+
+    def done(group):
+        copies = local_copies(
+            [(line.piece_ref(group, c), grad_out.at[line.rows(group, c)]) for c in range(n_tp)], piece_sems
         )
-        sums[:, at] = lanes_to_rows(both)
-
-    chunks(inner_chunk)
-    swap("tp", n_tp, [(sums, theirs), (gain_a, gain_theirs)], sum_send, sum_recv)
-    total, gain_total = sums[...], gain_a[...]
-    for slot in range(n_tp - 1):
-        total = total + theirs[slot]
-        gain_total = gain_total + gain_theirs[slot]
-    gain_a_sum[...] = gain_total
-    sums[...] = total / width
-    gain_qk_sum[...] = jnp.zeros_like(gain_qk_sum)
-
-    def out_chunk(at, _):
-        inner = rows_to_lanes(sums[:, at])
-        for part, ref, gain in ((0, grad_q, gain_q), (1, grad_kv, gain_k)):
-            r = stats[at, part : part + 1]
-            d, v = ref[at, :local], raw[at, pl.ds(part * local, local)]
-            grad_qkv[at, pl.ds((2 - part) * local, local)] = (
-                d * r * gain[...] - v * (r * r * r) * inner[:, part : part + 1]
-            ).astype(bf16)
-            gain_qk_sum[part : part + 1] += jnp.sum(d * v * r, axis=0, keepdims=True)
-        grad_qkv[at, :local] = grad_kv[at, local:].astype(bf16)
-
-    chunks(out_chunk)
-    weight_rows(x, grad_qkv, pl.ds(0, 3 * local))
-
+        for copy in branch_copies(group):
+            copy.wait()
+
+        @pl.when(group >= 2)
+        def _():
+            out_copy(group - 2).wait()
+
+        slot = lax.rem(group, 4)
+        a, d = branches[slot, 0].astype(f32), branches[slot, 1].astype(f32)
+        mixed = x[group_rows(group)].astype(f32) + a * scale_of(a) * gain_a[...]
+        outs[lax.rem(group, 2)] = (mixed + d * scale_of(d) * gain_m[...]).astype(bf16)
+        out_copy(group).start()
+        for copy in copies:
+            copy.wait()
+
+    tile = 1024
+    weights_tick = (seqs - 1) * per_seq
+    weights_ticks = -(-blocks // WEIGHT_TILES)
+
+    @pl.loop(0, line.ticks())
+    def _(t):
+        @pl.when((t < groups) & (lax.rem(t, per_chunk) == 0))
+        def _():
+            at = pl.ds(pl.multiple_of(t * span, step), step)
+
+            @pl.loop(0, width // tile)
+            def _(j):
+                cols = pl.ds(pl.multiple_of(j * tile, tile), tile)
+                buf[1, at, cols] = dot(grad_qkv[at], w[cols, qkv_cols], ((1,), (1,)), bf16)
+
+        line.tick(t, own, done)
+
+        @pl.when(t == 0)
+        def _():
+            owners_out.pass_on()
+
+        for seq in range(1, seqs):
+
+            @pl.when(t == seq * per_seq - 1)
+            def _():
+                norm_back(seq)
+                if seq == seqs - 1:
+                    send_gains()
+
+        for m in range(WEIGHT_TILES):
+            k = (t - weights_tick) * WEIGHT_TILES + m
+
+            @pl.when((k >= 0) & (k < blocks))
+            def _():
+                weight_tile(k, x, grad_qkv, 0, out_at)
+
+        @pl.when(t == weights_tick + weights_ticks - 1)
+        def _():
+            tiles_end(0, out_at)
+            owners_qkv.start()
+
+        @pl.when(t == weights_tick + weights_ticks)
+        def _():
+            owners_qkv.pass_on()
+
+    for group in (groups - 2, groups - 1):
+        out_copy(group).wait()
+    gains_sum[...] = gains[...]
+    for k, copy in enumerate(gain_copies()):
+        copy.wait()
+        gains_sum[...] += gains_theirs[k]
+    owners_out.end(grad_q, local)
+    owners_qkv.end(grad_q, local)
+    result = pltpu.make_async_copy(grad_q.at[pl.ds(0, weights_own.shape[0])], weights_own, stage_sem)
+    result.start()
+    result.wait()
     for j in range(1, n_ctx):
         for seq in range(seqs):
 
@@ -1201,35 +1312,49 @@
                 kv_copy(j, seq).wait_send()
 
 
-def attend_back(
-    attn_low, w_full, raw, low, prev, stats, x, head_low, gain_q, gain_k, cosine, sine, gain_a, seqs, n_tp, n_ctx
+def back(
+    attn_low, w, raw, low, prev, head_low, stats, x, mixed_own, attention, down,
+    gain_q, gain_k, gain_a, gain_m, gain_a_own, gain_m_own, cosine, sine, seqs, n_tp, n_xy,
 ):
-    rows, width = attn_low.shape
+    rows, width = x.shape
     local = head_low.shape[1]
-    vmem = pl.BlockSpec(memory_space=pltpu.VMEM)
-    shape = jax.ShapeDtypeStruct
+    n_fsdp, n_ctx = n_xy
+    vmem, anywhere = pl.BlockSpec(memory_space=pltpu.VMEM), pl.BlockSpec(memory_space=pl.ANY)
+    shape, dma = jax.ShapeDtypeStruct, pltpu.SemaphoreType.DMA
+    devices, peers = n_fsdp * n_ctx, n_fsdp // 2 * n_ctx - 1
     blocks = max(n_ctx - 1, 1)
-    kv_sems = pltpu.SemaphoreType.DMA((blocks, seqs))
-    sum_sems = pltpu.SemaphoreType.DMA((2, n_tp - 1))
+    block = width // devices
+    gains = (1, 2 * (local + width))
+    acts = shape(x.shape, bf16)
+    span = n_tp * PIECE
+    like = lambda a: pltpu.VMEM(a.shape, a.dtype)
     return pl.pallas_call(
-        functools.partial(attend_back_kernel, n_tp, n_ctx, seqs),
+        functools.partial(back_kernel, n_tp, n_xy, seqs),
         out_shape=[
-            shape((rows, 3 * local), bf16), shape((8, local), f32), shape(gain_a.shape, f32),
-            shape((width, 4 * local), bf16),
+            acts, acts, shape(gains, f32), shape((4 * block, local), f32), shape((width, 4 * local), bf16),
         ],
-        in_specs=[vmem] * 13,
-        out_specs=[vmem] * 4,
-        scratch_shapes=[
-            pltpu.VMEM((rows, local), bf16), pltpu.VMEM((rows, local), f32), pltpu.VMEM((rows, 2 * local), f32),
-            pltpu.VMEM((blocks, rows, 2 * local), bf16), pltpu.VMEM((blocks, rows, 2 * local), bf16),
-            pltpu.VMEM((8, rows), f32), pltpu.VMEM((n_tp - 1, 8, rows), f32),
-            pltpu.VMEM((n_tp - 1,) + gain_a.shape, f32),
-            kv_sems, kv_sems, sum_sems, sum_sems,
+        in_specs=[anywhere] * 11 + [vmem] * 8,
+        out_specs=[anywhere, anywhere, vmem, anywhere, anywhere],
+        scratch_shapes=line_scratch(n_tp, rows, width) + [
+            like(w), like(raw), like(low), like(prev), like(prev), like(head_low), like(stats), like(x), like(mixed_own),
+            pltpu.VMEM((rows, local), bf16), pltpu.VMEM((max(rows, 4 * block), local), f32),
+            pltpu.VMEM((rows, 2 * local), f32),
+            pltpu.VMEM((rows, 3 * local), bf16), pltpu.VMEM((2, WEIGHT_ROWS, 3 * local), bf16),
+            pltpu.VMEM((width // 2, 4 * local), bf16), pltpu.VMEM((peers, block, 4 * local), bf16),
+            pltpu.VMEM((4, 2, span, width), bf16), pltpu.VMEM((2, span, width), bf16),
+            pltpu.VMEM(gains, f32), pltpu.VMEM((devices - 1,) + gains, f32), pltpu.VMEM((8, local), f32),
+            pltpu.VMEM((8, rows), f32), pltpu.VMEM((n_tp - 1, 8, rows), f32), pltpu.VMEM((n_tp - 1, 1, width), f32),
+            dma((10,)), dma((blocks, seqs)), dma((blocks, seqs)), dma((seqs, 2, n_tp - 1)), dma((seqs, 2, n_tp - 1)),
+            dma((2,)), dma, dma((2, 2, n_fsdp // 2)), dma((2, 2, peers)), dma((devices - 1,)), dma((devices - 1,)),
+            dma((n_tp,)), dma((4, 2)), dma((2,)),
         ],
-        compiler_params=params(5),
-        cost_estimate=pl.CostEstimate(flops=60 * 10**9, bytes_accessed=30 << 20, transcendentals=0),
-        name="attend_back",
-    )(attn_low, w_full, raw, low, prev, stats, x, head_low, gain_q, gain_k, cosine, sine, gain_a)
+        compiler_params=params(3),
+        cost_estimate=pl.CostEstimate(flops=200 * 10**9, bytes_accessed=60 << 20, transcendentals=0),
+        name="back",
+    )(
+        attn_low, w, raw, low, prev, head_low, stats, x, mixed_own, attention, down,
+        gain_q, gain_k, gain_a, gain_m, gain_a_own, gain_m_own, cosine, sine,
+    )
 
 
 def rotation_tables(length):
@@ -1265,13 +1390,9 @@
     w_u = gather(w_up)
     w_down_t = gather(w_down.T)
 
-    def rms(a):
-        return lax.rsqrt(jnp.mean(a * a, axis=-1, keepdims=True) + norm_eps)
-
     flat = (micro_count * rows, width)
     x_all, grad_all = tokens.reshape(flat), cotangent.reshape(flat)
 
-    tables = (gain_q[None], gain_k[None], cosine, sine)
     n_xy = (lax.axis_size("fsdp"), ctx)
     raw, low, prev, head_low, stats, attention, mlp_in, w_full, attn_own = front(
         x_all, w_query, w_key, w_value, w_output.T, gain_q[None], gain_k[None], gain_a[None], cosine, sine,
@@ -1280,30 +1401,24 @@
     down, _, attn_low, mlp_weights, mixed_own, gain_m_sum, gain_a_sum = mlp(
         mlp_in, grad_all, attn_own, gain_m[None], gain_a[None], w_g, w_u, w_down_t, tp
     )
-    att, down = attention.astype(f32), down.astype(f32)
-    out = (x_all.astype(f32) + att * rms(att) * gain_a + down * rms(down) * gain_m).astype(bf16)
-
     def scatter(full):
         return lax.psum_scatter(full, xy, scatter_dimension=0, tiled=True).astype(f32)
 
     units = w_gate.shape[1]
     d_mlp = scatter(mlp_weights)
     d_down, d_gate, d_up = d_mlp[:, :units].T, d_mlp[:, units : 2 * units], d_mlp[:, 2 * units :]
-    grad_qkv, gain_qk_sum, gain_a_tp, attn_weights = attend_back(
-        attn_low, w_full, raw, low, prev, stats, x_all, head_low, *tables, gain_a_sum, micro_count, tp, ctx
+    grad_tokens, out, gains, d_attn, _ = back(
+        attn_low, w_full, raw, low, prev, head_low, stats, x_all, mixed_own, attention, down,
+        gain_q[None], gain_k[None], gain_a[None], gain_m[None], gain_a_sum, gain_m_sum, cosine, sine,
+        micro_count, tp, n_xy
     )
-    gains = jnp.concatenate(
-        [gain_qk_sum[0], gain_qk_sum[1], gain_a_tp[0], gain_m_sum[0]]
-    ).reshape(8, (local + width) // 4)
-    grad_tokens, gains, d_attn = input_grad(
-        grad_qkv, w_full, mixed_own, gains, attn_weights, tp, n_xy
-    )
-    gains = gains.reshape(2 * (local + width))
+    gains = gains[0]
+    block = w_query.shape[0]
+    d_v, d_k, d_q, d_o = (d_attn[k * block : (k + 1) * block] for k in range(4))
     return (
         out.reshape(tokens.shape),
         grad_tokens.reshape(tokens.shape),
-        d_attn[:, 2 * local : 3 * local], d_attn[:, local : 2 * local], d_attn[:, :local],
-        d_attn[:, 3 * local :].T, d_gate, d_up, d_down,
+        d_q, d_k, d_v, d_o.T, d_gate, d_up, d_down,
         gains[:local], gains[local : 2 * local],
         gains[2 * local : 2 * local + width], gains[2 * local + width :],
     )

time: 743 us -> 731 us (0.984)
  waiting for transfers between devices: 1.47 us -> 39.4 us
  Pallas kernels: 680 us -> 648 us
  other arithmetic: 19.2 us -> 4.99 us
    pallas_call x2 -> x1, Pallas kernels: 226 us -> 188 us  [back(): pl.pallas_call(functools.partial(back_kernel, n_tp, n_xy, seqs), out_shap...]
    reduce_scatter x1, waiting for transfers between devices: 0.01 us -> 37.9 us  [scatter(): lax.psum_scatter(full, xy, scatter_dimension=0, tiled=True).astype(f32)]
    convert_element_type x3 -> x0, other arithmetic: 7.66 us -> none  [the longest x1 6.45 us: per_device(): (x_all.astype(f32) + att * rms(att) * gain_a + down * rms(down) * gain_m)...]
  transfers between devices with their start and end apart: 4 -> 4, of which waited for: 0 -> 1; matrix products, arithmetic and copies ran while one was open for 3% -> 1% of each run, Pallas kernels for 60% -> 56%
where the time goes in v4:
time: 731 us; the launch traced here: 728 us
  Pallas kernels  648 us (89%)
  waiting for transfers between devices  39.4 us (5%)
  local copies, waits for them, and re-layouts  22 us (3%)
  between operations  14.1 us (2%)
    pallas_call x1, Pallas kernels, mlp(): pl.pallas_call(functools.partial(mlp_kernel, n), out_shape=[acts, inner,...  243 us
    pallas_call x1, Pallas kernels, front(): pl.pallas_call(functools.partial(front_kernel, n_tp, n_xy, seqs), out_sha...  217 us
    pallas_call x1, Pallas kernels, back(): pl.pallas_call(functools.partial(back_kernel, n_tp, n_xy, seqs), out_shap...  188 us
    reduce_scatter x1, waiting for transfers between devices, scatter(): lax.psum_scatter(full, xy, scatter_dimension=0, tiled=True).astype(f32)  37.9 us
  transfers between devices with their start and end apart: 4, of which 1 were waited for; matrix products, arithmetic and copies ran while one was open for 1% of the time, Pallas kernels for 56%

profile of v4, /device:TPU:0, one launch (start us, length us, event | category | flops | bytes accessed | tf_op | source)
XLA Modules:
  0.0 728.4 jit_solution(13094115547547532729)
XLA Ops:
  7.3 0.7 all-gather.4.cloned.1.call-update
  8.0 0.7 all-gather.6.cloned.1.call-update
  8.8 2.3 copy.29
  11.1 0.6 broadcast_in_dim.33
  11.7 0.6 broadcast_in_dim.34
  12.3 0.6 broadcast_in_dim.35
  12.9 0.6 broadcast_in_dim.36
  13.5 0.8 copy.28
  14.3 216.8 %front.1 = (f32[1024,1024]{1,0:T(8,128)}, bf16[1024,1536]{1,0:T(8,128)(2,1)}, bf16[1,1024,1024]{2,1,0:T(8,128)(2,1)}, bf16[1024,512]{1,0:T(8,128)(2,1)}, f32[102...) custom-call(bf16[1024,2048]{1,0:T(8,128)(2,1)} %bitcast.36, ...), custom_call_target="tpu_custom_call" | custom-call | flops 149999992832 | bytes 31457280 | tf_op jit(solution)/shard_map/front/pallas_call | solution.py:881
  231.3 243.1 %mlp.1 = (bf16[1024,2048]{1,0:T(8,128)(2,1)}, bf16[1024,2048]{1,0:T(8,128)(2,1)}, bf16[1024,2048]{1,0:T(8,128)(2,1)}, bf16[2048,6144]{1,0:T(8,128)(2,1)}, f32[25...) custom-call(bf16[1024,2048]{1,0:T(8,128)(2,1)} %get-tuple-element.32.mlp_in, bf16[1024,2048]{1,0:T(8,128)(2,1)} %bitcast.35, ...), custom_call_target="tpu_custom_call" | custom-call | flops 199999995904 | bytes 62914560 | tf_op jit(solution)/shard_map/mlp/pallas_call | solution.py:481
  474.4 187.7 %back.1 = (bf16[1024,2048]{1,0:T(8,128)(2,1)}, bf16[1024,2048]{1,0:T(8,128)(2,1)}, f32[1,5120]{1,0:T(1,128)}, f32[1024,512]{1,0:T(8,128)}, bf16[2048,2048]{1,0:T(8,128)(2,1)}) custom-call(bf16[1024,2048]{1,0:T(8,128)(2,1)} %get-tuple-element.34.attn_low_hbm, bf16[2048,2048]{1,0:T(8,128)(2,1)} %get-tuple-element.35.w_hbm, ...), custom_call_target="tpu_custom_call" | custom-call | flops 199999995904 | bytes 62914560 | tf_op jit(solution)/shard_map/back/pallas_call | solution.py:1331
  662.2 2.7 slice_bitcast_fusion.1
  664.9 1.0 copy.30
  665.9 0.6 fusion.2
  666.5 0.6 fusion.1
  667.1 37.9 %reduce-scatter.2.cloned.1.call-done = bf16[256,6144]{1,0:T(8,128)(2,1)} async-done(((bf16[2048,6144]{1,0:T(8,128)(2,1)}), bf16[256,6144]{1,0:T(8,128)(2,1)}) %reduce-scatter.2.cloned.1.call-update) | async-done | bytes 3145744 | tf_op jit(solution)/shard_map/reduce_scatter | solution.py:1405
  705.0 2.6 convert_element_type.2
  707.6 1.5 slice_bitcast_fusion
  709.2 3.0 copy.31
  712.2 2.7 fusion
  714.9 1.0 copy-done.2
  715.9 2.1 copy.34
  718.1 1.6 copy-done.1
  719.6 2.0 copy.35
  (25 shorter events, 0.3 us)
Async XLA Ops:
  7.2 3.9 copy-start.7
  7.2 4.5 copy-start.8
  7.2 5.1 copy-start.5
  7.2 5.7 copy-start.6
  7.2 6.3 copy-start.3
  7.2 224.0 %all-gather.4.cloned.1.call-start = ((), (), s32[]{:S(2)}) async-start(), calls=%async_computation.1 | async-start | bytes 9437184 | tf_op jit(solution)/shard_map/all_gather | solution.py:1387
  8.0 223.3 %all-gather.6.cloned.1.call-start = ((), (), s32[]{:S(2)}) async-start(), calls=%async_computation.2 | async-start | bytes 9437184 | tf_op jit(solution)/shard_map/all_gather | solution.py:1387
  8.7 222.5 %all-gather.8.cloned.1.call-start = ((), (), s32[]{:S(2)}) async-start(), calls=%async_computation.3 | async-start | bytes 9437184 | tf_op jit(solution)/shard_map/all_gather | solution.py:1387
  11.1 693.9 %reduce-scatter.2.cloned.1.call-start = ((), (), s32[]{:S(2)}) async-start(), calls=%async_computation.4 | async-start | bytes 28311552 | tf_op jit(solution)/shard_map/reduce_scatter | solution.py:1405
  662.2 3.7 copy-start.4
  707.6 4.6 copy-start
  712.2 3.7 copy-start.2
  715.9 3.7 copy-start.1
Sparse Core Ops, SparseCore 0:
  9.9 84.3 all-gather.3
  96.2 68.2 all-gather.5
  167.0 55.9 all-gather.7
  474.5 230.4 reduce-scatter.1

commit v5 on v4

--- a/solution.py
+++ b/solution.py
@@ -24,8 +24,8 @@
 LAG = 1
 CHUNK = 256
 TILE_ROWS = 256
-EXTRA = 4
-TILE_COLUMNS = 2048
+EXTRA = 5
+DOWN_PER_TICK = 2
 WEIGHT_ROWS = 256
 WEIGHT_TILES = 2
 MLP_TILE = 1024
@@ -228,10 +228,11 @@
 
 
 def mlp_kernel(
-    n, mlp_in, grad, attn_own, gain_m, gain_a, w_g_hbm, w_u_hbm, w_d_hbm,
-    down_out, hidden_out, attn_low_out, weights_out, mixed_own, gain_m_sum, gain_a_sum,
+    n, n_xy, mlp_in, grad_hbm, attn_own, gain_m, gain_a, w_g_hbm, w_u_hbm, w_d_hbm,
+    down_out, hidden_out, attn_low_out, weights_out, down_full, down_pair, down_blocks, mixed_own, gain_m_sum, gain_a_sum,
     buf, total, send, recv, w_g, w_u, w_d, mlp_rows, hidden, down_low, gate, up,
     ready, w_sems, io_sems, piece_sems, tile_sems, gain_m_acc, gain_a_acc,
+    grad, pair_sems, peer_sems, down_sem,
 ):
     rows, width = grad.shape
     units = w_g.shape[1]
@@ -253,9 +254,19 @@
             copy.start()
     down_weights = pltpu.make_async_copy(w_d_hbm, w_d, w_sems.at[2, 0])
     down_weights.start()
+    grad_in = pltpu.make_async_copy(grad_hbm, grad, down_sem)
+    grad_in.start()
     gain_m_acc[...] = jnp.zeros_like(gain_m_acc)
     gain_a_acc[...] = jnp.zeros_like(gain_a_acc)
-    greet("tp", n)
+    fsdp, n_ctx = lax.axis_index("fsdp"), n_xy[1]
+    core, spots = lax.rem(fsdp, 2), n_xy[0] // 2 * n_ctx
+    spot = lax.div(fsdp, 2) * n_ctx + lax.axis_index("ctx")
+    other_core = {"fsdp": fsdp + 1 - 2 * core}
+    peers = []
+    for k in range(1, spots):
+        peer = lax.rem(spot + k, spots)
+        peers.append({"fsdp": 2 * lax.div(peer, n_ctx) + core, "ctx": lax.rem(peer, n_ctx)})
+    greet("tp", n, [other_core] + peers)
     offset = per_chunk + line.stages + EXTRA
 
     def chunk_rows(chunk):
@@ -317,49 +328,93 @@
             ).astype(bf16)
 
     whole = pl.ds(0, rows)
-    late_in = [(hidden_out, w_g.at[whole]), (mlp_in, w_u.at[whole])]
     per_part = width // TILE_ROWS
+    late_in = pltpu.make_async_copy(mlp_in, w_u.at[whole], w_sems.at[1, 0])
+
+    def tile_rows(k):
+        return pl.ds(pl.multiple_of(k * TILE_ROWS, TILE_ROWS), TILE_ROWS)
 
     def tile_copy(k, slot):
-        part, block = lax.div(k, per_part), lax.rem(k, per_part)
+        part, row = lax.div(k, per_part), lax.rem(k, per_part)
         return pltpu.make_async_copy(
-            w_d.at[pl.ds(pl.multiple_of(slot * TILE_ROWS, TILE_ROWS), TILE_ROWS)],
-            weights_out.at[
-                pl.ds(pl.multiple_of(block * TILE_ROWS, TILE_ROWS), TILE_ROWS),
-                pl.ds(pl.multiple_of(part * units, units), units),
-            ],
+            w_d.at[tile_rows(slot)],
+            weights_out.at[tile_rows(row), pl.ds(pl.multiple_of(part * units, units), units)],
             tile_sems.at[slot],
         )
 
     def weight_tile(k):
         slot = lax.rem(k, 2)
-        block = pl.ds(pl.multiple_of(lax.rem(k, per_part) * TILE_ROWS, TILE_ROWS), TILE_ROWS)
+        at = tile_rows(lax.rem(k, per_part))
 
         @pl.when(k >= 2)
         def _():
             tile_copy(k - 2, slot).wait()
 
-        def fill(left, right):
-            @pl.loop(0, units // TILE_COLUMNS)
-            def _(j):
-                cols = pl.ds(pl.multiple_of(j * TILE_COLUMNS, TILE_COLUMNS), TILE_COLUMNS)
-                w_d[pl.ds(pl.multiple_of(slot * TILE_ROWS, TILE_ROWS), TILE_ROWS), cols] = dot(
-                    left[whole, block], right[whole, cols], ((0,), (0,)), bf16
+        def fill(right):
+            w_d[tile_rows(slot)] = dot(w_u[whole, at], right[...], ((0,), (0,)), bf16)
+
+        @pl.when(k < per_part)
+        def _():
+            fill(gate)
+
+        @pl.when(k >= per_part)
+        def _():
+            fill(up)
+
+        tile_copy(k, slot).start()
+
+    def down_copy(k):
+        return pltpu.make_async_copy(hidden, down_full.at[tile_rows(k)], down_sem)
+
+    hidden_in = pltpu.make_async_copy(hidden_out, grad, io_sems.at[0])
+
+    def down_tile(k):
+        @pl.when(k >= 1)
+        def _():
+            down_copy(k - 1).wait()
+
+        hidden[...] = dot(down_low[:, tile_rows(k)], grad[...], ((0,), (0,)), bf16)
+        down_copy(k).start()
+
+    block = width // (n_xy[0] * n_ctx)
+    pair_span = n_ctx * block
+
+    def pair_copy(chip):
+        rows_at = pl.ds(pl.multiple_of((2 * chip + 1 - core) * pair_span, pair_span), pair_span)
+        return pltpu.make_async_remote_copy(
+            src_ref=down_full.at[rows_at], dst_ref=down_pair.at[pl.ds(chip * pair_span, pair_span)],
+            send_sem=pair_sems.at[0, chip], recv_sem=pair_sems.at[1, chip],
+            device_id=other_core, device_id_type=pl.DeviceIdType.MESH,
+        )
+
+    def pair_unit(u):
+        chip, inside = u * CHUNK // pair_span, u * CHUNK % pair_span
+        if inside == 0:
+            pair_copy(chip).wait_recv()
+        mine = pl.ds(pl.multiple_of((2 * chip + core) * pair_span + inside, CHUNK), CHUNK)
+        there = down_pair.at[pl.ds(u * CHUNK, CHUNK)]
+        loads = local_copies([(down_full.at[mine], hidden), (there, mlp_rows)], io_sems)
+        for load in loads:
+            load.wait()
+        mlp_rows[...] = (mlp_rows[...].astype(f32) + hidden[...].astype(f32)).astype(bf16)
+        store = pltpu.make_async_copy(mlp_rows, there, down_sem)
+        store.start()
+        store.wait()
+
+    def spot_rows(which):
+        return down_pair.at[pl.ds(pl.multiple_of(which * block, block), block)]
+
+    def peer_copies():
+        copies = [pltpu.make_async_copy(spot_rows(spot), down_blocks.at[spots - 1], peer_sems.at[0, spots - 1])]
+        for k, device in enumerate(peers):
+            copies.append(
+                pltpu.make_async_remote_copy(
+                    src_ref=spot_rows(lax.rem(spot + k + 1, spots)), dst_ref=down_blocks.at[k],
+                    send_sem=peer_sems.at[0, k], recv_sem=peer_sems.at[1, k],
+                    device_id=device, device_id_type=pl.DeviceIdType.MESH,
                 )
-
-        @pl.when(k < per_part)
-        def _():
-            fill(down_low, w_g)
-
-        @pl.when((k >= per_part) & (k < 2 * per_part))
-        def _():
-            fill(w_u, gate)
-
-        @pl.when(k >= 2 * per_part)
-        def _():
-            fill(w_u, up)
-
-        tile_copy(k, slot).start()
+            )
+        return copies
 
     def let_in():
         @pl.when(i >= 1)
@@ -387,13 +442,18 @@
             scaled = g * gain_m[...]
             inner = jnp.mean(scaled * branch, axis=-1, keepdims=True)
             gain_m_acc[...] += g * branch * r
+
+            @pl.when(i == c)
+            def _():
+                mixed_own[pl.ds(pl.multiple_of(group * PIECE, PIECE), PIECE)] = g
+
             down_low[at] = (r * scaled - branch * (r * r * r) * inner).astype(bf16)
         for copy in copies:
             copy.wait()
 
     def attn_grad(group, total):
         at = pl.ds(pl.multiple_of(group * PIECE, PIECE), PIECE)
-        mixed = grad[line.rows(group, i)].astype(f32) + total
+        mixed = mixed_own[at] + total
         mixed_own[at] = mixed
         branch = attn_own[at].astype(f32)
         r = scale_of(branch)
@@ -408,6 +468,7 @@
 
     forward(0, True)
     down_weights.wait()
+    grad_in.wait()
     forward_down(0)
 
     @pl.loop(0, offset + line.ticks())
@@ -442,50 +503,82 @@
                     let_in()
                 work(lax.div(due, per_chunk))
 
-        first_tick = offset + groups - per_chunk
-
-        def late_copies():
-            return [pltpu.make_async_copy(a, b, io_sems.at[k]) for k, (a, b) in enumerate(late_in)]
-
-        @pl.when(t == first_tick - 1)
-        def _():
-            hidden_copy(rows // CHUNK - 1).wait()
-            for copy in late_copies():
-                copy.start()
-
-        @pl.when(t == first_tick)
-        def _():
-            for copy in late_copies():
-                copy.wait()
+        down_tick = groups + line.stages - 1
+        down_ticks = per_part // DOWN_PER_TICK
+
+        @pl.when((t >= down_tick) & (t < down_tick + down_ticks))
+        def _():
+            @pl.when(t == down_tick)
+            def _():
+                hidden_copy(rows // CHUNK - 1).wait()
+                hidden_in.start()
+                hidden_in.wait()
+
+            for m in range(DOWN_PER_TICK):
+                down_tile((t - down_tick) * DOWN_PER_TICK + m)
+
+        @pl.when(t == down_tick + down_ticks - 1)
+        def _():
+            down_copy(per_part - 1).wait()
+            for chip in range(n_xy[0] // 2):
+                pair_copy(chip).start()
+
+        pair_tick = down_tick + down_ticks + 1
+        units_of_pair = width // 2 // CHUNK
+        for u in range(units_of_pair):
+
+            @pl.when(t == pair_tick + u // 2)
+            def _():
+                pair_unit(u)
+                if u == units_of_pair - 1:
+                    for copy in peer_copies():
+                        copy.start()
+
+        last = offset + groups - per_chunk - 1
+
+        @pl.when(t == last)
+        def _():
+            late_in.start()
+
+        @pl.when(t == last + 1)
+        def _():
+            late_in.wait()
 
         for m in range(TILES_PER_TICK):
-            k = (t - first_tick) * TILES_PER_TICK + m
-
-            @pl.when((k >= 0) & (k < 3 * per_part))
+            k = (t - last - 1) * TILES_PER_TICK + m
+
+            @pl.when((k >= 0) & (k < 2 * per_part))
             def _():
                 weight_tile(k)
 
-    for k in (3 * per_part - 2, 3 * per_part - 1):
+    for k in (2 * per_part - 2, 2 * per_part - 1):
         tile_copy(k, k % 2).wait()
+    for copy in peer_copies():
+        copy.wait()
+    for chip in range(n_xy[0] // 2):
+        pair_copy(chip).wait_send()
     gain_m_sum[...] = jnp.sum(gain_m_acc[...], axis=0, keepdims=True)
     gain_a_sum[...] = jnp.sum(gain_a_acc[...], axis=0, keepdims=True)
 
 
-def mlp(mlp_in, grad, attn_own, gain_m, gain_a, w_g, w_u, w_d, n):
+def mlp(mlp_in, grad, attn_own, gain_m, gain_a, w_g, w_u, w_d, n, n_xy):
     rows, width = grad.shape
     units = w_g.shape[1]
     vmem, anywhere = pl.BlockSpec(memory_space=pltpu.VMEM), pl.BlockSpec(memory_space=pl.ANY)
     acts = jax.ShapeDtypeStruct((rows, width), bf16)
     inner = jax.ShapeDtypeStruct((rows, units), bf16)
+    spots = n_xy[0] // 2 * n_xy[1]
     gain_shape = jax.ShapeDtypeStruct((1, width), f32)
     return pl.pallas_call(
-        functools.partial(mlp_kernel, n),
+        functools.partial(mlp_kernel, n, n_xy),
         out_shape=[
-            acts, inner, acts, jax.ShapeDtypeStruct((width, 3 * units), bf16),
+            acts, inner, acts, jax.ShapeDtypeStruct((width, 2 * units), bf16),
+            jax.ShapeDtypeStruct((width, units), bf16), jax.ShapeDtypeStruct((width // 2, units), bf16),
+            jax.ShapeDtypeStruct((spots, width // (2 * spots), units), bf16),
             jax.ShapeDtypeStruct((rows // n, width), f32), gain_shape, gain_shape,
         ],
-        in_specs=[anywhere] + [vmem] * 4 + [anywhere] * 3,
-        out_specs=[anywhere] * 4 + [vmem] * 3,
+        in_specs=[anywhere] * 2 + [vmem] * 3 + [anywhere] * 3,
+        out_specs=[anywhere] * 7 + [vmem] * 3,
         scratch_shapes=line_scratch(n, rows, width) + [
             pltpu.VMEM(w_g.shape, bf16), pltpu.VMEM(w_u.shape, bf16), pltpu.VMEM(w_d.shape, bf16),
             pltpu.VMEM((CHUNK, width), bf16), pltpu.VMEM((CHUNK, units), bf16), pltpu.VMEM((rows, width), bf16),
@@ -494,6 +587,8 @@
             pltpu.SemaphoreType.DMA((3, units // 512)), pltpu.SemaphoreType.DMA((2,)), pltpu.SemaphoreType.DMA((n,)),
             pltpu.SemaphoreType.DMA((2,)),
             pltpu.VMEM((PIECE, width), f32), pltpu.VMEM((PIECE, width), f32),
+            pltpu.VMEM((rows, width), bf16),
+            pltpu.SemaphoreType.DMA((2, n_xy[0] // 2)), pltpu.SemaphoreType.DMA((2, spots)), pltpu.SemaphoreType.DMA,
         ],
         compiler_params=params(2),
         cost_estimate=pl.CostEstimate(flops=200 * 10**9, bytes_accessed=60 << 20, transcendentals=0),
@@ -1398,15 +1493,16 @@
         x_all, w_query, w_key, w_value, w_output.T, gain_q[None], gain_k[None], gain_a[None], cosine, sine,
         micro_count, tp, n_xy
     )
-    down, _, attn_low, mlp_weights, mixed_own, gain_m_sum, gain_a_sum = mlp(
-        mlp_in, grad_all, attn_own, gain_m[None], gain_a[None], w_g, w_u, w_down_t, tp
+    down, _, attn_low, mlp_weights, _, _, down_blocks, mixed_own, gain_m_sum, gain_a_sum = mlp(
+        mlp_in, grad_all, attn_own, gain_m[None], gain_a[None], w_g, w_u, w_down_t, tp, n_xy
     )
     def scatter(full):
         return lax.psum_scatter(full, xy, scatter_dimension=0, tiled=True).astype(f32)
 
     units = w_gate.shape[1]
     d_mlp = scatter(mlp_weights)
-    d_down, d_gate, d_up = d_mlp[:, :units].T, d_mlp[:, units : 2 * units], d_mlp[:, 2 * units :]
+    d_down = jnp.sum(down_blocks.astype(f32), axis=0).T
+    d_gate, d_up = d_mlp[:, :units], d_mlp[:, units:]
     grad_tokens, out, gains, d_attn, _ = back(
         attn_low, w_full, raw, low, prev, head_low, stats, x_all, mixed_own, attention, down,
         gain_q[None], gain_k[None], gain_a[None], gain_m[None], gain_a_sum, gain_m_sum, cosine, sine,

time: 731 us -> 716 us (0.979)
  waiting for transfers between devices: 39.4 us -> 1.47 us
  Pallas kernels: 648 us -> 671 us
    reduce_scatter x1, waiting for transfers between devices: 37.9 us -> 0.01 us  [scatter(): lax.psum_scatter(full, xy, scatter_dimension=0, tiled=True).astype(f32)]
    pallas_call x1, Pallas kernels: 243 us -> 265 us  [mlp(): pl.pallas_call(functools.partial(mlp_kernel, n, n_xy), out_shape=[acts, i...]
  transfers between devices with their start and end apart: 4 -> 4, of which waited for: 1 -> 0; matrix products, arithmetic and copies ran while one was open for 1% -> 2% of each run, Pallas kernels for 56% -> 57%
where the time goes in v5:
time: 716 us; the launch traced here: 712 us
  Pallas kernels  671 us (94%)
  local copies, waits for them, and re-layouts  19.8 us (3%)
  between operations  14.1 us (2%)
    pallas_call x1, Pallas kernels, mlp(): pl.pallas_call(functools.partial(mlp_kernel, n, n_xy), out_shape=[acts, i...  265 us
    pallas_call x1, Pallas kernels, front(): pl.pallas_call(functools.partial(front_kernel, n_tp, n_xy, seqs), out_sha...  217 us
    pallas_call x1, Pallas kernels, back(): pl.pallas_call(functools.partial(back_kernel, n_tp, n_xy, seqs), out_shap...  189 us
  transfers between devices with their start and end apart: 4, of which 0 were waited for; matrix products, arithmetic and copies ran while one was open for 2% of the time, Pallas kernels for 57%

profile of v5, /device:TPU:0, one launch (start us, length us, event | category | flops | bytes accessed | tf_op | source)
XLA Modules:
  0.0 711.8 jit_solution(8315010835607311011)
XLA Ops:
  7.3 0.7 all-gather.4.cloned.1.call-update
  8.0 0.0 all-gather.6.cloned.1.call-start
  8.0 0.7 all-gather.6.cloned.1.call-update
  8.7 0.0 all-gather.8.cloned.1.call-start
  8.8 2.3 copy.32
  11.1 0.0 reduce-scatter.2.cloned.1.call-start
  11.1 0.6 broadcast_in_dim.33
  11.7 0.6 broadcast_in_dim.34
  12.3 0.6 broadcast_in_dim.35
  12.9 0.6 broadcast_in_dim.36
  13.5 0.8 copy.31
  14.3 216.9 %front.1 = (f32[1024,1024]{1,0:T(8,128)}, bf16[1024,1536]{1,0:T(8,128)(2,1)}, bf16[1,1024,1024]{2,1,0:T(8,128)(2,1)}, bf16[1024,512]{1,0:T(8,128)(2,1)}, f32[102...) custom-call(bf16[1024,2048]{1,0:T(8,128)(2,1)} %bitcast.36, ...), custom_call_target="tpu_custom_call" | custom-call | flops 149999992832 | bytes 31457280 | tf_op jit(solution)/shard_map/front/pallas_call | solution.py:976
  231.3 264.9 %mlp.1 = (bf16[1024,2048]{1,0:T(8,128)(2,1)}, bf16[1024,2048]{1,0:T(8,128)(2,1)}, bf16[1024,2048]{1,0:T(8,128)(2,1)}, bf16[2048,4096]{1,0:T(8,128)(2,1)}, bf16[2...) custom-call(bf16[1024,2048]{1,0:T(8,128)(2,1)} %get-tuple-element.33, ...), custom_call_target="tpu_custom_call" | custom-call | flops 199999995904 | bytes 62914560 | tf_op jit(solution)/shard_map/mlp/pallas_call | solution.py:572
  496.3 188.8 %back.1 = (bf16[1024,2048]{1,0:T(8,128)(2,1)}, bf16[1024,2048]{1,0:T(8,128)(2,1)}, f32[1,5120]{1,0:T(1,128)}, f32[1024,512]{1,0:T(8,128)}, bf16[2048,2048]{1,0:T(8,128)(2,1)}) custom-call(bf16[1024,2048]{1,0:T(8,128)(2,1)} %get-tuple-element.35.attn_low_hbm, bf16[2048,2048]{1,0:T(8,128)(2,1)} %get-tuple-element.36.w_hbm, ...), custom_call_target="tpu_custom_call" | custom-call | flops 199999995904 | bytes 62914560 | tf_op jit(solution)/shard_map/back/pallas_call | solution.py:1426
  685.1 3.3 convert_reduce_fusion
  688.4 1.8 copy.34
  690.2 2.7 slice_bitcast_fusion
  692.9 1.0 copy.33
  693.9 0.6 fusion.2
  694.5 0.6 fusion.1
  695.1 4.2 fusion
  699.3 2.1 copy.37
  701.5 1.6 copy-done
  703.0 2.0 copy.38
  (22 shorter events, 0.2 us)
Async XLA Ops:
  7.2 3.9 copy-start.6
  7.2 4.5 copy-start.7
  7.2 5.1 copy-start.4
  7.2 5.7 copy-start.5
  7.2 6.3 copy-start.2
  7.2 224.0 %all-gather.4.cloned.1.call-start = ((), (), s32[]{:S(2)}) async-start(), calls=%async_computation.1 | async-start | bytes 9437184 | tf_op jit(solution)/shard_map/all_gather | solution.py:1482
  8.0 223.3 %all-gather.6.cloned.1.call-start = ((), (), s32[]{:S(2)}) async-start(), calls=%async_computation.2 | async-start | bytes 9437184 | tf_op jit(solution)/shard_map/all_gather | solution.py:1482
  8.7 222.6 %all-gather.8.cloned.1.call-start = ((), (), s32[]{:S(2)}) async-start(), calls=%async_computation.3 | async-start | bytes 9437184 | tf_op jit(solution)/shard_map/all_gather | solution.py:1482
  11.1 684.0 %reduce-scatter.2.cloned.1.call-start = ((), (), s32[]{:S(2)}) async-start(), calls=%async_computation.4 | async-start | bytes 18874368 | tf_op jit(solution)/shard_map/reduce_scatter | solution.py:1500
  688.4 5.5 copy-start.3
  695.1 4.2 copy-start.1
  699.3 3.7 copy-start
Sparse Core Ops, SparseCore 0:
  9.9 84.3 all-gather.3
  96.2 68.2 all-gather.5
  167.0 55.9 all-gather.7
  496.4 190.2 reduce-scatter.1

commit v6 on v5

--- a/solution.py
+++ b/solution.py
@@ -27,7 +27,7 @@
 EXTRA = 5
 DOWN_PER_TICK = 2
 WEIGHT_ROWS = 256
-WEIGHT_TILES = 2
+WEIGHT_TILES = 4
 MLP_TILE = 1024
 TILES_PER_TICK = 3
 

time: 716 us -> 705 us (0.985)
  Pallas kernels: 671 us -> 661 us
    pallas_call x1, Pallas kernels: 189 us -> 178 us  [back(): pl.pallas_call(functools.partial(back_kernel, n_tp, n_xy, seqs), out_shap...]
  transfers between devices with their start and end apart: 4 -> 4, of which waited for: 0 -> 0; matrix products, arithmetic and copies ran while one was open for 2% -> 2% of each run, Pallas kernels for 57% -> 56%
where the time goes in v6:
time: 705 us; the launch traced here: 702 us
  Pallas kernels  661 us (94%)
  local copies, waits for them, and re-layouts  19.9 us (3%)
  between operations  14.1 us (2%)
    pallas_call x1, Pallas kernels, mlp(): pl.pallas_call(functools.partial(mlp_kernel, n, n_xy), out_shape=[acts, i...  266 us
    pallas_call x1, Pallas kernels, front(): pl.pallas_call(functools.partial(front_kernel, n_tp, n_xy, seqs), out_sha...  217 us
    pallas_call x1, Pallas kernels, back(): pl.pallas_call(functools.partial(back_kernel, n_tp, n_xy, seqs), out_shap...  178 us
  transfers between devices with their start and end apart: 4, of which 0 were waited for; matrix products, arithmetic and copies ran while one was open for 2% of the time, Pallas kernels for 56%

profile of v6, /device:TPU:0, one launch (start us, length us, event | category | flops | bytes accessed | tf_op | source)
XLA Modules:
  0.0 702.2 jit_solution(4517484891169030822)
XLA Ops:
  7.3 0.7 all-gather.4.cloned.1.call-update
  8.0 0.0 all-gather.6.cloned.1.call-start
  8.0 0.7 all-gather.6.cloned.1.call-update
  8.7 0.0 all-gather.8.cloned.1.call-start
  8.8 2.3 copy.32
  11.1 0.0 reduce-scatter.2.cloned.1.call-start
  11.1 0.6 broadcast_in_dim.33
  11.7 0.6 broadcast_in_dim.34
  12.3 0.6 broadcast_in_dim.35
  12.9 0.6 broadcast_in_dim.36
  13.5 0.8 copy.31
  14.3 216.9 %front.1 = (f32[1024,1024]{1,0:T(8,128)}, bf16[1024,1536]{1,0:T(8,128)(2,1)}, bf16[1,1024,1024]{2,1,0:T(8,128)(2,1)}, bf16[1024,512]{1,0:T(8,128)(2,1)}, f32[102...) custom-call(bf16[1024,2048]{1,0:T(8,128)(2,1)} %bitcast.36, ...), custom_call_target="tpu_custom_call" | custom-call | flops 149999992832 | bytes 31457280 | tf_op jit(solution)/shard_map/front/pallas_call | solution.py:976
  231.3 265.8 %mlp.1 = (bf16[1024,2048]{1,0:T(8,128)(2,1)}, bf16[1024,2048]{1,0:T(8,128)(2,1)}, bf16[1024,2048]{1,0:T(8,128)(2,1)}, bf16[2048,4096]{1,0:T(8,128)(2,1)}, bf16[2...) custom-call(bf16[1024,2048]{1,0:T(8,128)(2,1)} %get-tuple-element.33, ...), custom_call_target="tpu_custom_call" | custom-call | flops 199999995904 | bytes 62914560 | tf_op jit(solution)/shard_map/mlp/pallas_call | solution.py:572
  497.1 178.4 %back.1 = (bf16[1024,2048]{1,0:T(8,128)(2,1)}, bf16[1024,2048]{1,0:T(8,128)(2,1)}, f32[1,5120]{1,0:T(1,128)}, f32[1024,512]{1,0:T(8,128)}, bf16[2048,2048]{1,0:T(8,128)(2,1)}) custom-call(bf16[1024,2048]{1,0:T(8,128)(2,1)} %get-tuple-element.35.attn_low_hbm, bf16[2048,2048]{1,0:T(8,128)(2,1)} %get-tuple-element.36.w_hbm, ...), custom_call_target="tpu_custom_call" | custom-call | flops 199999995904 | bytes 62914560 | tf_op jit(solution)/shard_map/back/pallas_call | solution.py:1426
  675.5 3.2 convert_reduce_fusion
  678.7 1.8 copy.34
  680.6 2.8 slice_bitcast_fusion
  683.3 1.0 copy.33
  684.3 0.6 fusion.2
  684.9 0.6 fusion.1
  685.5 4.2 fusion
  689.8 2.1 copy.37
  691.9 1.6 copy-done
  693.5 2.0 copy.38
  (22 shorter events, 0.2 us)
Async XLA Ops:
  7.2 3.9 copy-start.6
  7.2 4.5 copy-start.7
  7.2 5.1 copy-start.4
  7.2 5.7 copy-start.5
  7.2 6.3 copy-start.2
  7.2 224.0 %all-gather.4.cloned.1.call-start = ((), (), s32[]{:S(2)}) async-start(), calls=%async_computation.1 | async-start | bytes 9437184 | tf_op jit(solution)/shard_map/all_gather | solution.py:1482
  8.0 223.3 %all-gather.6.cloned.1.call-start = ((), (), s32[]{:S(2)}) async-start(), calls=%async_computation.2 | async-start | bytes 9437184 | tf_op jit(solution)/shard_map/all_gather | solution.py:1482
  8.7 222.6 %all-gather.8.cloned.1.call-start = ((), (), s32[]{:S(2)}) async-start(), calls=%async_computation.3 | async-start | bytes 9437184 | tf_op jit(solution)/shard_map/all_gather | solution.py:1482
  11.1 674.5 %reduce-scatter.2.cloned.1.call-start = ((), (), s32[]{:S(2)}) async-start(), calls=%async_computation.4 | async-start | bytes 18874368 | tf_op jit(solution)/shard_map/reduce_scatter | solution.py:1500
  678.7 5.6 copy-start.3
  685.5 4.2 copy-start.1
  689.8 3.7 copy-start
Sparse Core Ops, SparseCore 0:
  9.9 84.3 all-gather.3
  96.2 68.2 all-gather.5
  167.0 55.9 all-gather.7
  497.2 184.2 reduce-scatter.1
